TPU v7x, 32 devices: a whole 2x2x4 slice. The times are simulated.
32 devices in a mesh: lon: 4 (over y, core), lat: 8 (over z, x).
Axes of the slice: x: 2, y: 2, z: 4, core: 2. Of those that a mesh axis runs over, the one named last changes fastest.
Arguments:
- grid: bfloat16 [12, 2, 2, 1024, 4096], P(None, None, None, 'lat', 'lon'), may hold values from -6 to 6
- legendre: bfloat16 [4, 256, 1024, 2, 512], P('lon', None, 'lat'), may hold values from -0.25 to 0.25
Outputs:
- spectral: float32 [4, 256, 8, 2, 2, 2, 512], P('lon', 'lat')
All inputs are finite; a program needn't handle non-finite values.
Results may differ from a plain program's by a relative error of at most 0.0029.
Values sent between devices are 32-bit elements; how exact they have to be, the bound alone decides.
No kernel may reach another device: no remote copies, remote signals or barrier semaphores. Data moves between devices by JAX's collectives and lax.ppermute only.
A program may use at most 320 MiB of HBM per device.

v0:
```python
import math

import jax
import jax.numpy as jnp
from jax import lax
from jax.sharding import PartitionSpec as P

NLON = 4096
WAVES = 1024


adiabatic_exponent = 0.286


def shifted(block, axis, distance):
    devices = range(lax.axis_size(axis))
    route = [(i - distance, i) for i in devices if i - distance in devices]
    return lax.ppermute(block, axis, route)


def tendency_fields(numeric_buffer_grid):
    eastward_flow_speed, poleward_flow_speed, local_spin_field, flow_spreading_rate = (
        numeric_buffer_grid[0],
        numeric_buffer_grid[1],
        numeric_buffer_grid[2],
        numeric_buffer_grid[3],
    )
    kinetic_warmth_field, water_vapour_mixing = (numeric_buffer_grid[4], numeric_buffer_grid[5])
    warmth_eastward_slope, warmth_poleward_slope = (numeric_buffer_grid[6], numeric_buffer_grid[7])
    vapour_eastward_slope, vapour_poleward_slope = (numeric_buffer_grid[8], numeric_buffer_grid[9])
    ground_load_eastward_slope, ground_load_poleward_slope = (
        numeric_buffer_grid[10],
        numeric_buffer_grid[11],
    )
    return jnp.stack(
        [
            local_spin_field * poleward_flow_speed
            - kinetic_warmth_field * ground_load_eastward_slope,
            -local_spin_field * eastward_flow_speed
            - kinetic_warmth_field * ground_load_poleward_slope,
            eastward_flow_speed * poleward_flow_speed,
            -(
                eastward_flow_speed * warmth_eastward_slope
                + poleward_flow_speed * warmth_poleward_slope
            )
            + adiabatic_exponent * kinetic_warmth_field * flow_spreading_rate,
            -(
                eastward_flow_speed * vapour_eastward_slope
                + poleward_flow_speed * vapour_poleward_slope
            )
            - water_vapour_mixing * flow_spreading_rate,
            eastward_flow_speed * kinetic_warmth_field,
            poleward_flow_speed * kinetic_warmth_field,
            poleward_flow_speed * water_vapour_mixing,
        ],
        0,
    )


def phase_rows(lon_first, lon_number, devices, per_device):
    longitude = lon_first + lax.iota(jnp.int32, lon_number)
    owners = lax.iota(jnp.int32, devices)
    column = lax.iota(jnp.int32, per_device)
    wavenumber = owners[:, None] + devices * column[None, :]
    product = wavenumber[:, :, None] * longitude[None, None, :] % NLON
    angles = product.astype(jnp.float32) * (2.0 * math.pi / NLON)
    factor = 1.0 / math.sqrt(NLON)
    return jnp.stack([jnp.cos(angles) * factor, -jnp.sin(angles) * factor], 1)


def spectra_level(grid, legendre):
    tendencies = tendency_fields(grid.astype(jnp.float32))
    tend_shape = tendencies.shape
    lon_local = tend_shape[4]
    row_count = tend_shape[0] * tend_shape[1] * tend_shape[2] * tend_shape[3]
    flattened = tendencies.reshape(row_count, lon_local)
    devices = lax.axis_size("lon")
    lon_rank = lax.axis_index("lon")
    per_device = legendre.shape[1]
    phases = phase_rows(lon_rank * lon_local, lon_local, devices, per_device)
    section = phases
    received = lax.psum_scatter(
        lax.dot_general(
            section,
            flattened,
            (((3,), (1,)), ((), ())),
            precision=lax.Precision.HIGHEST,
            preferred_element_type=jnp.float32,
        ),
        "lon",
        scatter_dimension=0,
        tiled=True,
    )
    spectra = received.reshape(2, per_device, row_count)
    shaped = spectra.reshape(2, per_device, tend_shape[0], tend_shape[1], 2, tend_shape[3])
    northern = shaped[:, :, :, :, 0]
    southern = shaped[:, :, :, :, 1]
    folded = jnp.stack([northern + southern, northern - southern], 0).astype(jnp.bfloat16)
    weights = legendre[0]
    lat_count = lax.axis_size("lat")
    own_rows = per_device // lat_count
    half_degrees = weights.shape[-1]
    quarter = half_degrees // 2
    weights_low = weights[:, :, :, :quarter]
    window = folded
    section = weights_low
    lower_part = lax.psum_scatter(
        jnp.einsum("ecsklj,sjeh->sklceh", window, section, preferred_element_type=jnp.float32),
        "lat",
        scatter_dimension=0,
        tiled=True,
    )
    half_rows = per_device // 2
    half_count = lat_count // 2
    block = own_rows // 2
    weights_high = weights[:half_rows, :, :, quarter:]
    folded_high = folded[:, :, :half_rows]
    index = lax.iota(jnp.int32, lax.axis_size("lat") * block)
    target = index // block
    within = index % block
    upper = (target >= half_count).astype(jnp.int32)
    owner = target - half_count * upper
    rows = owner * own_rows + upper * block + within
    window = jnp.take(folded_high, rows, axis=2)
    section = jnp.take(weights_high, rows, axis=0)
    upper_part = lax.psum_scatter(
        jnp.einsum("ecsklj,sjeh->sklceh", window, section, preferred_element_type=jnp.float32),
        "lat",
        scatter_dimension=0,
        tiled=True,
    )
    moved_rows = shifted(upper_part, "lat", -half_count)
    lower_owner = lax.axis_index("lat") < half_count
    high_all = jnp.concatenate([upper_part, moved_rows], 0)
    high_all = jnp.where(lower_owner, high_all, jnp.zeros((), jnp.float32))
    result = jnp.concatenate([lower_part, high_all], 5)
    column = lax.axis_index("lat") * own_rows + lax.iota(jnp.int32, own_rows)
    wavenumber = lon_rank + devices * column
    degree = (
        2 * lax.iota(jnp.int32, half_degrees)[None, None, :] + lax.iota(jnp.int32, 2)[None, :, None]
    )
    inside = wavenumber[:, None, None] + degree < WAVES
    result = jnp.where(inside[:, None, None, None, :, :], result, jnp.zeros((), jnp.float32))
    return result[None]


def local(grid, legendre):
    return spectra_level(grid, legendre)


def solution(mesh):
    in_specs = (P(None, None, None, "lat", "lon"), P("lon", None, "lat", None, None))
    out_specs = P("lon", "lat", None, None, None, None, None)
    return jax.shard_map(local, mesh=mesh, in_specs=in_specs, out_specs=out_specs, check_vma=False)
```

profile of v0, /device:TPU:0, one launch (start us, length us, event | category | flops | bytes accessed | tf_op | source)
XLA Modules:
  0.0 922.9 jit_solution(4573625227145439938)
XLA Ops:
  6.5 0.0 reduce-scatter.4.cloned.1.call-start
  6.5 7.1 convert_element_type.20
  13.7 2.5 fusion.33
  16.2 2.5 fusion.31
  18.7 1.9 multiply_dynamic-update-slice_fusion.3
  20.5 3.1 fusion.29
  23.6 3.1 fusion.25
  26.7 1.9 multiply_dynamic-update-slice_fusion.2
  28.6 1.9 multiply_dynamic-update-slice_fusion.1
  30.5 1.9 multiply_dynamic-update-slice_fusion
  32.4 16.9 %cosine_multiply_fusion = (f32[4,1,256,1024]{3,2,1,0:T(8,128)S(1)}, f32[4,1,256,1024]{3,2,1,0:T(8,128)S(1)}) fusion(s32[1024]{0:T(1024)S(1)} %iota_add_fusion, s32[4,256]{1,0:T(4,128)S(1)} %iota_add_fusion.1), kind=kLoop, calls=%fused_computation.30 | loop fusion | flops 17825792 | bytes 8396800 | tf_op jit(solution)/shard_map/mul | solution.py:68
  49.3 113.6 %fusion.6 = f32[4,2,256,4096]{3,2,1,0:T(8,128)} fusion(f32[4096,1024,1,1]{1,0,3,2:T(8,128)} %bitcast.45, f32[4,1,256,1024]{3,2,1,0:T(8,128)S(1)} %get-tuple-element.10, f32[4,1,256,1024]{3,2,1,0:T(8,128)S(1)} %get-tuple-element.9), kind=kOutput, calls=%fused_computation.10 | convolution fusion | flops 103081312256 | bytes 58720256 | tf_op jit(solution)/shard_map/dot_general | solution.py:83
  162.9 0.0 reduce-scatter.4.cloned.1.call-update
  162.9 0.0 reduce-scatter.8.cloned.1.call-start
  163.0 53.6 %copy.26 = bf16[1,256,128,2,512]{4,2,3,1,0:T(8,128)(2,1)} copy(bf16[1,256,128,2,512]{4,3,2,1,0:T(2,128)(2,1)} %param.3) | data formatting | bytes 134217728 | tf_op args[1]
  216.5 14.1 %slice.87 = bf16[128,128,2,256]{3,1,2,0:T(8,128)(2,1)} slice(bf16[256,128,2,512]{3,1,2,0:T(8,128)(2,1)} %bitcast.43), slice={[0:128], [0:128], [0:2], [256:512]} | slice | bytes 33554432 | tf_op jit(solution)/shard_map/slice | solution.py:116
  230.7 14.3 %gather_fusion = bf16[128,128,2,256]{3,1,2,0:T(8,128)(2,1)} fusion(bf16[128,128,2,256]{3,1,2,0:T(8,128)(2,1)} %slice.87, s32[1024]{0:T(1024)S(1)} %pad_clamp_fusion), kind=kCustom, calls=%fused_computation | custom fusion | bytes 33554944 | tf_op jit(solution)/shard_map/jit(_take)/gather | solution.py:125
  245.0 153.0 %reduce-scatter.4.cloned.1.call-done = f32[1,2,256,4096]{3,2,1,0:T(8,128)} async-done(((f32[4,2,256,4096]{3,2,1,0:T(8,128)}), f32[1,2,256,4096]{3,2,1,0:T(8,128)}) %reduce-scatter.4.cloned.1.call-update) | async-done | bytes 8388624 | tf_op jit(solution)/shard_map/reduce_scatter | solution.py:82
  398.0 11.8 %reshape_reshape.3 = f32[2,256,8,2,2,128]{5,4,3,2,1,0:T(2,128)} reshape(f32[1,2,256,4096]{3,2,1,0:T(8,128)} %reduce-scatter.4.cloned.1.call-done) | data formatting | bytes 16777216 | tf_op jit(solution)/shard_map/reshape;reshape | solution.py:95
  409.8 11.1 %fusion.51 = (f32[2,256,8,2,1,128]{5,4,3,2,1,0:T(1,128)S(1)}, f32[2,256,8,2,1,128]{5,4,3,2,1,0:T(1,128)S(1)}) fusion(f32[2,256,8,2,2,128]{5,4,3,2,1,0:T(2,128)} %reshape_reshape.3), kind=kLoop, calls=%fused_computation.100 | loop fusion | bytes 16777216 | tf_op jit(solution)/shard_map/slice | solution.py:96
  420.9 0.7 fusion.20
  421.6 0.0 copy-start
  421.6 1.3 copy-done
  422.9 1.5 pad_maximum_fusion
  424.4 3.8 gather_fusion.1
  428.2 10.0 %fusion.17 = f32[128,8,2,2,2,256]{5,1,2,3,4,0:T(8,128)} fusion(bf16[128,128,2,256]{3,1,2,0:T(8,128)(2,1)} %gather_fusion, pred[128]{0:T(512)(128)(4,1)S(1)} %compare_and_fusion, bf16[128,2,2,8,2,128]{5,3,4,2,1,0:T(8,128)(2,1)} %gather_fusion.1), kind=kOutput, calls=%fused_computation.31 | convolution fusion | flops 546308096 | bytes 27263104 | tf_op jit(solution)/shard_map/ecsklj,sjeh->sklceh/dot_general | solution.py:127
  438.2 0.0 reduce-scatter.8.cloned.1.call-update
  438.2 0.0 reduce-scatter.6.cloned.1.call-start
  438.3 19.3 %fusion.5 = f32[256,8,2,2,2,256]{5,1,2,3,4,0:T(8,128)} fusion(bf16[256,128,2,512]{3,1,2,0:T(8,128)(2,1)} %bitcast.43, bf16[1,2,256,8,2,128]{5,3,4,1,0,2:T(8,128)(2,1)} %copy-done, bf16[1,2,256,8,2,128]{5,3,4,1,0,2:T(8,128)(2,1)S(1)} %get-tuple-element.5), kind=kOutput, calls=%fused_computation.9 | convolution fusion | flops 1075838976 | bytes 54525952 | tf_op jit(solution)/shard_map/ecsklj,sjeh->sklceh/dot_general | solution.py:108
  457.5 0.0 reduce-scatter.6.cloned.1.call-update
  457.6 128.2 %reduce-scatter.8.cloned.1.call-done = f32[16,8,2,2,2,256]{5,1,2,3,4,0:T(8,128)} async-done(((f32[128,8,2,2,2,256]{5,1,2,3,4,0:T(8,128)}), f32[16,8,2,2,2,256]{5,1,2,3,4,0:T(8,128)}) %reduce-scatter.8.cloned.1.call-update) | async-done | bytes 1048592 | tf_op jit(solution)/shard_map/reduce_scatter | solution.py:126
  585.8 1.5 collective-permute-start
  587.3 0.2 add_compare_fusion
  587.5 104.0 %collective-permute-done = f32[16,8,2,2,2,256]{5,1,2,3,4,0:T(8,128)S(1)} collective-permute-done((f32[16,8,2,2,2,256]{5,1,2,3,4,0:T(8,128)}, f32[16,8,2,2,2,256]{5,1,2,3,4,0:T(8,128)S(1)}, u32[]{:S(2)}, u32[]{:S(2)}) %collective-permute-start) | collective-permute-done | bytes 1048608 | tf_op jit(solution)/shard_map/ppermute | solution.py:18
  691.5 1.6 fusion.34
  693.1 215.6 %reduce-scatter.6.cloned.1.call-done = f32[32,8,2,2,2,256]{5,1,2,3,4,0:T(8,128)} async-done(((f32[256,8,2,2,2,256]{5,1,2,3,4,0:T(8,128)}), f32[32,8,2,2,2,256]{5,1,2,3,4,0:T(8,128)}) %reduce-scatter.6.cloned.1.call-update) | async-done | bytes 2097168 | tf_op jit(solution)/shard_map/reduce_scatter | solution.py:107
  908.7 2.2 maximum_select_fusion
  910.9 5.3 copy.7
  (9 shorter events, 0.1 us)
Async XLA Ops:
  6.5 391.5 %reduce-scatter.4.cloned.1.call-start = ((), (), s32[]{:S(2)}) async-start(), calls=%async_computation.3 | async-start | bytes 41943040 | tf_op jit(solution)/shard_map/reduce_scatter | solution.py:82
  162.9 422.9 %reduce-scatter.8.cloned.1.call-start = ((), (), s32[]{:S(2)}) async-start(), calls=%async_computation.5 | async-start | bytes 9437184 | tf_op jit(solution)/shard_map/reduce_scatter | solution.py:126
  421.6 1.3 copy-start
  438.2 470.5 %reduce-scatter.6.cloned.1.call-start = ((), (), s32[]{:S(2)}) async-start(), calls=%async_computation.4 | async-start | bytes 18874368 | tf_op jit(solution)/shard_map/reduce_scatter | solution.py:107
  585.8 105.7 %collective-permute-start = (f32[16,8,2,2,2,256]{5,1,2,3,4,0:T(8,128)}, f32[16,8,2,2,2,256]{5,1,2,3,4,0:T(8,128)S(1)}, u32[]{:S(2)}, u32[]{:S(2)}) collective-permute-start(f32[16,8,2,2,2,256]{5,1,2,3,4,0:T(8,128)} %reduce-scatter.8.cloned.1.call-done), channel_id=1, source_target_pairs={{4,0},{5,1},{6,2},{7,3},{12,8},{13,9},{14,10},{15,11},{20,16},{21,... | collective-permute-start | bytes 3145736 | tf_op jit(solution)/shard_map/ppermute | solution.py:18
Sparse Core Ops, SparseCore 0:
  163.0 234.9 reduce-scatter.3
  438.3 147.4 reduce-scatter.7
  589.6 319.0 reduce-scatter.5
where the time goes:
time: 929 us; the launch traced here: 923 us
  waiting for transfers between devices  601 us (65%)
  matrix products  143 us (15%)
  local copies, waits for them, and re-layouts  115 us (12%)
  other arithmetic  48.9 us (5%)
  between operations  13.4 us (1%)
    reduce_scatter x2, waiting for transfers between devices, spectra_level(): lax.psum_scatter(jnp.einsum('ecsklj,sjeh->sklceh', window, section, prefe...  344 us
    reduce_scatter x1, waiting for transfers between devices, spectra_level(): lax.psum_scatter(lax.dot_general(section, flattened, (((3,), (1,)), ((),...  153 us
    dot_general x1, matrix products, spectra_level(): lax.dot_general(section, flattened, (((3,), (1,)), ((), ())), precision=l...  114 us
    ppermute x1, waiting for transfers between devices, shifted(): return lax.ppermute(block, axis, route)  104 us
    unnamed x3, local copies, waits for them, and re-layouts  54.9 us
    dot_general x2, matrix products, spectra_level(): jnp.einsum('ecsklj,sjeh->sklceh', window, section, preferred_element_type...  29.3 us
  transfers between devices with their start and end apart: 4, of which 4 were waited for; matrix products, arithmetic and copies ran while one was open for 11% of the time, Pallas kernels for 0%

commit v1 on v0

v1 whole, which is shorter than its diff:
```python
import math

import jax
import jax.numpy as jnp
import numpy as np
from jax import lax
from jax.experimental import pallas as pl
from jax.experimental.pallas import tpu as pltpu
from jax.sharding import PartitionSpec as P


ADIABATIC = 0.286
LANES = 128
SPLIT = ((1, 1, 2), (2, 1, 1))
ROWS_CONTRACTED = (((1,), (1,)), ((), ()))


def tendency_kernel(grid_ref, high_ref, low_ref, scratch):
    pairs = grid_ref.shape[3]
    pieces = grid_ref.shape[4] // LANES

    def field(n):
        return [grid_ref[n, 0, h].astype(jnp.float32) for h in range(2)]

    u, v, zeta, div, temp, hum, temp_x, temp_y, hum_x, hum_y, press_x, press_y = [
        field(n) for n in range(12)
    ]
    formulas = [
        lambda h: zeta[h] * v[h] - temp[h] * press_x[h],
        lambda h: -zeta[h] * u[h] - temp[h] * press_y[h],
        lambda h: u[h] * v[h],
        lambda h: -(u[h] * temp_x[h] + v[h] * temp_y[h]) + ADIABATIC * temp[h] * div[h],
        lambda h: -(u[h] * hum_x[h] + v[h] * hum_y[h]) - hum[h] * div[h],
        lambda h: u[h] * temp[h],
        lambda h: v[h] * temp[h],
        lambda h: v[h] * hum[h],
    ]
    for t, formula in enumerate(formulas):
        north, south = formula(0), formula(1)
        even, odd = north + south, north - south
        for piece in range(pieces):
            lanes = slice(piece * LANES, (piece + 1) * LANES)
            place = t * pieces + piece
            scratch[place, pl.ds(0, pairs, stride=2), :] = even[:, lanes]
            scratch[place, pl.ds(1, pairs, stride=2), :] = odd[:, lanes]
            whole = scratch[place]
            high = whole.astype(jnp.bfloat16)
            high_ref[t, 0, :, lanes] = high
            low_ref[t, 0, :, lanes] = (whole - high.astype(jnp.float32)).astype(jnp.bfloat16)


def folded_tendencies(grid):
    fields, levels, hemispheres, pairs, longitudes = grid.shape
    width = min(256, longitudes)
    shape = jax.ShapeDtypeStruct((8, levels, 2 * pairs, longitudes), jnp.bfloat16)
    high, low = pl.pallas_call(
        tendency_kernel,
        grid=(levels, longitudes // width),
        in_specs=[
            pl.BlockSpec((fields, 1, hemispheres, pairs, width), lambda l, x: (0, l, 0, 0, x))
        ],
        out_specs=[pl.BlockSpec((8, 1, 2 * pairs, width), lambda l, x: (0, l, 0, x))] * 2,
        out_shape=(shape, shape),
        scratch_shapes=[pltpu.VMEM((8 * width // LANES, 2 * pairs, LANES), jnp.float32)],
        cost_estimate=pl.CostEstimate(
            flops=4 * grid.size, bytes_accessed=5 * grid.size, transcendentals=0
        ),
        name="tendencies",
    )(grid)
    rows = 8 * levels * 2 * pairs
    return high.reshape(rows, longitudes), low.reshape(rows, longitudes)


def product3(phase_high, phase_low, high, low):
    def one(a, b):
        return lax.dot_general(a, b, ROWS_CONTRACTED, preferred_element_type=jnp.float32)

    return one(phase_high, high) + (one(phase_high, low) + one(phase_low, high))


def first_fourier_kernel(ph_ref, pl_ref, high_ref, low_ref, out_ref):
    out_ref[...] = product3(ph_ref[...], pl_ref[...], high_ref[...], low_ref[...])


def second_fourier_kernel(ph_ref, pl_ref, high_ref, low_ref, came_ref, *out_refs):
    total = product3(ph_ref[...], pl_ref[...], high_ref[...], low_ref[...]) + came_ref[...]
    start = 0
    for out_ref in out_refs:
        rows = out_ref.shape[0]
        out_ref[...] = total[start : start + rows]
        start += rows


def fourier(phases, tendencies, came=None, parts=()):
    high, low = tendencies
    orders, longitudes = phases[0].shape
    rows = high.shape[0]
    block = min(512, rows)
    whole = pl.BlockSpec((orders, longitudes), lambda r: (0, 0))
    part = pl.BlockSpec((block, longitudes), lambda r: (r, 0))

    def columns(count):
        return pl.BlockSpec((count, block), lambda r: (0, r))

    cost = pl.CostEstimate(
        flops=6 * orders * longitudes * rows,
        bytes_accessed=4 * rows * (longitudes + orders),
        transcendentals=0,
    )
    if came is None:
        return pl.pallas_call(
            first_fourier_kernel,
            grid=(rows // block,),
            in_specs=[whole, whole, part, part],
            out_specs=columns(orders),
            out_shape=jax.ShapeDtypeStruct((orders, rows), jnp.float32),
            cost_estimate=cost,
            name="fourier_first",
        )(*phases, high, low)
    return pl.pallas_call(
        second_fourier_kernel,
        grid=(rows // block,),
        in_specs=[whole, whole, part, part, columns(orders)],
        out_specs=[columns(count) for count in parts],
        out_shape=[jax.ShapeDtypeStruct((count, rows), jnp.float32) for count in parts],
        cost_estimate=cost,
        name="fourier_second",
    )(*phases, high, low, came)


def legendre_kernel(
    sent, depth, last, parity_ref, zone_ref, tile_ref, place_ref, near_ref, came_ref, weights_ref, *rest
):
    folded = rest[-1]
    step = pl.program_id(0)
    count = near_ref.shape[0] // 2
    span = 2 * depth
    batch = near_ref.shape[1] // span
    width = weights_ref.shape[4]

    @pl.when(tile_ref[step] == 0)
    def _():
        total = near_ref[...] + came_ref[...]
        rows = total.reshape(2 * count, batch, span).astype(jnp.bfloat16)
        parity = lax.broadcasted_iota(jnp.int32, (2 * batch, span), 1) % 2
        for r in range(count):
            both = jnp.concatenate([rows[r], rows[count + r]], 0)
            zero = jnp.zeros_like(both)
            folded[r, : 2 * batch] = jnp.where(parity == 0, both, zero)
            folded[r, 2 * batch :] = jnp.where(parity == 1, both, zero)

    start = pl.multiple_of(place_ref[step], LANES)
    values = []
    for r in range(count):
        weights = weights_ref[0, r].reshape(span, width)
        value = jnp.dot(folded[r], weights, preferred_element_type=jnp.float32)
        values += [(r, e, value[e * 2 * batch : (e + 1) * 2 * batch]) for e in range(2)]
    if sent:
        for r, e, value in values:
            rest[0][r, e, :, pl.ds(start, width)] = value
        return
    add_ref, down_ref, up_ref = rest[:3]
    skip = add_ref.shape[3] - down_ref.shape[3]
    sums = [(r, e, value + add_ref[r, e, :, pl.ds(start, width)]) for r, e, value in values]

    @pl.when(zone_ref[step] < last)
    def _():
        for r, e, value in sums:
            down_ref[r, e, :, pl.ds(pl.multiple_of(start - skip, LANES), width)] = value

    @pl.when(zone_ref[step] > 0)
    def _():
        for r, e, value in sums:
            up_ref[r, e, :, pl.ds(start, width)] = value


def degree_plan(zones, half_degrees):
    widths = [-(-(half_degrees - half_degrees * z // zones) // LANES) * LANES for z in range(zones)]
    tile = min(2 * LANES, half_degrees)
    order = list(range(zones))[::-1]
    places, start = [0] * zones, 0
    for z in order:
        places[z] = start
        start += widths[z]
    steps = [(z, k, places[z] + k * tile) for z in order for k in range(-(-widths[z] // tile))]
    return widths, places, start, tile, np.array(steps, np.int32)


def project(plan, parity, place, count, own, near, came, weights, add=None):
    widths, places, total, tile, steps = plan
    zones = len(widths)
    depth = weights.shape[2]
    rows = near.shape[1]
    batch = rows // (2 * depth)
    first = 0 if add is not None else 1

    def rows_of(step, parity, zone, tile_, place_):
        return (first * zones + zone[step], 0)

    def weights_of(step, parity, zone, tile_, place_):
        return (0, (2 * zone[step] + parity[0]) * (own // count) + place // count, 0, 0, tile_[step])

    def lanes(width):
        return pl.BlockSpec((count, 2, 2 * batch, width), lambda step, *_: (0, 0, 0, 0))

    kept = [total - widths[-1], places[0] + tile - LANES]
    outs = [total] if add is None else kept
    in_specs = [
        pl.BlockSpec((2 * count, rows), rows_of),
        pl.BlockSpec((2 * count, rows), rows_of),
        pl.BlockSpec((1, count, depth, 2, tile), weights_of),
    ]
    operands = [near, came, weights]
    if add is not None:
        in_specs.append(lanes(total))
        operands.append(add)

    def kernel(*refs):
        legendre_kernel(add is None, depth, zones - 1, *refs)

    cells = len(steps) * count * tile
    return pl.pallas_call(
        kernel,
        grid_spec=pltpu.PrefetchScalarGridSpec(
            num_scalar_prefetch=4,
            grid=(len(steps),),
            in_specs=in_specs,
            out_specs=[lanes(width) for width in outs],
            scratch_shapes=[pltpu.VMEM((count, 4 * batch, 2 * depth), jnp.bfloat16)],
        ),
        out_shape=[
            jax.ShapeDtypeStruct((count, 2, 2 * batch, width), jnp.float32) for width in outs
        ],
        cost_estimate=pl.CostEstimate(
            flops=4 * cells * 4 * batch * depth,
            bytes_accessed=4 * cells * depth + 8 * count * batch * total,
            transcendentals=0,
        ),
        name="legendre_kept" if add is not None else "legendre_sent",
    )(parity.astype(jnp.int32).reshape(1), *[jnp.asarray(steps[:, k]) for k in range(3)], *operands)


def hop(value, source, target):
    pairs = [(2 * source + x, 2 * target + x) for x in range(2)]
    return lax.ppermute(value, "lat", pairs)


def after(value, *earlier):
    return lax.optimization_barrier((value, *earlier))[0]


def sizes(own):
    unit = own // 8
    if unit % 4:
        return [[own]]
    return [[unit * k for k in group] for group in SPLIT]


def local(grid, legendre):
    lon_count, lat_count = lax.axis_size("lon"), lax.axis_size("lat")
    lon, lat = lax.axis_index("lon"), lax.axis_index("lat")
    levels, longitudes = grid.shape[1], grid.shape[4]
    nlon = longitudes * lon_count
    per, half_degrees = legendre.shape[1], legendre.shape[4]
    own, zones = per // lat_count, lat_count // 2
    waves = per * lon_count
    side, zone = lat % 2, lat // 2
    plan = degree_plan(zones, half_degrees)
    widths, places, total = plan[:3]

    tendencies = folded_tendencies(grid)

    longitude = lon * longitudes + lax.iota(jnp.int32, longitudes)

    def table(wavenumbers, scale):
        product = wavenumbers[..., None] * longitude % nlon
        angles = product.astype(jnp.float32) * (2.0 * math.pi / nlon)
        return jnp.cos(angles) * scale, jnp.sin(angles) * scale

    bands = jnp.stack([2 * lax.iota(jnp.int32, zones) + (side ^ k) for k in range(2)], 0)
    coarse = table(lon_count * own * bands.reshape(-1), 1.0)
    keep = list(range(lon_count - 2, -1, -2))
    halves = [keep[: len(keep) // 2], keep[len(keep) // 2 :]]

    def phases(bit, chunks):
        blocks = []
        for rels in halves:
            for place, count in chunks:
                fine = lon_count * (place + lax.iota(jnp.int32, count))
                fine = jnp.stack([lon ^ (rel | bit) for rel in rels])[:, None] + fine
                cos, sin = table(fine, 1.0 / math.sqrt(nlon))
                first = jnp.concatenate([cos, -sin], 1)[:, None]
                second = jnp.concatenate([sin, cos], 1)[:, None]
                both = coarse[0][:, None] * first - coarse[1][:, None] * second
                blocks.append(both.reshape(-1, longitudes))
        both = jnp.concatenate(blocks, 0)
        top = lax.reduce_precision(both, 8, 7)
        return top.astype(jnp.bfloat16), (both - top).astype(jnp.bfloat16)

    def lon_swap(value, bit):
        return lax.ppermute(value, "lon", [(i, i ^ bit) for i in range(lon_count)])

    groups, place = [], 0
    for group in sizes(own):
        chunks = []
        for count in group:
            chunks.append((place, count))
            place += count
        groups.append(chunks)

    swapped, before = [], None
    for chunks in groups:
        here = tendencies if before is None else (after(tendencies[0], before), tendencies[1])
        ready = phases(1, chunks)
        before = fourier(ready, here)
        swapped.append(lon_swap(before, 1))
    pieces = []
    for chunks, came in zip(groups, swapped):
        parts = [len(keep) // 2 * 4 * zones * count for _, count in chunks] * 2
        here = (after(tendencies[0], before), tendencies[1])
        ready = phases(0, chunks)
        blocks = fourier(ready, here, came, parts)
        before = blocks[-1]
        for k, (place, count) in enumerate(chunks):
            far, near = blocks[k], blocks[len(chunks) + k]
            bit = lon_count // 2
            while bit > 2:
                near = near + lon_swap(far, bit)
                rows = near.shape[0] // 2
                far, near = near[:rows], near[rows:]
                bit //= 2
            pieces.append((place, count, near, lon_swap(far, bit)))

    def finish(count, place, mine):
        mine = mine.reshape(count, 2, 2, 8, levels, half_degrees).transpose(0, 3, 4, 2, 1, 5)
        wavenumber = lon + lon_count * (lat * own + place + lax.iota(jnp.int32, count))
        degree = (
            2 * lax.iota(jnp.int32, half_degrees)[None, None, :]
            + lax.iota(jnp.int32, 2)[None, :, None]
        )
        inside = wavenumber[:, None, None] + degree < waves
        return jnp.where(inside[:, None, None, None, :, :], mine, jnp.zeros((), jnp.float32))

    result = jnp.zeros((own, 8, levels, 2, 2, half_degrees), jnp.float32)
    given, chains, states, kept = [None] * len(pieces), [], [], []

    def send(k):
        place, count, near, came = pieces[k]
        if k > 1:
            near = after(near, *kept[k - 2])
        (value,) = project(plan, 1 - side, place, count, own, near, came, legendre)
        given[k] = lax.ppermute(value, "lat", [(i, i ^ 1) for i in range(lat_count)])

    for k, (place, count, near, came) in enumerate(pieces):
        if k == 0:
            send(0)
        if k + 1 < len(pieces):
            send(k + 1)
        waits = []
        for number, chain in enumerate(chains):
            state = next(chain, None)
            if state is not None:
                states[number] = state
                waits.extend(state)
        near = after(near, *waits) if waits else near
        block = project(plan, side, place, count, own, near, came, legendre, given[k])
        kept.append(block)
        chains.append(line(block, zones, zone, plan, half_degrees))
        states.append(next(chains[-1]))
    for k, chain in enumerate(chains):
        for state in chain:
            states[k] = state
        place, count = pieces[k][:2]
        mine = finish(count, place, states[k][0])
        result = lax.dynamic_update_slice(result, mine, (place,) + (0,) * 5)
    return result[None]


def line(block, zones, zone, plan, half_degrees):
    widths, places, _ = plan[:3]
    downs, ups = [block[0]], [block[1]]
    came_down, came_up = [], []
    for k in range(zones - 1):
        came_down.append(hop(downs[k], zones - 1 - k, zones - 2 - k))
        came_up.append(hop(ups[k], k, k + 1))
        yield (downs[k], ups[k])
        if k < zones - 2:
            cut = widths[zones - 2 - k]
            downs.append(downs[k][..., cut:] + came_down[k][..., cut:])
            ups.append(ups[k][..., : places[k + 1]] + came_up[k][..., : places[k + 1]])
    downs, ups, came_down, came_up = lax.optimization_barrier((downs, ups, came_down, came_up))
    mine = None
    for z in range(zones):
        width = widths[z]
        if z == zones - 1:
            value = ups[0][..., :width]
        else:
            k = zones - 2 - z
            value = downs[k][..., :width] + came_down[k][..., :width]
        if z > 0:
            value = value + came_up[z - 1][..., places[z] : places[z] + width]
        value = jnp.pad(value, ((0, 0), (0, 0), (0, 0), (0, half_degrees - width)))
        mine = value if mine is None else jnp.where(zone == z, value, mine)
    yield (mine,)


def solution(mesh):
    in_specs = (P(None, None, None, "lat", "lon"), P("lon", None, "lat", None, None))
    out_specs = P("lon", "lat", None, None, None, None, None)

    return jax.shard_map(local, mesh=mesh, in_specs=in_specs, out_specs=out_specs, check_vma=False)
```

time: 929 us -> 603 us (0.65)
  waiting for transfers between devices: 601 us -> 150 us
  Pallas kernels: 0 us -> 187 us
  matrix products: 143 us -> 0 us
  starting transfers between devices: 1.54 us -> 131 us
  local copies, waits for them, and re-layouts: 115 us -> 24.3 us
  other arithmetic: 48.9 us -> 101 us
  between operations: 13.4 us -> 1.3 us
    reduce_scatter x3 -> x0, waiting for transfers between devices: 497 us -> none  [the longest x2 344 us: spectra_level(): lax.psum_scatter(jnp.einsum('ecsklj,sjeh->sklceh', window, section, prefe...]
    pallas_call x0 -> x17, Pallas kernels: none -> 187 us  [the longest x12 95.5 us: project(): pl.pallas_call(kernel, grid_spec=pltpu.PrefetchScalarGridSpec(num_scalar_...]
    dot_general x3 -> x0, matrix products: 143 us -> none  [the longest x1 114 us: spectra_level(): lax.dot_general(section, flattened, (((3,), (1,)), ((), ())), precision=l...]
    ppermute x1 -> x50, starting transfers between devices: 1.45 us -> 131 us  [the longest x36 113 us: hop(): return lax.ppermute(value, 'lat', pairs)]
    add x5 -> x60, other arithmetic: 0.74 us -> 59.5 us  [the longest x18 21.8 us: line(): value = value + came_up[z - 1][..., places[z]:places[z] + width]]
    ppermute x1 -> x50, waiting for transfers between devices: 104 us -> 150 us  [the longest x8 76.3 us: lon_swap(): return lax.ppermute(value, 'lon', [(i, i ^ bit) for i in range(lon_count)])]
    unnamed x3 -> x86, local copies, waits for them, and re-layouts: 54.9 us -> 11.2 us
    slice x2 -> x0, local copies, waits for them, and re-layouts: 25.2 us -> none  [the longest x1 14.1 us: spectra_level(): weights_high = weights[:half_rows, :, :, quarter:]]
  transfers between devices with their start and end apart: 4 -> 50, of which waited for: 4 -> 11; matrix products, arithmetic and copies ran while one was open for 11% -> 16% of each run, Pallas kernels for 0% -> 26%
where the time goes in v1:
time: 603 us; the launch traced here: 594 us
  Pallas kernels  187 us (31%)
  waiting for transfers between devices  150 us (25%)
  starting transfers between devices  131 us (22%)
  other arithmetic  101 us (17%)
  local copies, waits for them, and re-layouts  24.3 us (4%)
    ppermute x36, starting transfers between devices, hop(): return lax.ppermute(value, 'lat', pairs)  113 us
    pallas_call x12, Pallas kernels, project(): pl.pallas_call(kernel, grid_spec=pltpu.PrefetchScalarGridSpec(num_scalar_...  95.5 us
    ppermute x8, waiting for transfers between devices, lon_swap(): return lax.ppermute(value, 'lon', [(i, i ^ bit) for i in range(lon_count)])  76.3 us
    ppermute x36, waiting for transfers between devices, hop(): return lax.ppermute(value, 'lat', pairs)  65.9 us
    pallas_call x2, Pallas kernels, fourier(): pl.pallas_call(second_fourier_kernel, grid=(rows // block,), in_specs=[wh...  38.9 us
    pallas_call x2, Pallas kernels, fourier(): pl.pallas_call(first_fourier_kernel, grid=(rows // block,), in_specs=[who...  36.6 us
    add x18, other arithmetic, line(): value = value + came_up[z - 1][..., places[z]:places[z] + width]  21.8 us
    add x12, other arithmetic, line(): ups.append(ups[k][..., :places[k + 1]] + came_up[k][..., :places[k + 1]])  18.9 us
  transfers between devices with their start and end apart: 50, of which 11 were waited for; matrix products, arithmetic and copies ran while one was open for 16% of the time, Pallas kernels for 26%

profile of v1, /device:TPU:0, one launch (start us, length us, event | category | flops | bytes accessed | tf_op | source)
XLA Modules:
  0.0 594.0 jit_solution(7638384513815951178)
XLA Ops:
  6.5 2.2 fusion.116
  16.4 16.3 %tendencies.1 = (bf16[8,2,256,1024]{3,2,1,0:T(8,128)(2,1)}, bf16[8,2,256,1024]{3,2,1,0:T(8,128)(2,1)}) custom-call(bf16[12,2,2,128,1024]{4,3,2,1,0:T(8,128)(2,1)} %grid_ref.1), custom_call_target="tpu_custom_call" | custom-call | flops 25165824 | bytes 31457280 | tf_op jit(solution)/shard_map/tendencies/pallas_call | solution.py:56
  32.7 18.2 %fourier_first.2 = f32[512,4096]{1,0:T(8,128)} custom-call(bf16[512,1024]{1,0:T(8,128)(2,1)} %get-tuple-element.204.ph_ref, bf16[512,1024]{1,0:T(8,128)(2,1)} %get-tuple-element.203.pl_ref, bf16[4096,1024]{1,0:T(8,128)(2,1)} %bitcast.184, bf16[4096,1024]{1,0:T(8,128)(2,1)} %bitcast.188), custom_call_target="tpu_custom_call" | custom-call | flops 12884901888 | bytes 25165824 | tf_op jit(solution)/shard_map/fourier_first/pallas_call | solution.py:111
  54.1 18.4 %fourier_first.3 = f32[512,4096]{1,0:T(8,128)} custom-call(bf16[512,1024]{1,0:T(8,128)(2,1)} %get-tuple-element.206.ph_ref, bf16[512,1024]{1,0:T(8,128)(2,1)} %get-tuple-element.205.pl_ref, bf16[4096,1024]{1,0:T(8,128)(2,1)} %bitcast.185, bf16[4096,1024]{1,0:T(8,128)(2,1)} %bitcast.189), custom_call_target="tpu_custom_call" | custom-call | flops 12884901888 | bytes 25165824 | tf_op jit(solution)/shard_map/fourier_first/pallas_call | solution.py:111
  74.3 19.4 %fourier_second.2 = (f32[64,4096]{1,0:T(8,128)}, f32[64,4096]{1,0:T(8,128)}, f32[128,4096]{1,0:T(8,128)}, f32[64,4096]{1,0:T(8,128)}, f32[64,4096]{1,0:T(8,128)}, /*index=5*/f32[128,4096]{1,0:T(8,128)}) custom-call(bf16[512,1024]{1,0:T(8,128)(2,1)} %get-tuple-element.208.ph_ref, bf16[512,1024]{1,0:T(8,128)(2,1)} %get-tuple-element.207.pl_ref, ...), custom_call_target="tpu_custom_call" | custom-call | flops 12884901888 | bytes 25165824 | tf_op jit(solution)/shard_map/fourier_second/pallas_call | solution.py:120
  93.7 3.0 collective-permute-start.1
  96.8 24.1 %collective-permute-done.1.refs_5_ = f32[64,4096]{1,0:T(8,128)S(1)} collective-permute-done((f32[64,4096]{1,0:T(8,128)}, f32[64,4096]{1,0:T(8,128)S(1)}, u32[]{:S(2)}, u32[]{:S(2)}) %collective-permute-start.1) | collective-permute-done | bytes 1048608 | tf_op jit(solution)/shard_map/ppermute | solution.py:301
  121.9 6.8 %legendre_sent.6 = f32[4,2,32,1280]{3,2,1,0:T(8,128)} custom-call(s32[1]{0:T(128)} %bitcast.57.refs_0_, s32[6]{0:T(128)} %constant.224.clone.refs_1_, s32[6]{0:T(128)} %constant.225.clone.refs_2_, s32[6]{0:T(128)} %constant.226.clone.refs_3_, f32[64,4096]{1,0:T(8,128)} %get-tuple-element.107.refs_4_, f32[64,4096]{1,0:T(8,128)} %copy-done.6, ...), custom_call_target="tpu_custom_call" | custom-call | flops 201326592 | bytes 3801088 | tf_op jit(solution)/shard_map/legendre_sent/pallas_call | solution.py:222
  128.7 2.0 collective-permute-start.2
  132.2 3.3 fusion.3
  135.5 52.2 %collective-permute-done.9.refs_5_ = f32[64,4096]{1,0:T(8,128)S(1)} collective-permute-done((f32[64,4096]{1,0:T(8,128)}, f32[64,4096]{1,0:T(8,128)S(1)}, u32[]{:S(2)}, u32[]{:S(2)}) %collective-permute-start.9) | collective-permute-done | bytes 1048608 | tf_op jit(solution)/shard_map/ppermute | solution.py:301
  188.7 6.7 %legendre_sent.7 = f32[4,2,32,1280]{3,2,1,0:T(8,128)} custom-call(s32[1]{0:T(128)} %bitcast.57.refs_0_, s32[6]{0:T(128)} %constant.224.clone.refs_1_, s32[6]{0:T(128)} %constant.225.clone.refs_2_, s32[6]{0:T(128)} %constant.226.clone.refs_3_, f32[64,4096]{1,0:T(8,128)} %get-tuple-element.122.refs_4_, f32[64,4096]{1,0:T(8,128)} %copy-done.5, ...), custom_call_target="tpu_custom_call" | custom-call | flops 201326592 | bytes 3801088 | tf_op jit(solution)/shard_map/legendre_sent/pallas_call | solution.py:222
  197.1 7.6 %legendre_kept.6 = (f32[4,2,32,1152]{3,2,1,0:T(8,128)}, f32[4,2,32,896]{3,2,1,0:T(8,128)}) custom-call(s32[1]{0:T(128)} %bitcast.refs_0_, s32[6]{0:T(128)} %constant.224.clone.refs_1_, s32[6]{0:T(128)} %constant.225.clone.refs_2_, s32[6]{0:T(128)} %constant.226.clone.refs_3_, f32[64,4096]{1,0:T(8,128)} %get-tuple-element.107.refs_4_, f32[64,4096]{1,0:T(8,128)} %copy-done.6, ...), custom_call_target="tpu_custom_call" | custom-call | flops 201326592 | bytes 3801088 | tf_op jit(solution)/shard_map/legendre_kept/pallas_call | solution.py:222
  204.7 3.5 collective-permute-start.5
  211.3 8.7 %legendre_sent.8 = f32[8,2,32,1280]{3,2,1,0:T(8,128)} custom-call(s32[1]{0:T(128)} %bitcast.57.refs_0_, s32[6]{0:T(128)} %constant.224.clone.refs_1_, s32[6]{0:T(128)} %constant.225.clone.refs_2_, s32[6]{0:T(128)} %constant.226.clone.refs_3_, f32[128,4096]{1,0:T(8,128)} %get-tuple-element.139.refs_4_, f32[128,4096]{1,0:T(8,128)} %copy-done.1, ...), custom_call_target="tpu_custom_call" | custom-call | flops 402653184 | bytes 7602176 | tf_op jit(solution)/shard_map/legendre_sent/pallas_call | solution.py:222
  220.5 19.4 %fourier_second.3 = (f32[128,4096]{1,0:T(8,128)}, f32[64,4096]{1,0:T(8,128)}, f32[64,4096]{1,0:T(8,128)}, f32[128,4096]{1,0:T(8,128)}, f32[64,4096]{1,0:T(8,128)}, /*index=5*/f32[64,4096]{1,0:T(8,128)}) custom-call(bf16[512,1024]{1,0:T(8,128)(2,1)} %get-tuple-element.202.ph_ref, bf16[512,1024]{1,0:T(8,128)(2,1)} %get-tuple-element.201.pl_ref, ...), custom_call_target="tpu_custom_call" | custom-call | flops 12884901888 | bytes 25165824 | tf_op jit(solution)/shard_map/fourier_second/pallas_call | solution.py:120
  245.8 7.6 %legendre_kept.7 = (f32[4,2,32,1152]{3,2,1,0:T(8,128)}, f32[4,2,32,896]{3,2,1,0:T(8,128)}) custom-call(s32[1]{0:T(128)} %bitcast.refs_0_, s32[6]{0:T(128)} %constant.224.clone.refs_1_, s32[6]{0:T(128)} %constant.225.clone.refs_2_, s32[6]{0:T(128)} %constant.226.clone.refs_3_, f32[64,4096]{1,0:T(8,128)} %get-tuple-element.122.refs_4_, f32[64,4096]{1,0:T(8,128)} %copy-done.5, ...), custom_call_target="tpu_custom_call" | custom-call | flops 201326592 | bytes 3801088 | tf_op jit(solution)/shard_map/legendre_kept/pallas_call | solution.py:222
  253.4 3.3 collective-permute-start.13
  259.8 15.0 %collective-permute-done.13 = f32[4,2,32,896]{3,2,1,0:T(8,128)S(1)} collective-permute-done((f32[4,2,32,896]{3,2,1,0:T(8,128)}, f32[4,2,32,896]{3,2,1,0:T(8,128)S(1)}, u32[]{:S(2)}, u32[]{:S(2)}) %collective-permute-start.13) | collective-permute-done | bytes 917536 | tf_op jit(solution)/shard_map/ppermute | solution.py:245
  274.8 2.1 slice_add_fusion.20
  279.1 2.9 collective-permute-done.18.refs_7_
  282.0 10.4 %legendre_kept.8 = (f32[8,2,32,1152]{3,2,1,0:T(8,128)}, f32[8,2,32,896]{3,2,1,0:T(8,128)}) custom-call(s32[1]{0:T(128)} %bitcast.refs_0_, s32[6]{0:T(128)} %constant.224.clone.refs_1_, s32[6]{0:T(128)} %constant.225.clone.refs_2_, s32[6]{0:T(128)} %constant.226.clone.refs_3_, f32[128,4096]{1,0:T(8,128)} %get-tuple-element.139.refs_4_, ...), custom_call_target="tpu_custom_call" | custom-call | flops 402653184 | bytes 7602176 | tf_op jit(solution)/shard_map/legendre_kept/pallas_call | solution.py:222
  292.5 2.2 collective-permute-start.19
  296.0 8.7 %legendre_sent.9 = f32[8,2,32,1280]{3,2,1,0:T(8,128)} custom-call(s32[1]{0:T(128)} %bitcast.57.refs_0_, s32[6]{0:T(128)} %constant.224.clone.refs_1_, s32[6]{0:T(128)} %constant.225.clone.refs_2_, s32[6]{0:T(128)} %constant.226.clone.refs_3_, f32[128,4096]{1,0:T(8,128)} %get-tuple-element.156.refs_4_, f32[128,4096]{1,0:T(8,128)} %copy-done, ...), custom_call_target="tpu_custom_call" | custom-call | flops 402653184 | bytes 7602176 | tf_op jit(solution)/shard_map/legendre_sent/pallas_call | solution.py:222
  308.2 9.7 %collective-permute-start.21 = (f32[8,2,32,896]{3,2,1,0:T(8,128)}, f32[8,2,32,896]{3,2,1,0:T(8,128)S(1)}, u32[]{:S(2)}, u32[]{:S(2)}) collective-permute-start(f32[8,2,32,896]{3,2,1,0:T(8,128)} %get-tuple-element.142), channel_id=1, source_target_pairs={{0,2},{1,3},{8,10},{9,11},{16,18},{17,19},{24,26},{25,27}} | collective-permute-start | bytes 5505032 | tf_op jit(solution)/shard_map/ppermute | solution.py:245
  320.5 3.8 collective-permute-done.7
  331.1 22.8 %collective-permute-done.21 = f32[8,2,32,896]{3,2,1,0:T(8,128)S(1)} collective-permute-done((f32[8,2,32,896]{3,2,1,0:T(8,128)}, f32[8,2,32,896]{3,2,1,0:T(8,128)S(1)}, u32[]{:S(2)}, u32[]{:S(2)}) %collective-permute-start.21) | collective-permute-done | bytes 1835040 | tf_op jit(solution)/shard_map/ppermute | solution.py:245
  353.9 2.7 slice_add_fusion.9
  356.6 1.8 slice_add_fusion.1
  358.4 3.9 collective-permute-done.27.refs_7_
  362.4 10.3 %legendre_kept.9 = (f32[8,2,32,1152]{3,2,1,0:T(8,128)}, f32[8,2,32,896]{3,2,1,0:T(8,128)}) custom-call(s32[1]{0:T(128)} %bitcast.refs_0_, s32[6]{0:T(128)} %constant.224.clone.refs_1_, s32[6]{0:T(128)} %constant.225.clone.refs_2_, s32[6]{0:T(128)} %constant.226.clone.refs_3_, f32[128,4096]{1,0:T(8,128)} %get-tuple-element.156.refs_4_, f32[128,4096]{1,0:T(8,128)} %copy-done, ...), custom_call_target="tpu_custom_call" | custom-call | flops 402653184 | bytes 7602176 | tf_op jit(solution)/shard_map/legendre_kept/pallas_call | solution.py:222
  372.6 4.5 collective-permute-start.30
  377.1 2.1 collective-permute-start.28
  379.2 1.9 collective-permute-start.20
  382.4 2.1 reshape.5440
  385.9 2.3 fusion.4
  388.2 6.7 %legendre_sent.10 = f32[4,2,32,1280]{3,2,1,0:T(8,128)} custom-call(s32[1]{0:T(128)} %bitcast.57.refs_0_, s32[6]{0:T(128)} %constant.224.clone.refs_1_, s32[6]{0:T(128)} %constant.225.clone.refs_2_, s32[6]{0:T(128)} %constant.226.clone.refs_3_, f32[64,4096]{1,0:T(8,128)} %get-tuple-element.172.refs_4_, f32[64,4096]{1,0:T(8,128)} %copy-done.4, ...), custom_call_target="tpu_custom_call" | custom-call | flops 201326592 | bytes 3801088 | tf_op jit(solution)/shard_map/legendre_sent/pallas_call | solution.py:222
  400.7 2.0 select_select_fusion.4
  405.9 7.0 %collective-permute-done.30 = f32[8,2,32,896]{3,2,1,0:T(8,128)} collective-permute-done((f32[8,2,32,896]{3,2,1,0:T(8,128)}, f32[8,2,32,896]{3,2,1,0:T(8,128)}, u32[]{:S(2)}, u32[]{:S(2)}) %collective-permute-start.30) | collective-permute-done | bytes 1835040 | tf_op jit(solution)/shard_map/ppermute | solution.py:245
  412.9 2.4 slice_add_fusion.8
  417.0 2.4 slice_add_fusion.3
  420.7 1.8 slice_add_fusion
  423.1 7.6 %legendre_kept.10 = (f32[4,2,32,1152]{3,2,1,0:T(8,128)}, f32[4,2,32,896]{3,2,1,0:T(8,128)}) custom-call(s32[1]{0:T(128)} %bitcast.refs_0_, s32[6]{0:T(128)} %constant.224.clone.refs_1_, s32[6]{0:T(128)} %constant.225.clone.refs_2_, s32[6]{0:T(128)} %constant.226.clone.refs_3_, f32[64,4096]{1,0:T(8,128)} %get-tuple-element.172.refs_4_, f32[64,4096]{1,0:T(8,128)} %copy-done.4, ...), custom_call_target="tpu_custom_call" | custom-call | flops 201326592 | bytes 3801088 | tf_op jit(solution)/shard_map/legendre_kept/pallas_call | solution.py:222
  430.7 1.8 collective-permute-start.36
  432.5 4.1 pad_bitcast_fusion
  440.9 6.8 %legendre_sent.11 = f32[4,2,32,1280]{3,2,1,0:T(8,128)} custom-call(s32[1]{0:T(128)} %bitcast.57.refs_0_, s32[6]{0:T(128)} %constant.224.clone.refs_1_, s32[6]{0:T(128)} %constant.225.clone.refs_2_, s32[6]{0:T(128)} %constant.226.clone.refs_3_, f32[64,4096]{1,0:T(8,128)} %get-tuple-element.188.refs_4_, f32[64,4096]{1,0:T(8,128)} %copy-done.3, ...), custom_call_target="tpu_custom_call" | custom-call | flops 201326592 | bytes 3801088 | tf_op jit(solution)/shard_map/legendre_sent/pallas_call | solution.py:222
  449.3 1.9 collective-permute-start.29
  451.2 1.8 slice_add_fusion.26
  453.0 13.6 %collective-permute-start.38 = (f32[4,2,32,896]{3,2,1,0:T(8,128)}, f32[4,2,32,896]{3,2,1,0:T(8,128)}, u32[]{:S(2)}, u32[]{:S(2)}) collective-permute-start(f32[4,2,32,896]{3,2,1,0:T(8,128)} %get-tuple-element.175), channel_id=1, source_target_pairs={{0,2},{1,3},{8,10},{9,11},{16,18},{17,19},{24,26},{25,27}} | collective-permute-start | bytes 2752520 | tf_op jit(solution)/shard_map/ppermute | solution.py:245
  468.0 1.8 slice_add_fusion.11
  471.1 2.2 slice_add_fusion.5
  475.9 2.9 select_select_fusion.1
  478.8 1.9 reshape.5442
  482.8 2.0 bitcast_dynamic-update-slice_fusion.1
  491.6 7.6 %legendre_kept.11 = (f32[4,2,32,1152]{3,2,1,0:T(8,128)}, f32[4,2,32,896]{3,2,1,0:T(8,128)}) custom-call(s32[1]{0:T(128)} %bitcast.refs_0_, s32[6]{0:T(128)} %constant.224.clone.refs_1_, s32[6]{0:T(128)} %constant.225.clone.refs_2_, s32[6]{0:T(128)} %constant.226.clone.refs_3_, f32[64,4096]{1,0:T(8,128)} %get-tuple-element.188.refs_4_, f32[64,4096]{1,0:T(8,128)} %copy-done.3, ...), custom_call_target="tpu_custom_call" | custom-call | flops 201326592 | bytes 3801088 | tf_op jit(solution)/shard_map/legendre_kept/pallas_call | solution.py:222
  499.2 40.0 %collective-permute-start.46 = (f32[4,2,32,896]{3,2,1,0:T(8,128)}, f32[4,2,32,896]{3,2,1,0:T(8,128)}, u32[]{:S(2)}, u32[]{:S(2)}) collective-permute-start(f32[4,2,32,896]{3,2,1,0:T(8,128)} %get-tuple-element.191), channel_id=1, source_target_pairs={{0,2},{1,3},{8,10},{9,11},{16,18},{17,19},{24,26},{25,27}} | collective-permute-start | bytes 2752520 | tf_op jit(solution)/shard_map/ppermute | solution.py:245
  544.4 2.0 select_select_fusion.3
  547.7 4.5 collective-permute-done.46
  552.3 1.9 slice_add_fusion.18
  555.6 2.5 slice_add_fusion.4
  563.8 2.5 select_select_fusion
  566.3 1.8 reshape.5443
  570.8 2.0 bitcast_dynamic-update-slice_fusion
  575.8 12.6 %collective-permute-done.48 = f32[4,2,32,512]{3,2,1,0:T(8,128)S(1)} collective-permute-done((f32[4,2,32,512]{3,2,1,0:T(8,128)S(1)}, f32[4,2,32,512]{3,2,1,0:T(8,128)S(1)}, u32[]{:S(2)}, u32[]{:S(2)}) %collective-permute-start.48) | collective-permute-done | bytes 524320 | tf_op jit(solution)/shard_map/ppermute | solution.py:245
  (266 shorter events, 112.5 us)
Async XLA Ops:
  50.9 23.4 %collective-permute-start = (f32[512,4096]{1,0:T(8,128)}, f32[512,4096]{1,0:T(8,128)}, u32[]{:S(2)}, u32[]{:S(2)}) collective-permute-start(f32[512,4096]{1,0:T(8,128)} %fourier_first.2), channel_id=1, source_target_pairs={{0,8},{8,0},{16,24},{24,16},{1,9},{9,1},{17,25},{25,17},{2,10},{10... | collective-permute-start | bytes 25165832 | tf_op jit(solution)/shard_map/ppermute | solution.py:301
  54.0 18.4 %copy-start.10 = (f32[512,1024]{1,0:T(8,128)S(1)}, f32[512,1024]{1,0:T(8,128)}, u32[]{:S(2)}) copy-start(f32[512,1024]{1,0:T(8,128)} %get-tuple-element.227) | copy-start | bytes 6291460
  72.5 148.0 %collective-permute-start.25 = (f32[512,4096]{1,0:T(8,128)}, f32[512,4096]{1,0:T(8,128)}, u32[]{:S(2)}, u32[]{:S(2)}) collective-permute-start(f32[512,4096]{1,0:T(8,128)} %fourier_first.3), channel_id=1, source_target_pairs={{0,8},{8,0},{16,24},{24,16},{1,9},{9,1},{17,25},{25,17},{2,10},{10... | collective-permute-start | bytes 25165832 | tf_op jit(solution)/shard_map/ppermute | solution.py:301
  93.7 27.2 %collective-permute-start.1 = (f32[64,4096]{1,0:T(8,128)}, f32[64,4096]{1,0:T(8,128)S(1)}, u32[]{:S(2)}, u32[]{:S(2)}) collective-permute-start(f32[64,4096]{1,0:T(8,128)} %get-tuple-element.108), channel_id=1, source_target_pairs={{0,16},{8,24},{16,0},{24,8},{1,17},{9,25},{17,1},{25,9},{2,18},{10... | collective-permute-start | bytes 3145736 | tf_op jit(solution)/shard_map/ppermute | solution.py:301
  96.7 113.3 %collective-permute-start.17 = (f32[128,4096]{1,0:T(8,128)}, f32[128,4096]{1,0:T(8,128)S(1)}, u32[]{:S(2)}, u32[]{:S(2)}) collective-permute-start(f32[128,4096]{1,0:T(8,128)} %get-tuple-element.138), channel_id=1, source_target_pairs={{0,16},{8,24},{16,0},{24,8},{1,17},{9,25},{17,1},{25,9},{2,18},{10... | collective-permute-start | bytes 6291464 | tf_op jit(solution)/shard_map/ppermute | solution.py:301
  128.7 68.5 %collective-permute-start.2 = (f32[4,2,32,1280]{3,2,1,0:T(8,128)}, f32[4,2,32,1280]{3,2,1,0:T(8,128)}, u32[]{:S(2)}, u32[]{:S(2)}) collective-permute-start(f32[4,2,32,1280]{3,2,1,0:T(8,128)} %legendre_sent.6), channel_id=1, source_target_pairs={{0,1},{1,0},{2,3},{3,2},{4,5},{5,4},{6,7},{7,6},{8,9},{9,8},{10,11... | collective-permute-start | bytes 3932168 | tf_op jit(solution)/shard_map/ppermute | solution.py:352
  130.7 57.0 %collective-permute-start.9 = (f32[64,4096]{1,0:T(8,128)}, f32[64,4096]{1,0:T(8,128)S(1)}, u32[]{:S(2)}, u32[]{:S(2)}) collective-permute-start(f32[64,4096]{1,0:T(8,128)} %get-tuple-element.123), channel_id=1, source_target_pairs={{0,16},{8,24},{16,0},{24,8},{1,17},{9,25},{17,1},{25,9},{2,18},{10... | collective-permute-start | bytes 3145736 | tf_op jit(solution)/shard_map/ppermute | solution.py:301
  195.4 50.4 %collective-permute-start.10 = (f32[4,2,32,1280]{3,2,1,0:T(8,128)}, f32[4,2,32,1280]{3,2,1,0:T(8,128)}, u32[]{:S(2)}, u32[]{:S(2)}) collective-permute-start(f32[4,2,32,1280]{3,2,1,0:T(8,128)} %legendre_sent.7), channel_id=1, source_target_pairs={{0,1},{1,0},{2,3},{3,2},{4,5},{5,4},{6,7},{7,6},{8,9},{9,8},{10,11... | collective-permute-start | bytes 3932168 | tf_op jit(solution)/shard_map/ppermute | solution.py:352
  204.7 36.8 %collective-permute-start.5 = (f32[4,2,32,896]{3,2,1,0:T(8,128)}, f32[4,2,32,896]{3,2,1,0:T(8,128)S(1)}, u32[]{:S(2)}, u32[]{:S(2)}) collective-permute-start(f32[4,2,32,896]{3,2,1,0:T(8,128)} %get-tuple-element.111), channel_id=1, source_target_pairs={{0,2},{1,3},{8,10},{9,11},{16,18},{17,19},{24,26},{25,27}} | collective-permute-start | bytes 2752520 | tf_op jit(solution)/shard_map/ppermute | solution.py:245
  208.3 36.0 %collective-permute-start.3 = (f32[4,2,32,1152]{3,2,1,0:T(8,128)}, f32[4,2,32,1152]{3,2,1,0:T(8,128)}, u32[]{:S(2)}, u32[]{:S(2)}) collective-permute-start(f32[4,2,32,1152]{3,2,1,0:T(8,128)} %get-tuple-element.113), channel_id=1, source_target_pairs={{6,4},{7,5},{14,12},{15,13},{22,20},{23,21},{30,28},{31,29}} | collective-permute-start | bytes 3538952 | tf_op jit(solution)/shard_map/ppermute | solution.py:245
  220.0 62.1 %collective-permute-start.18 = (f32[8,2,32,1280]{3,2,1,0:T(8,128)}, f32[8,2,32,1280]{3,2,1,0:T(8,128)}, u32[]{:S(2)}, u32[]{:S(2)}) collective-permute-start(f32[8,2,32,1280]{3,2,1,0:T(8,128)} %legendre_sent.8), channel_id=1, source_target_pairs={{0,1},{1,0},{2,3},{3,2},{4,5},{5,4},{6,7},{7,6},{8,9},{9,8},{10,11... | collective-permute-start | bytes 7864328 | tf_op jit(solution)/shard_map/ppermute | solution.py:352
  239.9 54.7 %collective-permute-start.26 = (f32[128,4096]{1,0:T(8,128)}, f32[128,4096]{1,0:T(8,128)S(1)}, u32[]{:S(2)}, u32[]{:S(2)}) collective-permute-start(f32[128,4096]{1,0:T(8,128)} %get-tuple-element.155), channel_id=1, source_target_pairs={{0,16},{8,24},{16,0},{24,8},{1,17},{9,25},{17,1},{25,9},{2,18},{10... | collective-permute-start | bytes 6291464 | tf_op jit(solution)/shard_map/ppermute | solution.py:301
  242.8 14.6 %collective-permute-start.6 = (f32[4,2,32,384]{3,2,1,0:T(8,128)S(1)}, f32[4,2,32,384]{3,2,1,0:T(8,128)}, u32[]{:S(2)}, u32[]{:S(2)}) collective-permute-start(f32[4,2,32,384]{3,2,1,0:T(8,128)S(1)} %slice_add_fusion.21), channel_id=1, source_target_pairs={{2,4},{3,5},{10,12},{11,13},{18,20},{19,21},{26,28},{27,29}} | collective-permute-start | bytes 1179656 | tf_op jit(solution)/shard_map/ppermute | solution.py:245
  245.8 31.0 %copy-start.8 = (f32[4,2,32,896]{3,2,1,0:T(8,128)}, f32[4,2,32,896]{3,2,1,0:T(8,128)S(1)}, u32[]{:S(2)}) copy-start(f32[4,2,32,896]{3,2,1,0:T(8,128)S(1)} %slice_add_fusion.7) | copy-start | bytes 2752516
  253.4 24.3 %copy-start.19 = (f32[4,2,32,1152]{3,2,1,0:T(8,128)S(1)}, f32[4,2,32,1152]{3,2,1,0:T(8,128)}, u32[]{:S(2)}) copy-start(f32[4,2,32,1152]{3,2,1,0:T(8,128)} %get-tuple-element.128) | copy-start | bytes 3538948
  253.4 21.3 %collective-permute-start.13 = (f32[4,2,32,896]{3,2,1,0:T(8,128)}, f32[4,2,32,896]{3,2,1,0:T(8,128)S(1)}, u32[]{:S(2)}, u32[]{:S(2)}) collective-permute-start(f32[4,2,32,896]{3,2,1,0:T(8,128)} %get-tuple-element.126), channel_id=1, source_target_pairs={{0,2},{1,3},{8,10},{9,11},{16,18},{17,19},{24,26},{25,27}} | collective-permute-start | bytes 2752520 | tf_op jit(solution)/shard_map/ppermute | solution.py:245
  256.7 20.1 %collective-permute-start.4 = (f32[4,2,32,896]{3,2,1,0:T(8,128)S(1)}, f32[4,2,32,896]{3,2,1,0:T(8,128)S(1)}, u32[]{:S(2)}, u32[]{:S(2)}) collective-permute-start(f32[4,2,32,896]{3,2,1,0:T(8,128)S(1)} %slice_add_fusion.7), channel_id=1, source_target_pairs={{4,2},{5,3},{12,10},{13,11},{20,18},{21,19},{28,26},{29,27}} | collective-permute-start | bytes 2752520 | tf_op jit(solution)/shard_map/ppermute | solution.py:245
  257.5 20.3 %collective-permute-start.11 = (f32[4,2,32,1152]{3,2,1,0:T(8,128)}, f32[4,2,32,1152]{3,2,1,0:T(8,128)S(1)}, u32[]{:S(2)}, u32[]{:S(2)}) collective-permute-start(f32[4,2,32,1152]{3,2,1,0:T(8,128)} %get-tuple-element.128), channel_id=1, source_target_pairs={{6,4},{7,5},{14,12},{15,13},{22,20},{23,21},{30,28},{31,29}} | collective-permute-start | bytes 3538952 | tf_op jit(solution)/shard_map/ppermute | solution.py:245
  292.4 13.7 %copy-start.26 = (f32[4,2,32,384]{3,2,1,0:T(8,128)S(1)}, f32[4,2,32,384]{3,2,1,0:T(8,128)}, u32[]{:S(2)}) copy-start(f32[4,2,32,384]{3,2,1,0:T(8,128)} %slice_add_fusion.20) | copy-start | bytes 1179652
  292.4 25.4 %copy-start.38 = (s32[4]{0:T(128)S(1)}, s32[4]{0:T(128)}, u32[]{:S(2)}) copy-start(s32[4]{0:T(128)} %get-tuple-element.428) | copy-start | bytes 52
  292.4 25.4 %copy-start.39 = (s32[4]{0:T(128)S(1)}, s32[4]{0:T(128)}, u32[]{:S(2)}) copy-start(s32[4]{0:T(128)} %get-tuple-element.426) | copy-start | bytes 52
  292.4 26.2 %copy-start.31 = (f32[4,2,32,128]{3,2,1,0:T(8,128)S(1)}, f32[4,2,32,128]{3,2,1,0:T(8,128)}, u32[]{:S(2)}) copy-start(f32[4,2,32,128]{3,2,1,0:T(8,128)} %slice_add_fusion.37) | copy-start | bytes 393220
  292.5 64.1 %collective-permute-start.19 = (f32[8,2,32,1152]{3,2,1,0:T(8,128)}, f32[8,2,32,1152]{3,2,1,0:T(8,128)}, u32[]{:S(2)}, u32[]{:S(2)}) collective-permute-start(f32[8,2,32,1152]{3,2,1,0:T(8,128)} %get-tuple-element.144), channel_id=1, source_target_pairs={{6,4},{7,5},{14,12},{15,13},{22,20},{23,21},{30,28},{31,29}} | collective-permute-start | bytes 7077896 | tf_op jit(solution)/shard_map/ppermute | solution.py:245
  304.7 57.7 %collective-permute-start.27 = (f32[8,2,32,1280]{3,2,1,0:T(8,128)}, f32[8,2,32,1280]{3,2,1,0:T(8,128)}, u32[]{:S(2)}, u32[]{:S(2)}) collective-permute-start(f32[8,2,32,1280]{3,2,1,0:T(8,128)} %legendre_sent.9), channel_id=1, source_target_pairs={{0,1},{1,0},{2,3},{3,2},{4,5},{5,4},{6,7},{7,6},{8,9},{9,8},{10,11... | collective-permute-start | bytes 7864328 | tf_op jit(solution)/shard_map/ppermute | solution.py:352
  306.1 12.5 %collective-permute-start.14 = (f32[4,2,32,384]{3,2,1,0:T(8,128)S(1)}, f32[4,2,32,384]{3,2,1,0:T(8,128)S(1)}, u32[]{:S(2)}, u32[]{:S(2)}) collective-permute-start(f32[4,2,32,384]{3,2,1,0:T(8,128)S(1)} %copy-done.26), channel_id=1, source_target_pairs={{2,4},{3,5},{10,12},{11,13},{18,20},{19,21},{26,28},{27,29}} | collective-permute-start | bytes 1179656 | tf_op jit(solution)/shard_map/ppermute | solution.py:245
  306.8 22.6 %copy-start.34 = (s32[2,512]{1,0:T(2,128)}, s32[2,512]{1,0:T(2,128)S(1)}, u32[]{:S(2)}) copy-start(s32[2,512]{1,0:T(2,128)S(1)} %iota_add_fusion.1) | copy-start | bytes 12292
  306.9 17.4 %collective-permute-start.7 = (f32[4,2,32,512]{3,2,1,0:T(8,128)S(1)}, f32[4,2,32,512]{3,2,1,0:T(8,128)S(1)}, u32[]{:S(2)}, u32[]{:S(2)}) collective-permute-start(f32[4,2,32,512]{3,2,1,0:T(8,128)S(1)} %slice_add_fusion.15), channel_id=1, source_target_pairs={{2,0},{3,1},{10,8},{11,9},{18,16},{19,17},{26,24},{27,25}} | collective-permute-start | bytes 1572872 | tf_op jit(solution)/shard_map/ppermute | solution.py:245
  308.2 45.8 %collective-permute-start.21 = (f32[8,2,32,896]{3,2,1,0:T(8,128)}, f32[8,2,32,896]{3,2,1,0:T(8,128)S(1)}, u32[]{:S(2)}, u32[]{:S(2)}) collective-permute-start(f32[8,2,32,896]{3,2,1,0:T(8,128)} %get-tuple-element.142), channel_id=1, source_target_pairs={{0,2},{1,3},{8,10},{9,11},{16,18},{17,19},{24,26},{25,27}} | collective-permute-start | bytes 5505032 | tf_op jit(solution)/shard_map/ppermute | solution.py:245
  318.6 1.3 collective-permute-start.8
  320.0 64.6 %collective-permute-start.34 = (f32[64,4096]{1,0:T(8,128)}, f32[64,4096]{1,0:T(8,128)S(1)}, u32[]{:S(2)}, u32[]{:S(2)}) collective-permute-start(f32[64,4096]{1,0:T(8,128)} %get-tuple-element.171), channel_id=1, source_target_pairs={{0,16},{8,24},{16,0},{24,8},{1,17},{9,25},{17,1},{25,9},{2,18},{10... | collective-permute-start | bytes 3145736 | tf_op jit(solution)/shard_map/ppermute | solution.py:301
  324.3 5.1 collective-permute-start.12
  329.4 27.2 %copy-start.11 = (f32[8,2,32,1152]{3,2,1,0:T(8,128)S(1)}, f32[8,2,32,1152]{3,2,1,0:T(8,128)}, u32[]{:S(2)}) copy-start(f32[8,2,32,1152]{3,2,1,0:T(8,128)} %get-tuple-element.144) | copy-start | bytes 7077892
  329.5 27.1 %copy-start.23 = (f32[4,2,32,896]{3,2,1,0:T(8,128)}, f32[4,2,32,896]{3,2,1,0:T(8,128)S(1)}, u32[]{:S(2)}) copy-start(f32[4,2,32,896]{3,2,1,0:T(8,128)S(1)} %collective-permute-done.12) | copy-start | bytes 2752516
  329.5 66.9 %collective-permute-start.15 = (f32[4,2,32,512]{3,2,1,0:T(8,128)S(1)}, f32[4,2,32,512]{3,2,1,0:T(8,128)}, u32[]{:S(2)}, u32[]{:S(2)}) collective-permute-start(f32[4,2,32,512]{3,2,1,0:T(8,128)S(1)} %slice_add_fusion.14), channel_id=1, source_target_pairs={{2,0},{3,1},{10,8},{11,9},{18,16},{19,17},{26,24},{27,25}} | collective-permute-start | bytes 1572872 | tf_op jit(solution)/shard_map/ppermute | solution.py:245
  358.4 58.5 %copy-start.2 = (f32[8,2,32,896]{3,2,1,0:T(8,128)}, f32[8,2,32,896]{3,2,1,0:T(8,128)S(1)}, u32[]{:S(2)}) copy-start(f32[8,2,32,896]{3,2,1,0:T(8,128)S(1)} %slice_add_fusion.1) | copy-start | bytes 5505028
  358.4 26.1 %copy-start.32 = (f32[4,2,32,128]{3,2,1,0:T(8,128)S(1)}, f32[4,2,32,128]{3,2,1,0:T(8,128)}, u32[]{:S(2)}) copy-start(f32[4,2,32,128]{3,2,1,0:T(8,128)} %slice_add_fusion.36) | copy-start | bytes 393220
  372.6 40.3 %collective-permute-start.30 = (f32[8,2,32,896]{3,2,1,0:T(8,128)}, f32[8,2,32,896]{3,2,1,0:T(8,128)}, u32[]{:S(2)}, u32[]{:S(2)}) collective-permute-start(f32[8,2,32,896]{3,2,1,0:T(8,128)} %get-tuple-element.159), channel_id=1, source_target_pairs={{0,2},{1,3},{8,10},{9,11},{16,18},{17,19},{24,26},{25,27}} | collective-permute-start | bytes 5505032 | tf_op jit(solution)/shard_map/ppermute | solution.py:245
  377.1 43.6 %collective-permute-start.28 = (f32[8,2,32,1152]{3,2,1,0:T(8,128)}, f32[8,2,32,1152]{3,2,1,0:T(8,128)}, u32[]{:S(2)}, u32[]{:S(2)}) collective-permute-start(f32[8,2,32,1152]{3,2,1,0:T(8,128)} %get-tuple-element.161), channel_id=1, source_target_pairs={{6,4},{7,5},{14,12},{15,13},{22,20},{23,21},{30,28},{31,29}} | collective-permute-start | bytes 7077896 | tf_op jit(solution)/shard_map/ppermute | solution.py:245
  379.2 37.8 %collective-permute-start.20 = (f32[8,2,32,896]{3,2,1,0:T(8,128)S(1)}, f32[8,2,32,896]{3,2,1,0:T(8,128)}, u32[]{:S(2)}, u32[]{:S(2)}) collective-permute-start(f32[8,2,32,896]{3,2,1,0:T(8,128)S(1)} %slice_add_fusion.1), channel_id=1, source_target_pairs={{4,2},{5,3},{12,10},{13,11},{20,18},{21,19},{28,26},{29,27}} | collective-permute-start | bytes 5505032 | tf_op jit(solution)/shard_map/ppermute | solution.py:245
  384.6 10.4 %collective-permute-start.16 = (f32[4,2,32,128]{3,2,1,0:T(8,128)S(1)}, f32[4,2,32,128]{3,2,1,0:T(8,128)}, u32[]{:S(2)}, u32[]{:S(2)}) collective-permute-start(f32[4,2,32,128]{3,2,1,0:T(8,128)S(1)} %copy-done.32), channel_id=1, source_target_pairs={{4,6},{5,7},{12,14},{13,15},{20,22},{21,23},{28,30},{29,31}} | collective-permute-start | bytes 393224 | tf_op jit(solution)/shard_map/ppermute | solution.py:245
  395.0 28.2 %collective-permute-start.35 = (f32[4,2,32,1280]{3,2,1,0:T(8,128)}, f32[4,2,32,1280]{3,2,1,0:T(8,128)}, u32[]{:S(2)}, u32[]{:S(2)}) collective-permute-start(f32[4,2,32,1280]{3,2,1,0:T(8,128)} %legendre_sent.10), channel_id=1, source_target_pairs={{0,1},{1,0},{2,3},{3,2},{4,5},{5,4},{6,7},{7,6},{8,9},{9,8},{10,11... | collective-permute-start | bytes 3932168 | tf_op jit(solution)/shard_map/ppermute | solution.py:352
  396.5 6.2 %collective-permute-start.22 = (f32[8,2,32,384]{3,2,1,0:T(8,128)}, f32[8,2,32,384]{3,2,1,0:T(8,128)S(1)}, u32[]{:S(2)}, u32[]{:S(2)}) collective-permute-start(f32[8,2,32,384]{3,2,1,0:T(8,128)} %slice_add_fusion.9), channel_id=1, source_target_pairs={{2,4},{3,5},{10,12},{11,13},{18,20},{19,21},{26,28},{27,29}} | collective-permute-start | bytes 2359304 | tf_op jit(solution)/shard_map/ppermute | solution.py:245
  402.7 37.3 %collective-permute-start.42 = (f32[64,4096]{1,0:T(8,128)}, f32[64,4096]{1,0:T(8,128)S(1)}, u32[]{:S(2)}, u32[]{:S(2)}) collective-permute-start(f32[64,4096]{1,0:T(8,128)} %get-tuple-element.187), channel_id=1, source_target_pairs={{0,16},{8,24},{16,0},{24,8},{1,17},{9,25},{17,1},{25,9},{2,18},{10... | collective-permute-start | bytes 3145736 | tf_op jit(solution)/shard_map/ppermute | solution.py:301
  415.3 34.0 %collective-permute-start.31 = (f32[8,2,32,384]{3,2,1,0:T(8,128)}, f32[8,2,32,384]{3,2,1,0:T(8,128)}, u32[]{:S(2)}, u32[]{:S(2)}) collective-permute-start(f32[8,2,32,384]{3,2,1,0:T(8,128)} %slice_add_fusion.8), channel_id=1, source_target_pairs={{2,4},{3,5},{10,12},{11,13},{18,20},{19,21},{26,28},{27,29}} | collective-permute-start | bytes 2359304 | tf_op jit(solution)/shard_map/ppermute | solution.py:245
  419.3 47.3 %collective-permute-start.23 = (f32[8,2,32,512]{3,2,1,0:T(8,128)}, f32[8,2,32,512]{3,2,1,0:T(8,128)}, u32[]{:S(2)}, u32[]{:S(2)}) collective-permute-start(f32[8,2,32,512]{3,2,1,0:T(8,128)} %slice_add_fusion.3), channel_id=1, source_target_pairs={{2,0},{3,1},{10,8},{11,9},{18,16},{19,17},{26,24},{27,25}} | collective-permute-start | bytes 3145736 | tf_op jit(solution)/shard_map/ppermute | solution.py:245
  430.7 40.4 %collective-permute-start.36 = (f32[4,2,32,1152]{3,2,1,0:T(8,128)}, f32[4,2,32,1152]{3,2,1,0:T(8,128)}, u32[]{:S(2)}, u32[]{:S(2)}) collective-permute-start(f32[4,2,32,1152]{3,2,1,0:T(8,128)} %get-tuple-element.177), channel_id=1, source_target_pairs={{6,4},{7,5},{14,12},{15,13},{22,20},{23,21},{30,28},{31,29}} | collective-permute-start | bytes 3538952 | tf_op jit(solution)/shard_map/ppermute | solution.py:245
  439.3 13.7 %collective-permute-start.24 = (f32[8,2,32,128]{3,2,1,0:T(8,128)}, f32[8,2,32,128]{3,2,1,0:T(8,128)S(1)}, u32[]{:S(2)}, u32[]{:S(2)}) collective-permute-start(f32[8,2,32,128]{3,2,1,0:T(8,128)} %slice_add_fusion.27), channel_id=1, source_target_pairs={{4,6},{5,7},{12,14},{13,15},{20,22},{21,23},{28,30},{29,31}} | collective-permute-start | bytes 786440 | tf_op jit(solution)/shard_map/ppermute | solution.py:245
  447.8 22.0 %copy-start.25 = (f32[8,2,32,384]{3,2,1,0:T(8,128)S(1)}, f32[8,2,32,384]{3,2,1,0:T(8,128)}, u32[]{:S(2)}) copy-start(f32[8,2,32,384]{3,2,1,0:T(8,128)} %copy-done.24) | copy-start | bytes 2359300
  447.8 43.8 %collective-permute-start.43 = (f32[4,2,32,1280]{3,2,1,0:T(8,128)}, f32[4,2,32,1280]{3,2,1,0:T(8,128)}, u32[]{:S(2)}, u32[]{:S(2)}) collective-permute-start(f32[4,2,32,1280]{3,2,1,0:T(8,128)} %legendre_sent.11), channel_id=1, source_target_pairs={{0,1},{1,0},{2,3},{3,2},{4,5},{5,4},{6,7},{7,6},{8,9},{9,8},{10,11... | collective-permute-start | bytes 3932168 | tf_op jit(solution)/shard_map/ppermute | solution.py:352
  449.3 39.5 %collective-permute-start.29 = (f32[8,2,32,896]{3,2,1,0:T(8,128)S(1)}, f32[8,2,32,896]{3,2,1,0:T(8,128)}, u32[]{:S(2)}, u32[]{:S(2)}) collective-permute-start(f32[8,2,32,896]{3,2,1,0:T(8,128)S(1)} %slice_add_fusion), channel_id=1, source_target_pairs={{4,2},{5,3},{12,10},{13,11},{20,18},{21,19},{28,26},{29,27}} | collective-permute-start | bytes 5505032 | tf_op jit(solution)/shard_map/ppermute | solution.py:245
  453.0 18.1 %copy-start.21 = (f32[4,2,32,1152]{3,2,1,0:T(8,128)S(1)}, f32[4,2,32,1152]{3,2,1,0:T(8,128)}, u32[]{:S(2)}) copy-start(f32[4,2,32,1152]{3,2,1,0:T(8,128)} %get-tuple-element.177) | copy-start | bytes 3538948
  453.0 27.7 %collective-permute-start.38 = (f32[4,2,32,896]{3,2,1,0:T(8,128)}, f32[4,2,32,896]{3,2,1,0:T(8,128)}, u32[]{:S(2)}, u32[]{:S(2)}) collective-permute-start(f32[4,2,32,896]{3,2,1,0:T(8,128)} %get-tuple-element.175), channel_id=1, source_target_pairs={{0,2},{1,3},{8,10},{9,11},{16,18},{17,19},{24,26},{25,27}} | collective-permute-start | bytes 2752520 | tf_op jit(solution)/shard_map/ppermute | solution.py:245
  466.6 89.0 %collective-permute-start.33 = (f32[8,2,32,128]{3,2,1,0:T(8,128)}, f32[8,2,32,128]{3,2,1,0:T(8,128)}, u32[]{:S(2)}, u32[]{:S(2)}) collective-permute-start(f32[8,2,32,128]{3,2,1,0:T(8,128)} %slice_add_fusion.26), channel_id=1, source_target_pairs={{4,6},{5,7},{12,14},{13,15},{20,22},{21,23},{28,30},{29,31}} | collective-permute-start | bytes 786440 | tf_op jit(solution)/shard_map/ppermute | solution.py:245
  473.3 11.5 %collective-permute-start.37 = (f32[4,2,32,896]{3,2,1,0:T(8,128)}, f32[4,2,32,896]{3,2,1,0:T(8,128)}, u32[]{:S(2)}, u32[]{:S(2)}) collective-permute-start(f32[4,2,32,896]{3,2,1,0:T(8,128)} %slice_add_fusion.5), channel_id=1, source_target_pairs={{4,2},{5,3},{12,10},{13,11},{20,18},{21,19},{28,26},{29,27}} | collective-permute-start | bytes 2752520 | tf_op jit(solution)/shard_map/ppermute | solution.py:245
  481.9 5.5 collective-permute-start.39
  486.1 54.9 %collective-permute-start.40 = (f32[4,2,32,512]{3,2,1,0:T(8,128)S(1)}, f32[4,2,32,512]{3,2,1,0:T(8,128)}, u32[]{:S(2)}, u32[]{:S(2)}) collective-permute-start(f32[4,2,32,512]{3,2,1,0:T(8,128)S(1)} %slice_add_fusion.13), channel_id=1, source_target_pairs={{2,0},{3,1},{10,8},{11,9},{18,16},{19,17},{26,24},{27,25}} | collective-permute-start | bytes 1572872 | tf_op jit(solution)/shard_map/ppermute | solution.py:245
  488.1 51.1 %collective-permute-start.41 = (f32[4,2,32,128]{3,2,1,0:T(8,128)}, f32[4,2,32,128]{3,2,1,0:T(8,128)S(1)}, u32[]{:S(2)}, u32[]{:S(2)}) collective-permute-start(f32[4,2,32,128]{3,2,1,0:T(8,128)} %slice_add_fusion.35), channel_id=1, source_target_pairs={{4,6},{5,7},{12,14},{13,15},{20,22},{21,23},{28,30},{29,31}} | collective-permute-start | bytes 393224 | tf_op jit(solution)/shard_map/ppermute | solution.py:245
  490.3 65.3 %collective-permute-start.32 = (f32[8,2,32,512]{3,2,1,0:T(8,128)S(1)}, f32[8,2,32,512]{3,2,1,0:T(8,128)}, u32[]{:S(2)}, u32[]{:S(2)}) collective-permute-start(f32[8,2,32,512]{3,2,1,0:T(8,128)S(1)} %slice_add_fusion.2), channel_id=1, source_target_pairs={{2,0},{3,1},{10,8},{11,9},{18,16},{19,17},{26,24},{27,25}} | collective-permute-start | bytes 3145736 | tf_op jit(solution)/shard_map/ppermute | solution.py:245
  499.2 53.0 %collective-permute-start.46 = (f32[4,2,32,896]{3,2,1,0:T(8,128)}, f32[4,2,32,896]{3,2,1,0:T(8,128)}, u32[]{:S(2)}, u32[]{:S(2)}) collective-permute-start(f32[4,2,32,896]{3,2,1,0:T(8,128)} %get-tuple-element.191), channel_id=1, source_target_pairs={{0,2},{1,3},{8,10},{9,11},{16,18},{17,19},{24,26},{25,27}} | collective-permute-start | bytes 2752520 | tf_op jit(solution)/shard_map/ppermute | solution.py:245
  539.2 16.3 %collective-permute-start.44 = (f32[4,2,32,1152]{3,2,1,0:T(8,128)}, f32[4,2,32,1152]{3,2,1,0:T(8,128)}, u32[]{:S(2)}, u32[]{:S(2)}) collective-permute-start(f32[4,2,32,1152]{3,2,1,0:T(8,128)} %get-tuple-element.193), channel_id=1, source_target_pairs={{6,4},{7,5},{14,12},{15,13},{22,20},{23,21},{30,28},{31,29}} | collective-permute-start | bytes 3538952 | tf_op jit(solution)/shard_map/ppermute | solution.py:245
  554.2 18.7 %collective-permute-start.47 = (f32[4,2,32,384]{3,2,1,0:T(8,128)}, f32[4,2,32,384]{3,2,1,0:T(8,128)}, u32[]{:S(2)}, u32[]{:S(2)}) collective-permute-start(f32[4,2,32,384]{3,2,1,0:T(8,128)} %slice_add_fusion.18), channel_id=1, source_target_pairs={{2,4},{3,5},{10,12},{11,13},{18,20},{19,21},{26,28},{27,29}} | collective-permute-start | bytes 1179656 | tf_op jit(solution)/shard_map/ppermute | solution.py:245
  558.1 10.1 %collective-permute-start.45 = (f32[4,2,32,896]{3,2,1,0:T(8,128)}, f32[4,2,32,896]{3,2,1,0:T(8,128)}, u32[]{:S(2)}, u32[]{:S(2)}) collective-permute-start(f32[4,2,32,896]{3,2,1,0:T(8,128)} %slice_add_fusion.4), channel_id=1, source_target_pairs={{4,2},{5,3},{12,10},{13,11},{20,18},{21,19},{28,26},{29,27}} | collective-permute-start | bytes 2752520 | tf_op jit(solution)/shard_map/ppermute | solution.py:245
  569.5 18.9 %collective-permute-start.48 = (f32[4,2,32,512]{3,2,1,0:T(8,128)S(1)}, f32[4,2,32,512]{3,2,1,0:T(8,128)S(1)}, u32[]{:S(2)}, u32[]{:S(2)}) collective-permute-start(f32[4,2,32,512]{3,2,1,0:T(8,128)S(1)} %slice_add_fusion.12), channel_id=1, source_target_pairs={{2,0},{3,1},{10,8},{11,9},{18,16},{19,17},{26,24},{27,25}} | collective-permute-start | bytes 1572872 | tf_op jit(solution)/shard_map/ppermute | solution.py:245
  573.8 2.0 collective-permute-start.49
  (26 other events, 81.9 us)

commit v2 on v1

--- a/solution.py
+++ b/solution.py
@@ -282,15 +282,19 @@
     keep = list(range(lon_count - 2, -1, -2))
     halves = [keep[: len(keep) // 2], keep[len(keep) // 2 :]]
 
+    steps = lon_count * lax.iota(jnp.int32, own)
+    rels = jnp.stack([lon ^ rel for rel in range(lon_count)])
+    cos, sin = table(rels[:, None] + steps, 1.0 / math.sqrt(nlon))
+
     def phases(bit, chunks):
         blocks = []
-        for rels in halves:
+        for some in halves:
             for place, count in chunks:
-                fine = lon_count * (place + lax.iota(jnp.int32, count))
-                fine = jnp.stack([lon ^ (rel | bit) for rel in rels])[:, None] + fine
-                cos, sin = table(fine, 1.0 / math.sqrt(nlon))
-                first = jnp.concatenate([cos, -sin], 1)[:, None]
-                second = jnp.concatenate([sin, cos], 1)[:, None]
+                def fine(values):
+                    return jnp.stack([values[rel | bit, place : place + count] for rel in some])
+
+                first = jnp.concatenate([fine(cos), -fine(sin)], 1)[:, None]
+                second = jnp.concatenate([fine(sin), fine(cos)], 1)[:, None]
                 both = coarse[0][:, None] * first - coarse[1][:, None] * second
                 blocks.append(both.reshape(-1, longitudes))
         both = jnp.concatenate(blocks, 0)
@@ -342,7 +346,7 @@
         return jnp.where(inside[:, None, None, None, :, :], mine, jnp.zeros((), jnp.float32))
 
     result = jnp.zeros((own, 8, levels, 2, 2, half_degrees), jnp.float32)
-    given, chains, states, kept = [None] * len(pieces), [], [], []
+    given, chains, kept = [None] * len(pieces), [], []
 
     def send(k):
         place, count, near, came = pieces[k]
@@ -351,6 +355,7 @@
         (value,) = project(plan, 1 - side, place, count, own, near, came, legendre)
         given[k] = lax.ppermute(value, "lat", [(i, i ^ 1) for i in range(lat_count)])
 
+    rounds = max(zones - 1, 1)
     for k, (place, count, near, came) in enumerate(pieces):
         if k == 0:
             send(0)
@@ -358,25 +363,33 @@
             send(k + 1)
         waits = []
         for number, chain in enumerate(chains):
-            state = next(chain, None)
-            if state is not None:
-                states[number] = state
-                waits.extend(state)
+            if k - number < rounds:
+                waits.extend(next(chain))
         near = after(near, *waits) if waits else near
         block = project(plan, side, place, count, own, near, came, legendre, given[k])
         kept.append(block)
-        chains.append(line(block, zones, zone, plan, half_degrees))
-        states.append(next(chains[-1]))
-    for k, chain in enumerate(chains):
+        chains.append(line(block, zones, plan))
+        next(chains[-1])
+    ends = []
+    for chain in chains:
+        state = None
         for state in chain:
-            states[k] = state
-        place, count = pieces[k][:2]
-        mine = finish(count, place, states[k][0])
+            pass
+        ends.append(state)
+    parts = []
+    for numbers in (range(len(ends) - 1), range(len(ends) - 1, len(ends))):
+        if len(numbers) == 0:
+            continue
+        blocks = [close(*ends[k], zone, plan, half_degrees, kept[-1]) for k in numbers]
+        place = pieces[numbers[0]][0]
+        count = sum(pieces[k][1] for k in numbers)
+        mine = finish(count, place, jnp.concatenate(blocks, 0))
         result = lax.dynamic_update_slice(result, mine, (place,) + (0,) * 5)
+        parts.append(mine)
     return result[None]
 
 
-def line(block, zones, zone, plan, half_degrees):
+def line(block, zones, plan):
     widths, places, _ = plan[:3]
     downs, ups = [block[0]], [block[1]]
     came_down, came_up = [], []
@@ -388,7 +401,15 @@
             cut = widths[zones - 2 - k]
             downs.append(downs[k][..., cut:] + came_down[k][..., cut:])
             ups.append(ups[k][..., : places[k + 1]] + came_up[k][..., : places[k + 1]])
-    downs, ups, came_down, came_up = lax.optimization_barrier((downs, ups, came_down, came_up))
+    yield downs, ups, came_down, came_up
+
+
+def close(downs, ups, came_down, came_up, zone, plan, half_degrees, last):
+    widths, places, _ = plan[:3]
+    zones = len(widths)
+    downs, ups, came_down, came_up, _ = lax.optimization_barrier(
+        (downs, ups, came_down, came_up, last)
+    )
     mine = None
     for z in range(zones):
         width = widths[z]
@@ -401,7 +422,7 @@
             value = value + came_up[z - 1][..., places[z] : places[z] + width]
         value = jnp.pad(value, ((0, 0), (0, 0), (0, 0), (0, half_degrees - width)))
         mine = value if mine is None else jnp.where(zone == z, value, mine)
-    yield (mine,)
+    return mine
 
 
 def solution(mesh):

time: 603 us -> 608 us (level)
  waiting for transfers between devices: 150 us -> 221 us
  starting transfers between devices: 131 us -> 74.5 us
    ppermute x36, starting transfers between devices: 113 us -> 56.3 us  [hop(): return lax.ppermute(value, 'lat', pairs)]
    ppermute x6, waiting for transfers between devices: 7.48 us -> 38.1 us  [send(): lax.ppermute(value, 'lat', [(i, i ^ 1) for i in range(lat_count)])]
    ppermute x36, waiting for transfers between devices: 65.9 us -> 88.2 us  [hop(): return lax.ppermute(value, 'lat', pairs)]
    ppermute x8, waiting for transfers between devices: 76.3 us -> 95.1 us  [lon_swap(): return lax.ppermute(value, 'lon', [(i, i ^ bit) for i in range(lon_count)])]
    select_n x6 -> x1, other arithmetic: 10.5 us -> 0.16 us  [close(): mine = value if mine is None else jnp.where(zone == z, value, mine)]
    dynamic_update_slice x5 -> x0, other arithmetic: 7.86 us -> none  [local(): result = lax.dynamic_update_slice(result, mine, (place,) + (0,) * 5)]
    broadcast_in_dim x0 -> x1, other arithmetic: none -> 7.41 us  [local(): return result[None]]
    unnamed x7 -> x11, other arithmetic: 2.46 us -> 9.26 us
  transfers between devices with their start and end apart: 50 -> 50, of which waited for: 11 -> 13; matrix products, arithmetic and copies ran while one was open for 16% -> 14% of each run, Pallas kernels for 26% -> 24%
where the time goes in v2:
time: 608 us; the launch traced here: 601 us
  waiting for transfers between devices  221 us (36%)
  Pallas kernels  187 us (31%)
  other arithmetic  97.3 us (16%)
  starting transfers between devices  74.5 us (12%)
  local copies, waits for them, and re-layouts  19.1 us (3%)
    pallas_call x12, Pallas kernels, project(): pl.pallas_call(kernel, grid_spec=pltpu.PrefetchScalarGridSpec(num_scalar_...  95.4 us
    ppermute x8, waiting for transfers between devices, lon_swap(): return lax.ppermute(value, 'lon', [(i, i ^ bit) for i in range(lon_count)])  95.1 us
    ppermute x36, waiting for transfers between devices, hop(): return lax.ppermute(value, 'lat', pairs)  88.2 us
    ppermute x36, starting transfers between devices, hop(): return lax.ppermute(value, 'lat', pairs)  56.3 us
    pallas_call x2, Pallas kernels, fourier(): pl.pallas_call(second_fourier_kernel, grid=(rows // block,), in_specs=[wh...  38.9 us
    ppermute x6, waiting for transfers between devices, send(): lax.ppermute(value, 'lat', [(i, i ^ 1) for i in range(lat_count)])  38.1 us
    pallas_call x2, Pallas kernels, fourier(): pl.pallas_call(first_fourier_kernel, grid=(rows // block,), in_specs=[who...  36.5 us
    add x18, other arithmetic, close(): value = value + came_up[z - 1][..., places[z]:places[z] + width]  21.5 us
  transfers between devices with their start and end apart: 50, of which 13 were waited for; matrix products, arithmetic and copies ran while one was open for 14% of the time, Pallas kernels for 24%

profile of v2, /device:TPU:0, one launch (start us, length us, event | category | flops | bytes accessed | tf_op | source)
XLA Modules:
  0.0 601.0 jit_solution(12578291770053363713)
XLA Ops:
  0.2 2.1 sine_multiply_fusion
  10.6 1.8 fusion.3
  12.4 16.4 %tendencies.1 = (bf16[8,2,256,1024]{3,2,1,0:T(8,128)(2,1)}, bf16[8,2,256,1024]{3,2,1,0:T(8,128)(2,1)}) custom-call(bf16[12,2,2,128,1024]{4,3,2,1,0:T(8,128)(2,1)} %grid_ref.1), custom_call_target="tpu_custom_call" | custom-call | flops 25165824 | bytes 31457280 | tf_op jit(solution)/shard_map/tendencies/pallas_call | solution.py:56
  28.7 18.2 %fourier_first.2 = f32[512,4096]{1,0:T(8,128)} custom-call(bf16[512,1024]{1,0:T(8,128)(2,1)} %get-tuple-element.202.ph_ref, bf16[512,1024]{1,0:T(8,128)(2,1)} %get-tuple-element.201.pl_ref, bf16[4096,1024]{1,0:T(8,128)(2,1)} %bitcast.162, bf16[4096,1024]{1,0:T(8,128)(2,1)} %bitcast.166), custom_call_target="tpu_custom_call" | custom-call | flops 12884901888 | bytes 25165824 | tf_op jit(solution)/shard_map/fourier_first/pallas_call | solution.py:111
  49.0 1.9 constant_dynamic-update-slice_fusion.1
  52.0 1.8 fusion.2
  53.7 18.4 %fourier_first.3 = f32[512,4096]{1,0:T(8,128)} custom-call(bf16[512,1024]{1,0:T(8,128)(2,1)} %get-tuple-element.204.ph_ref, bf16[512,1024]{1,0:T(8,128)(2,1)} %get-tuple-element.203.pl_ref, bf16[4096,1024]{1,0:T(8,128)(2,1)} %bitcast.163, bf16[4096,1024]{1,0:T(8,128)(2,1)} %bitcast.167), custom_call_target="tpu_custom_call" | custom-call | flops 12884901888 | bytes 25165824 | tf_op jit(solution)/shard_map/fourier_first/pallas_call | solution.py:111
  73.9 1.7 fusion.1
  75.6 19.4 %fourier_second.2 = (f32[64,4096]{1,0:T(8,128)}, f32[64,4096]{1,0:T(8,128)}, f32[128,4096]{1,0:T(8,128)}, f32[64,4096]{1,0:T(8,128)}, f32[64,4096]{1,0:T(8,128)}, /*index=5*/f32[128,4096]{1,0:T(8,128)}) custom-call(bf16[512,1024]{1,0:T(8,128)(2,1)} %get-tuple-element.206.ph_ref, bf16[512,1024]{1,0:T(8,128)(2,1)} %get-tuple-element.205.pl_ref, ...), custom_call_target="tpu_custom_call" | custom-call | flops 12884901888 | bytes 25165824 | tf_op jit(solution)/shard_map/fourier_second/pallas_call | solution.py:120
  95.0 3.0 collective-permute-start.1
  98.1 24.1 %collective-permute-done.1.refs_5_ = f32[64,4096]{1,0:T(8,128)S(1)} collective-permute-done((f32[64,4096]{1,0:T(8,128)}, f32[64,4096]{1,0:T(8,128)S(1)}, u32[]{:S(2)}, u32[]{:S(2)}) %collective-permute-start.1) | collective-permute-done | bytes 1048608 | tf_op jit(solution)/shard_map/ppermute | solution.py:305
  123.2 6.8 %legendre_sent.6 = f32[4,2,32,1280]{3,2,1,0:T(8,128)} custom-call(s32[1]{0:T(128)} %bitcast.61.refs_0_, s32[6]{0:T(128)} %constant.89.clone.refs_1_, s32[6]{0:T(128)} %constant.90.clone.refs_2_, s32[6]{0:T(128)} %constant.91.clone.refs_3_, f32[64,4096]{1,0:T(8,128)} %get-tuple-element.107.refs_4_, f32[64,4096]{1,0:T(8,128)} %copy-done.5, ...), custom_call_target="tpu_custom_call" | custom-call | flops 201326592 | bytes 3801088 | tf_op jit(solution)/shard_map/legendre_sent/pallas_call | solution.py:222
  130.0 2.0 collective-permute-start.2
  134.2 3.3 fusion.4
  137.5 51.5 %collective-permute-done.10.refs_5_ = f32[64,4096]{1,0:T(8,128)S(1)} collective-permute-done((f32[64,4096]{1,0:T(8,128)}, f32[64,4096]{1,0:T(8,128)S(1)}, u32[]{:S(2)}, u32[]{:S(2)}) %collective-permute-start.10) | collective-permute-done | bytes 1048608 | tf_op jit(solution)/shard_map/ppermute | solution.py:305
  190.0 6.7 %legendre_sent.7 = f32[4,2,32,1280]{3,2,1,0:T(8,128)} custom-call(s32[1]{0:T(128)} %bitcast.61.refs_0_, s32[6]{0:T(128)} %constant.89.clone.refs_1_, s32[6]{0:T(128)} %constant.90.clone.refs_2_, s32[6]{0:T(128)} %constant.91.clone.refs_3_, f32[64,4096]{1,0:T(8,128)} %get-tuple-element.116.refs_4_, f32[64,4096]{1,0:T(8,128)} %copy-done.3, ...), custom_call_target="tpu_custom_call" | custom-call | flops 201326592 | bytes 3801088 | tf_op jit(solution)/shard_map/legendre_sent/pallas_call | solution.py:222
  196.7 1.7 collective-permute-start.11
  198.4 7.6 %legendre_kept.6 = (f32[4,2,32,1152]{3,2,1,0:T(8,128)}, f32[4,2,32,896]{3,2,1,0:T(8,128)}) custom-call(s32[1]{0:T(128)} %bitcast.refs_0_, s32[6]{0:T(128)} %constant.89.clone.refs_1_, s32[6]{0:T(128)} %constant.90.clone.refs_2_, s32[6]{0:T(128)} %constant.91.clone.refs_3_, f32[64,4096]{1,0:T(8,128)} %get-tuple-element.107.refs_4_, f32[64,4096]{1,0:T(8,128)} %copy-done.5, ...), custom_call_target="tpu_custom_call" | custom-call | flops 201326592 | bytes 3801088 | tf_op jit(solution)/shard_map/legendre_kept/pallas_call | solution.py:222
  206.0 3.5 collective-permute-start.5
  212.6 8.7 %legendre_sent.8 = f32[8,2,32,1280]{3,2,1,0:T(8,128)} custom-call(s32[1]{0:T(128)} %bitcast.61.refs_0_, s32[6]{0:T(128)} %constant.89.clone.refs_1_, s32[6]{0:T(128)} %constant.90.clone.refs_2_, s32[6]{0:T(128)} %constant.91.clone.refs_3_, f32[128,4096]{1,0:T(8,128)} %get-tuple-element.122.refs_4_, f32[128,4096]{1,0:T(8,128)} %copy-done, ...), custom_call_target="tpu_custom_call" | custom-call | flops 402653184 | bytes 7602176 | tf_op jit(solution)/shard_map/legendre_sent/pallas_call | solution.py:222
  221.8 19.5 %fourier_second.3 = (f32[128,4096]{1,0:T(8,128)}, f32[64,4096]{1,0:T(8,128)}, f32[64,4096]{1,0:T(8,128)}, f32[128,4096]{1,0:T(8,128)}, f32[64,4096]{1,0:T(8,128)}, /*index=5*/f32[64,4096]{1,0:T(8,128)}) custom-call(bf16[512,1024]{1,0:T(8,128)(2,1)} %get-tuple-element.208.ph_ref, bf16[512,1024]{1,0:T(8,128)(2,1)} %get-tuple-element.207.pl_ref, ...), custom_call_target="tpu_custom_call" | custom-call | flops 12884901888 | bytes 25165824 | tf_op jit(solution)/shard_map/fourier_second/pallas_call | solution.py:120
  247.2 7.6 %legendre_kept.7 = (f32[4,2,32,1152]{3,2,1,0:T(8,128)}, f32[4,2,32,896]{3,2,1,0:T(8,128)}) custom-call(s32[1]{0:T(128)} %bitcast.refs_0_, s32[6]{0:T(128)} %constant.89.clone.refs_1_, s32[6]{0:T(128)} %constant.90.clone.refs_2_, s32[6]{0:T(128)} %constant.91.clone.refs_3_, f32[64,4096]{1,0:T(8,128)} %get-tuple-element.116.refs_4_, f32[64,4096]{1,0:T(8,128)} %copy-done.3, ...), custom_call_target="tpu_custom_call" | custom-call | flops 201326592 | bytes 3801088 | tf_op jit(solution)/shard_map/legendre_kept/pallas_call | solution.py:222
  254.8 3.3 collective-permute-start.14
  261.3 14.9 %collective-permute-done.14 = f32[4,2,32,896]{3,2,1,0:T(8,128)S(1)} collective-permute-done((f32[4,2,32,896]{3,2,1,0:T(8,128)}, f32[4,2,32,896]{3,2,1,0:T(8,128)S(1)}, u32[]{:S(2)}, u32[]{:S(2)}) %collective-permute-start.14) | collective-permute-done | bytes 917536 | tf_op jit(solution)/shard_map/ppermute | solution.py:245
  279.7 3.7 collective-permute-done.17.refs_7_
  283.4 10.3 %legendre_kept.8 = (f32[8,2,32,1152]{3,2,1,0:T(8,128)}, f32[8,2,32,896]{3,2,1,0:T(8,128)}) custom-call(s32[1]{0:T(128)} %bitcast.refs_0_, s32[6]{0:T(128)} %constant.89.clone.refs_1_, s32[6]{0:T(128)} %constant.90.clone.refs_2_, s32[6]{0:T(128)} %constant.91.clone.refs_3_, f32[128,4096]{1,0:T(8,128)} %get-tuple-element.122.refs_4_, f32[128,4096]{1,0:T(8,128)} %copy-done, ...), custom_call_target="tpu_custom_call" | custom-call | flops 402653184 | bytes 7602176 | tf_op jit(solution)/shard_map/legendre_kept/pallas_call | solution.py:222
  293.7 2.1 collective-permute-start.18
  297.2 8.7 %legendre_sent.9 = f32[8,2,32,1280]{3,2,1,0:T(8,128)} custom-call(s32[1]{0:T(128)} %bitcast.61.refs_0_, s32[6]{0:T(128)} %constant.89.clone.refs_1_, s32[6]{0:T(128)} %constant.90.clone.refs_2_, s32[6]{0:T(128)} %constant.91.clone.refs_3_, f32[128,4096]{1,0:T(8,128)} %get-tuple-element.127.refs_4_, f32[128,4096]{1,0:T(8,128)} %copy-done.1, ...), custom_call_target="tpu_custom_call" | custom-call | flops 402653184 | bytes 7602176 | tf_op jit(solution)/shard_map/legendre_sent/pallas_call | solution.py:222
  307.3 3.7 collective-permute-start.19
  314.2 34.4 %collective-permute-done.19 = f32[8,2,32,896]{3,2,1,0:T(8,128)S(1)} collective-permute-done((f32[8,2,32,896]{3,2,1,0:T(8,128)}, f32[8,2,32,896]{3,2,1,0:T(8,128)S(1)}, u32[]{:S(2)}, u32[]{:S(2)}) %collective-permute-start.19) | collective-permute-done | bytes 1835040 | tf_op jit(solution)/shard_map/ppermute | solution.py:245
  348.7 2.7 slice_add_fusion.9
  351.4 1.8 slice_add_fusion.1
  353.2 10.4 %collective-permute-done.21.refs_7_ = f32[8,2,32,1280]{3,2,1,0:T(8,128)} collective-permute-done((f32[8,2,32,1280]{3,2,1,0:T(8,128)}, f32[8,2,32,1280]{3,2,1,0:T(8,128)}, u32[]{:S(2)}, u32[]{:S(2)}) %collective-permute-start.21) | collective-permute-done | bytes 2621472 | tf_op jit(solution)/shard_map/ppermute | solution.py:356
  363.5 10.3 %legendre_kept.9 = (f32[8,2,32,1152]{3,2,1,0:T(8,128)}, f32[8,2,32,896]{3,2,1,0:T(8,128)}) custom-call(s32[1]{0:T(128)} %bitcast.refs_0_, s32[6]{0:T(128)} %constant.89.clone.refs_1_, s32[6]{0:T(128)} %constant.90.clone.refs_2_, s32[6]{0:T(128)} %constant.91.clone.refs_3_, f32[128,4096]{1,0:T(8,128)} %get-tuple-element.127.refs_4_, f32[128,4096]{1,0:T(8,128)} %copy-done.1, ...), custom_call_target="tpu_custom_call" | custom-call | flops 402653184 | bytes 7602176 | tf_op jit(solution)/shard_map/legendre_kept/pallas_call | solution.py:222
  373.9 4.5 collective-permute-start.24
  378.4 2.0 collective-permute-start.22
  380.4 1.9 collective-permute-start.26
  385.4 19.4 %collective-permute-done.28.refs_5_ = f32[64,4096]{1,0:T(8,128)S(1)} collective-permute-done((f32[64,4096]{1,0:T(8,128)}, f32[64,4096]{1,0:T(8,128)S(1)}, u32[]{:S(2)}, u32[]{:S(2)}) %collective-permute-start.28) | collective-permute-done | bytes 1048608 | tf_op jit(solution)/shard_map/ppermute | solution.py:305
  405.8 6.7 %legendre_sent.10 = f32[4,2,32,1280]{3,2,1,0:T(8,128)} custom-call(s32[1]{0:T(128)} %bitcast.61.refs_0_, s32[6]{0:T(128)} %constant.89.clone.refs_1_, s32[6]{0:T(128)} %constant.90.clone.refs_2_, s32[6]{0:T(128)} %constant.91.clone.refs_3_, f32[64,4096]{1,0:T(8,128)} %get-tuple-element.133.refs_4_, f32[64,4096]{1,0:T(8,128)} %copy-done.4, ...), custom_call_target="tpu_custom_call" | custom-call | flops 201326592 | bytes 3801088 | tf_op jit(solution)/shard_map/legendre_sent/pallas_call | solution.py:222
  415.5 1.8 slice_add_fusion.26
  417.3 2.4 slice_add_fusion.8
  419.7 2.5 slice_add_fusion.2
  422.2 3.0 slice_add_fusion
  425.2 1.9 collective-permute-start.23
  427.1 12.8 %collective-permute-done.29.refs_7_ = f32[4,2,32,1280]{3,2,1,0:T(8,128)} collective-permute-done((f32[4,2,32,1280]{3,2,1,0:T(8,128)}, f32[4,2,32,1280]{3,2,1,0:T(8,128)}, u32[]{:S(2)}, u32[]{:S(2)}) %collective-permute-start.29) | collective-permute-done | bytes 1310752 | tf_op jit(solution)/shard_map/ppermute | solution.py:356
  439.9 7.6 %legendre_kept.10 = (f32[4,2,32,1152]{3,2,1,0:T(8,128)}, f32[4,2,32,896]{3,2,1,0:T(8,128)}) custom-call(s32[1]{0:T(128)} %bitcast.refs_0_, s32[6]{0:T(128)} %constant.89.clone.refs_1_, s32[6]{0:T(128)} %constant.90.clone.refs_2_, s32[6]{0:T(128)} %constant.91.clone.refs_3_, f32[64,4096]{1,0:T(8,128)} %get-tuple-element.133.refs_4_, f32[64,4096]{1,0:T(8,128)} %copy-done.4, ...), custom_call_target="tpu_custom_call" | custom-call | flops 201326592 | bytes 3801088 | tf_op jit(solution)/shard_map/legendre_kept/pallas_call | solution.py:222
  447.5 2.3 collective-permute-start.31
  454.8 6.7 %legendre_sent.11 = f32[4,2,32,1280]{3,2,1,0:T(8,128)} custom-call(s32[1]{0:T(128)} %bitcast.61.refs_0_, s32[6]{0:T(128)} %constant.89.clone.refs_1_, s32[6]{0:T(128)} %constant.90.clone.refs_2_, s32[6]{0:T(128)} %constant.91.clone.refs_3_, f32[64,4096]{1,0:T(8,128)} %get-tuple-element.138.refs_4_, f32[64,4096]{1,0:T(8,128)} %copy-done.2, ...), custom_call_target="tpu_custom_call" | custom-call | flops 201326592 | bytes 3801088 | tf_op jit(solution)/shard_map/legendre_sent/pallas_call | solution.py:222
  461.5 3.1 collective-permute-done.31
  467.9 1.8 slice_add_fusion.27
  471.0 2.2 slice_add_fusion.5
  476.5 2.8 slice_add_fusion.3
  479.3 11.3 %collective-permute-done.33.refs_7_ = f32[4,2,32,1280]{3,2,1,0:T(8,128)} collective-permute-done((f32[4,2,32,1280]{3,2,1,0:T(8,128)}, f32[4,2,32,1280]{3,2,1,0:T(8,128)}, u32[]{:S(2)}, u32[]{:S(2)}) %collective-permute-start.33) | collective-permute-done | bytes 1310752 | tf_op jit(solution)/shard_map/ppermute | solution.py:356
  491.9 7.6 %legendre_kept.11 = (f32[4,2,32,1152]{3,2,1,0:T(8,128)}, f32[4,2,32,896]{3,2,1,0:T(8,128)}) custom-call(s32[1]{0:T(128)} %bitcast.refs_0_, s32[6]{0:T(128)} %constant.89.clone.refs_1_, s32[6]{0:T(128)} %constant.90.clone.refs_2_, s32[6]{0:T(128)} %constant.91.clone.refs_3_, f32[64,4096]{1,0:T(8,128)} %get-tuple-element.138.refs_4_, f32[64,4096]{1,0:T(8,128)} %copy-done.2, ...), custom_call_target="tpu_custom_call" | custom-call | flops 201326592 | bytes 3801088 | tf_op jit(solution)/shard_map/legendre_kept/pallas_call | solution.py:222
  506.7 2.0 select_dynamic-update-slice_fusion.4
  513.6 14.1 %collective-permute-done.36 = f32[8,2,32,512]{3,2,1,0:T(8,128)S(1)} collective-permute-done((f32[8,2,32,512]{3,2,1,0:T(8,128)S(1)}, f32[8,2,32,512]{3,2,1,0:T(8,128)S(1)}, u32[]{:S(2)}, u32[]{:S(2)}) %collective-permute-start.36) | collective-permute-done | bytes 1048608 | tf_op jit(solution)/shard_map/ppermute | solution.py:245
  529.2 2.2 select_dynamic-update-slice_fusion.3
  538.9 15.7 %collective-permute-done.42 = f32[4,2,32,512]{3,2,1,0:T(8,128)S(1)} collective-permute-done((f32[4,2,32,512]{3,2,1,0:T(8,128)S(1)}, f32[4,2,32,512]{3,2,1,0:T(8,128)S(1)}, u32[]{:S(2)}, u32[]{:S(2)}) %collective-permute-start.42) | collective-permute-done | bytes 524320 | tf_op jit(solution)/shard_map/ppermute | solution.py:245
  560.0 1.8 slice_add_fusion.10
  561.9 1.8 collective-permute-start.45
  567.0 5.4 reshape.621
  575.6 7.8 %fusion = f32[28,8,2,2,2,512]{5,4,3,2,1,0:T(2,128)} fusion(f32[28,2,2,8,2,512]{5,4,3,2,1,0:T(2,128)} %reshape.621, pred[28,2,512]{2,1,0:T(4,128)(4,1)S(1)} %add_compare_fusion), kind=kLoop, calls=%fused_computation.2 | loop fusion | flops 917504 | bytes 7368704 | tf_op jit(solution)/shard_map/jit(_where)/select_n | solution.py:346
  583.4 5.9 collective-permute-done.48
  593.3 7.4 %maximum_bitcast_fusion = f32[1,32,8,2,2,2,512]{6,5,4,3,2,1,0:T(2,128)} fusion(f32[4,8,2,2,2,512]{5,4,3,2,1,0:T(2,128)S(1)} %fusion.8, f32[28,8,2,2,2,512]{5,4,3,2,1,0:T(2,128)} %fusion), kind=kLoop, calls=%fused_computation | loop fusion | flops 1048576 | bytes 8388608 | tf_op jit(solution)/shard_map/broadcast_in_dim | solution.py:389
  (270 shorter events, 97.2 us)
Async XLA Ops:
  46.9 28.7 %collective-permute-start = (f32[512,4096]{1,0:T(8,128)}, f32[512,4096]{1,0:T(8,128)}, u32[]{:S(2)}, u32[]{:S(2)}) collective-permute-start(f32[512,4096]{1,0:T(8,128)} %fourier_first.2), channel_id=1, source_target_pairs={{0,8},{8,0},{16,24},{24,16},{1,9},{9,1},{17,25},{25,17},{2,10},{10... | collective-permute-start | bytes 25165832 | tf_op jit(solution)/shard_map/ppermute | solution.py:305
  53.7 19.3 %copy-start.12 = (f32[512,1024]{1,0:T(8,128)S(1)}, f32[512,1024]{1,0:T(8,128)}, u32[]{:S(2)}) copy-start(f32[512,1024]{1,0:T(8,128)} %get-tuple-element.296) | copy-start | bytes 6291460
  72.1 149.7 %collective-permute-start.9 = (f32[512,4096]{1,0:T(8,128)}, f32[512,4096]{1,0:T(8,128)}, u32[]{:S(2)}, u32[]{:S(2)}) collective-permute-start(f32[512,4096]{1,0:T(8,128)} %fourier_first.3), channel_id=1, source_target_pairs={{0,8},{8,0},{16,24},{24,16},{1,9},{9,1},{17,25},{25,17},{2,10},{10... | collective-permute-start | bytes 25165832 | tf_op jit(solution)/shard_map/ppermute | solution.py:305
  95.0 27.2 %collective-permute-start.1 = (f32[64,4096]{1,0:T(8,128)}, f32[64,4096]{1,0:T(8,128)S(1)}, u32[]{:S(2)}, u32[]{:S(2)}) collective-permute-start(f32[64,4096]{1,0:T(8,128)} %get-tuple-element.108), channel_id=1, source_target_pairs={{0,16},{8,24},{16,0},{24,8},{1,17},{9,25},{17,1},{25,9},{2,18},{10... | collective-permute-start | bytes 3145736 | tf_op jit(solution)/shard_map/ppermute | solution.py:305
  98.0 113.2 %collective-permute-start.16 = (f32[128,4096]{1,0:T(8,128)}, f32[128,4096]{1,0:T(8,128)S(1)}, u32[]{:S(2)}, u32[]{:S(2)}) collective-permute-start(f32[128,4096]{1,0:T(8,128)} %get-tuple-element.121), channel_id=1, source_target_pairs={{0,16},{8,24},{16,0},{24,8},{1,17},{9,25},{17,1},{25,9},{2,18},{10... | collective-permute-start | bytes 6291464 | tf_op jit(solution)/shard_map/ppermute | solution.py:305
  130.0 68.5 %collective-permute-start.2 = (f32[4,2,32,1280]{3,2,1,0:T(8,128)}, f32[4,2,32,1280]{3,2,1,0:T(8,128)}, u32[]{:S(2)}, u32[]{:S(2)}) collective-permute-start(f32[4,2,32,1280]{3,2,1,0:T(8,128)} %legendre_sent.6), channel_id=1, source_target_pairs={{0,1},{1,0},{2,3},{3,2},{4,5},{5,4},{6,7},{7,6},{8,9},{9,8},{10,11... | collective-permute-start | bytes 3932168 | tf_op jit(solution)/shard_map/ppermute | solution.py:356
  131.9 57.1 %collective-permute-start.10 = (f32[64,4096]{1,0:T(8,128)}, f32[64,4096]{1,0:T(8,128)S(1)}, u32[]{:S(2)}, u32[]{:S(2)}) collective-permute-start(f32[64,4096]{1,0:T(8,128)} %get-tuple-element.117), channel_id=1, source_target_pairs={{0,16},{8,24},{16,0},{24,8},{1,17},{9,25},{17,1},{25,9},{2,18},{10... | collective-permute-start | bytes 3145736 | tf_op jit(solution)/shard_map/ppermute | solution.py:305
  196.7 50.5 %collective-permute-start.11 = (f32[4,2,32,1280]{3,2,1,0:T(8,128)}, f32[4,2,32,1280]{3,2,1,0:T(8,128)}, u32[]{:S(2)}, u32[]{:S(2)}) collective-permute-start(f32[4,2,32,1280]{3,2,1,0:T(8,128)} %legendre_sent.7), channel_id=1, source_target_pairs={{0,1},{1,0},{2,3},{3,2},{4,5},{5,4},{6,7},{7,6},{8,9},{9,8},{10,11... | collective-permute-start | bytes 3932168 | tf_op jit(solution)/shard_map/ppermute | solution.py:356
  206.0 36.8 %collective-permute-start.5 = (f32[4,2,32,896]{3,2,1,0:T(8,128)}, f32[4,2,32,896]{3,2,1,0:T(8,128)S(1)}, u32[]{:S(2)}, u32[]{:S(2)}) collective-permute-start(f32[4,2,32,896]{3,2,1,0:T(8,128)} %get-tuple-element.141), channel_id=1, source_target_pairs={{0,2},{1,3},{8,10},{9,11},{16,18},{17,19},{24,26},{25,27}} | collective-permute-start | bytes 2752520 | tf_op jit(solution)/shard_map/ppermute | solution.py:245
  209.6 36.0 %collective-permute-start.3 = (f32[4,2,32,1152]{3,2,1,0:T(8,128)}, f32[4,2,32,1152]{3,2,1,0:T(8,128)}, u32[]{:S(2)}, u32[]{:S(2)}) collective-permute-start(f32[4,2,32,1152]{3,2,1,0:T(8,128)} %get-tuple-element.143), channel_id=1, source_target_pairs={{6,4},{7,5},{14,12},{15,13},{22,20},{23,21},{30,28},{31,29}} | collective-permute-start | bytes 3538952 | tf_op jit(solution)/shard_map/ppermute | solution.py:245
  221.2 62.1 %collective-permute-start.17 = (f32[8,2,32,1280]{3,2,1,0:T(8,128)}, f32[8,2,32,1280]{3,2,1,0:T(8,128)}, u32[]{:S(2)}, u32[]{:S(2)}) collective-permute-start(f32[8,2,32,1280]{3,2,1,0:T(8,128)} %legendre_sent.8), channel_id=1, source_target_pairs={{0,1},{1,0},{2,3},{3,2},{4,5},{5,4},{6,7},{7,6},{8,9},{9,8},{10,11... | collective-permute-start | bytes 7864328 | tf_op jit(solution)/shard_map/ppermute | solution.py:356
  241.3 54.4 %collective-permute-start.20 = (f32[128,4096]{1,0:T(8,128)}, f32[128,4096]{1,0:T(8,128)S(1)}, u32[]{:S(2)}, u32[]{:S(2)}) collective-permute-start(f32[128,4096]{1,0:T(8,128)} %get-tuple-element.126), channel_id=1, source_target_pairs={{0,16},{8,24},{16,0},{24,8},{1,17},{9,25},{17,1},{25,9},{2,18},{10... | collective-permute-start | bytes 6291464 | tf_op jit(solution)/shard_map/ppermute | solution.py:305
  244.2 14.6 %collective-permute-start.6 = (f32[4,2,32,384]{3,2,1,0:T(8,128)S(1)}, f32[4,2,32,384]{3,2,1,0:T(8,128)}, u32[]{:S(2)}, u32[]{:S(2)}) collective-permute-start(f32[4,2,32,384]{3,2,1,0:T(8,128)S(1)} %slice_add_fusion.21), channel_id=1, source_target_pairs={{2,4},{3,5},{10,12},{11,13},{18,20},{19,21},{26,28},{27,29}} | collective-permute-start | bytes 1179656 | tf_op jit(solution)/shard_map/ppermute | solution.py:245
  247.2 30.4 %copy-start.8 = (f32[4,2,32,896]{3,2,1,0:T(8,128)}, f32[4,2,32,896]{3,2,1,0:T(8,128)S(1)}, u32[]{:S(2)}) copy-start(f32[4,2,32,896]{3,2,1,0:T(8,128)S(1)} %slice_add_fusion.7) | copy-start | bytes 2752516
  254.8 23.9 %copy-start.18 = (f32[4,2,32,1152]{3,2,1,0:T(8,128)S(1)}, f32[4,2,32,1152]{3,2,1,0:T(8,128)}, u32[]{:S(2)}) copy-start(f32[4,2,32,1152]{3,2,1,0:T(8,128)} %get-tuple-element.153) | copy-start | bytes 3538948
  254.8 21.4 %collective-permute-start.14 = (f32[4,2,32,896]{3,2,1,0:T(8,128)}, f32[4,2,32,896]{3,2,1,0:T(8,128)S(1)}, u32[]{:S(2)}, u32[]{:S(2)}) collective-permute-start(f32[4,2,32,896]{3,2,1,0:T(8,128)} %get-tuple-element.151), channel_id=1, source_target_pairs={{0,2},{1,3},{8,10},{9,11},{16,18},{17,19},{24,26},{25,27}} | collective-permute-start | bytes 2752520 | tf_op jit(solution)/shard_map/ppermute | solution.py:245
  258.1 19.4 %collective-permute-start.4 = (f32[4,2,32,896]{3,2,1,0:T(8,128)S(1)}, f32[4,2,32,896]{3,2,1,0:T(8,128)S(1)}, u32[]{:S(2)}, u32[]{:S(2)}) collective-permute-start(f32[4,2,32,896]{3,2,1,0:T(8,128)S(1)} %slice_add_fusion.7), channel_id=1, source_target_pairs={{4,2},{5,3},{12,10},{13,11},{20,18},{21,19},{28,26},{29,27}} | collective-permute-start | bytes 2752520 | tf_op jit(solution)/shard_map/ppermute | solution.py:245
  258.8 19.8 %collective-permute-start.12 = (f32[4,2,32,1152]{3,2,1,0:T(8,128)}, f32[4,2,32,1152]{3,2,1,0:T(8,128)S(1)}, u32[]{:S(2)}, u32[]{:S(2)}) collective-permute-start(f32[4,2,32,1152]{3,2,1,0:T(8,128)} %get-tuple-element.153), channel_id=1, source_target_pairs={{6,4},{7,5},{14,12},{15,13},{22,20},{23,21},{30,28},{31,29}} | collective-permute-start | bytes 3538952 | tf_op jit(solution)/shard_map/ppermute | solution.py:245
  279.7 33.5 %copy-start.9 = (f32[4,2,32,896]{3,2,1,0:T(8,128)}, f32[4,2,32,896]{3,2,1,0:T(8,128)S(1)}, u32[]{:S(2)}) copy-start(f32[4,2,32,896]{3,2,1,0:T(8,128)S(1)} %slice_add_fusion.6) | copy-start | bytes 2752516
  293.7 57.7 %collective-permute-start.18 = (f32[8,2,32,1152]{3,2,1,0:T(8,128)}, f32[8,2,32,1152]{3,2,1,0:T(8,128)}, u32[]{:S(2)}, u32[]{:S(2)}) collective-permute-start(f32[8,2,32,1152]{3,2,1,0:T(8,128)} %get-tuple-element.163), channel_id=1, source_target_pairs={{6,4},{7,5},{14,12},{15,13},{22,20},{23,21},{30,28},{31,29}} | collective-permute-start | bytes 7077896 | tf_op jit(solution)/shard_map/ppermute | solution.py:245
  305.8 57.7 %collective-permute-start.21 = (f32[8,2,32,1280]{3,2,1,0:T(8,128)}, f32[8,2,32,1280]{3,2,1,0:T(8,128)}, u32[]{:S(2)}, u32[]{:S(2)}) collective-permute-start(f32[8,2,32,1280]{3,2,1,0:T(8,128)} %legendre_sent.9), channel_id=1, source_target_pairs={{0,1},{1,0},{2,3},{3,2},{4,5},{5,4},{6,7},{7,6},{8,9},{9,8},{10,11... | collective-permute-start | bytes 7864328 | tf_op jit(solution)/shard_map/ppermute | solution.py:356
  307.3 44.1 %copy-start.14 = (f32[8,2,32,1152]{3,2,1,0:T(8,128)S(1)}, f32[8,2,32,1152]{3,2,1,0:T(8,128)}, u32[]{:S(2)}) copy-start(f32[8,2,32,1152]{3,2,1,0:T(8,128)} %get-tuple-element.163) | copy-start | bytes 7077892
  307.3 41.4 %collective-permute-start.19 = (f32[8,2,32,896]{3,2,1,0:T(8,128)}, f32[8,2,32,896]{3,2,1,0:T(8,128)S(1)}, u32[]{:S(2)}, u32[]{:S(2)}) collective-permute-start(f32[8,2,32,896]{3,2,1,0:T(8,128)} %get-tuple-element.161), channel_id=1, source_target_pairs={{0,2},{1,3},{8,10},{9,11},{16,18},{17,19},{24,26},{25,27}} | collective-permute-start | bytes 5505032 | tf_op jit(solution)/shard_map/ppermute | solution.py:245
  311.0 2.2 collective-permute-start.13
  311.7 0.7 collective-permute-start.15
  373.9 43.5 %collective-permute-start.24 = (f32[8,2,32,896]{3,2,1,0:T(8,128)}, f32[8,2,32,896]{3,2,1,0:T(8,128)}, u32[]{:S(2)}, u32[]{:S(2)}) collective-permute-start(f32[8,2,32,896]{3,2,1,0:T(8,128)} %get-tuple-element.171), channel_id=1, source_target_pairs={{0,2},{1,3},{8,10},{9,11},{16,18},{17,19},{24,26},{25,27}} | collective-permute-start | bytes 5505032 | tf_op jit(solution)/shard_map/ppermute | solution.py:245
  378.4 43.8 %collective-permute-start.22 = (f32[8,2,32,1152]{3,2,1,0:T(8,128)}, f32[8,2,32,1152]{3,2,1,0:T(8,128)}, u32[]{:S(2)}, u32[]{:S(2)}) collective-permute-start(f32[8,2,32,1152]{3,2,1,0:T(8,128)} %get-tuple-element.173), channel_id=1, source_target_pairs={{6,4},{7,5},{14,12},{15,13},{22,20},{23,21},{30,28},{31,29}} | collective-permute-start | bytes 7077896 | tf_op jit(solution)/shard_map/ppermute | solution.py:245
  380.4 39.3 %collective-permute-start.26 = (f32[8,2,32,896]{3,2,1,0:T(8,128)S(1)}, f32[8,2,32,896]{3,2,1,0:T(8,128)}, u32[]{:S(2)}, u32[]{:S(2)}) collective-permute-start(f32[8,2,32,896]{3,2,1,0:T(8,128)S(1)} %slice_add_fusion.1), channel_id=1, source_target_pairs={{4,2},{5,3},{12,10},{13,11},{20,18},{21,19},{28,26},{29,27}} | collective-permute-start | bytes 5505032 | tf_op jit(solution)/shard_map/ppermute | solution.py:245
  382.3 22.5 %collective-permute-start.28 = (f32[64,4096]{1,0:T(8,128)}, f32[64,4096]{1,0:T(8,128)S(1)}, u32[]{:S(2)}, u32[]{:S(2)}) collective-permute-start(f32[64,4096]{1,0:T(8,128)} %get-tuple-element.132), channel_id=1, source_target_pairs={{0,16},{8,24},{16,0},{24,8},{1,17},{9,25},{17,1},{25,9},{2,18},{10... | collective-permute-start | bytes 3145736 | tf_op jit(solution)/shard_map/ppermute | solution.py:305
  383.9 30.1 %collective-permute-start.27 = (f32[8,2,32,384]{3,2,1,0:T(8,128)}, f32[8,2,32,384]{3,2,1,0:T(8,128)}, u32[]{:S(2)}, u32[]{:S(2)}) collective-permute-start(f32[8,2,32,384]{3,2,1,0:T(8,128)} %slice_add_fusion.9), channel_id=1, source_target_pairs={{2,4},{3,5},{10,12},{11,13},{18,20},{19,21},{26,28},{27,29}} | collective-permute-start | bytes 2359304 | tf_op jit(solution)/shard_map/ppermute | solution.py:245
  412.5 27.4 %collective-permute-start.29 = (f32[4,2,32,1280]{3,2,1,0:T(8,128)}, f32[4,2,32,1280]{3,2,1,0:T(8,128)}, u32[]{:S(2)}, u32[]{:S(2)}) collective-permute-start(f32[4,2,32,1280]{3,2,1,0:T(8,128)} %legendre_sent.10), channel_id=1, source_target_pairs={{0,1},{1,0},{2,3},{3,2},{4,5},{5,4},{6,7},{7,6},{8,9},{9,8},{10,11... | collective-permute-start | bytes 3932168 | tf_op jit(solution)/shard_map/ppermute | solution.py:356
  414.0 39.3 %collective-permute-start.32 = (f32[64,4096]{1,0:T(8,128)}, f32[64,4096]{1,0:T(8,128)S(1)}, u32[]{:S(2)}, u32[]{:S(2)}) collective-permute-start(f32[64,4096]{1,0:T(8,128)} %get-tuple-element.137), channel_id=1, source_target_pairs={{0,16},{8,24},{16,0},{24,8},{1,17},{9,25},{17,1},{25,9},{2,18},{10... | collective-permute-start | bytes 3145736 | tf_op jit(solution)/shard_map/ppermute | solution.py:305
  425.2 50.0 %collective-permute-start.23 = (f32[8,2,32,896]{3,2,1,0:T(8,128)}, f32[8,2,32,896]{3,2,1,0:T(8,128)}, u32[]{:S(2)}, u32[]{:S(2)}) collective-permute-start(f32[8,2,32,896]{3,2,1,0:T(8,128)} %slice_add_fusion), channel_id=1, source_target_pairs={{4,2},{5,3},{12,10},{13,11},{20,18},{21,19},{28,26},{29,27}} | collective-permute-start | bytes 5505032 | tf_op jit(solution)/shard_map/ppermute | solution.py:245
  447.5 17.1 %collective-permute-start.31 = (f32[4,2,32,896]{3,2,1,0:T(8,128)}, f32[4,2,32,896]{3,2,1,0:T(8,128)}, u32[]{:S(2)}, u32[]{:S(2)}) collective-permute-start(f32[4,2,32,896]{3,2,1,0:T(8,128)} %get-tuple-element.181), channel_id=1, source_target_pairs={{0,2},{1,3},{8,10},{9,11},{16,18},{17,19},{24,26},{25,27}} | collective-permute-start | bytes 2752520 | tf_op jit(solution)/shard_map/ppermute | solution.py:245
  449.8 19.9 %collective-permute-start.30 = (f32[4,2,32,1152]{3,2,1,0:T(8,128)}, f32[4,2,32,1152]{3,2,1,0:T(8,128)}, u32[]{:S(2)}, u32[]{:S(2)}) collective-permute-start(f32[4,2,32,1152]{3,2,1,0:T(8,128)} %get-tuple-element.183), channel_id=1, source_target_pairs={{6,4},{7,5},{14,12},{15,13},{22,20},{23,21},{30,28},{31,29}} | collective-permute-start | bytes 3538952 | tf_op jit(solution)/shard_map/ppermute | solution.py:245
  451.5 15.8 %collective-permute-start.25 = (f32[8,2,32,384]{3,2,1,0:T(8,128)}, f32[8,2,32,384]{3,2,1,0:T(8,128)}, u32[]{:S(2)}, u32[]{:S(2)}) collective-permute-start(f32[8,2,32,384]{3,2,1,0:T(8,128)} %slice_add_fusion.8), channel_id=1, source_target_pairs={{2,4},{3,5},{10,12},{11,13},{18,20},{19,21},{26,28},{27,29}} | collective-permute-start | bytes 2359304 | tf_op jit(solution)/shard_map/ppermute | solution.py:245
  453.3 16.4 %copy-start.15 = (f32[4,2,32,512]{3,2,1,0:T(8,128)S(1)}, f32[4,2,32,512]{3,2,1,0:T(8,128)}, u32[]{:S(2)}) copy-start(f32[4,2,32,512]{3,2,1,0:T(8,128)} %slice_add_fusion.15) | copy-start | bytes 1572868
  453.3 46.3 %collective-permute-start.8 = (f32[4,2,32,128]{3,2,1,0:T(8,128)}, f32[4,2,32,128]{3,2,1,0:T(8,128)}, u32[]{:S(2)}, u32[]{:S(2)}) collective-permute-start(f32[4,2,32,128]{3,2,1,0:T(8,128)} %slice_add_fusion.37), channel_id=1, source_target_pairs={{4,6},{5,7},{12,14},{13,15},{20,22},{21,23},{28,30},{29,31}} | collective-permute-start | bytes 393224 | tf_op jit(solution)/shard_map/ppermute | solution.py:245
  461.5 9.5 %copy-start.20 = (f32[4,2,32,1152]{3,2,1,0:T(8,128)S(1)}, f32[4,2,32,1152]{3,2,1,0:T(8,128)}, u32[]{:S(2)}) copy-start(f32[4,2,32,1152]{3,2,1,0:T(8,128)} %get-tuple-element.183) | copy-start | bytes 3538948
  464.7 25.9 %collective-permute-start.33 = (f32[4,2,32,1280]{3,2,1,0:T(8,128)}, f32[4,2,32,1280]{3,2,1,0:T(8,128)}, u32[]{:S(2)}, u32[]{:S(2)}) collective-permute-start(f32[4,2,32,1280]{3,2,1,0:T(8,128)} %legendre_sent.11), channel_id=1, source_target_pairs={{0,1},{1,0},{2,3},{3,2},{4,5},{5,4},{6,7},{7,6},{8,9},{9,8},{10,11... | collective-permute-start | bytes 3932168 | tf_op jit(solution)/shard_map/ppermute | solution.py:356
  467.2 6.0 collective-permute-start.41
  469.7 31.4 %collective-permute-start.7 = (f32[4,2,32,512]{3,2,1,0:T(8,128)S(1)}, f32[4,2,32,512]{3,2,1,0:T(8,128)}, u32[]{:S(2)}, u32[]{:S(2)}) collective-permute-start(f32[4,2,32,512]{3,2,1,0:T(8,128)S(1)} %copy-done.15), channel_id=1, source_target_pairs={{2,0},{3,1},{10,8},{11,9},{18,16},{19,17},{26,24},{27,25}} | collective-permute-start | bytes 1572872 | tf_op jit(solution)/shard_map/ppermute | solution.py:245
  473.2 32.1 %collective-permute-start.35 = (f32[4,2,32,128]{3,2,1,0:T(8,128)}, f32[4,2,32,128]{3,2,1,0:T(8,128)}, u32[]{:S(2)}, u32[]{:S(2)}) collective-permute-start(f32[4,2,32,128]{3,2,1,0:T(8,128)} %slice_add_fusion.36), channel_id=1, source_target_pairs={{4,6},{5,7},{12,14},{13,15},{20,22},{21,23},{28,30},{29,31}} | collective-permute-start | bytes 393224 | tf_op jit(solution)/shard_map/ppermute | solution.py:245
  475.2 30.8 %collective-permute-start.34 = (f32[4,2,32,512]{3,2,1,0:T(8,128)}, f32[4,2,32,512]{3,2,1,0:T(8,128)}, u32[]{:S(2)}, u32[]{:S(2)}) collective-permute-start(f32[4,2,32,512]{3,2,1,0:T(8,128)} %slice_add_fusion.14), channel_id=1, source_target_pairs={{2,0},{3,1},{10,8},{11,9},{18,16},{19,17},{26,24},{27,25}} | collective-permute-start | bytes 1572872 | tf_op jit(solution)/shard_map/ppermute | solution.py:245
  479.3 20.3 %copy-start.6 = (f32[8,2,32,512]{3,2,1,0:T(8,128)S(1)}, f32[8,2,32,512]{3,2,1,0:T(8,128)}, u32[]{:S(2)}) copy-start(f32[8,2,32,512]{3,2,1,0:T(8,128)} %slice_add_fusion.2) | copy-start | bytes 3145732
  490.6 21.7 %collective-permute-start.37 = (f32[8,2,32,128]{3,2,1,0:T(8,128)}, f32[8,2,32,128]{3,2,1,0:T(8,128)}, u32[]{:S(2)}, u32[]{:S(2)}) collective-permute-start(f32[8,2,32,128]{3,2,1,0:T(8,128)} %slice_add_fusion.26), channel_id=1, source_target_pairs={{4,6},{5,7},{12,14},{13,15},{20,22},{21,23},{28,30},{29,31}} | collective-permute-start | bytes 786440 | tf_op jit(solution)/shard_map/ppermute | solution.py:245
  499.6 5.7 copy-start.10
  499.6 6.4 %copy-start.32 = (f32[4,2,32,128]{3,2,1,0:T(8,128)S(1)}, f32[4,2,32,128]{3,2,1,0:T(8,128)}, u32[]{:S(2)}) copy-start(f32[4,2,32,128]{3,2,1,0:T(8,128)} %slice_add_fusion.35) | copy-start | bytes 393220
  499.6 28.1 %collective-permute-start.36 = (f32[8,2,32,512]{3,2,1,0:T(8,128)S(1)}, f32[8,2,32,512]{3,2,1,0:T(8,128)S(1)}, u32[]{:S(2)}, u32[]{:S(2)}) collective-permute-start(f32[8,2,32,512]{3,2,1,0:T(8,128)S(1)} %copy-done.6), channel_id=1, source_target_pairs={{2,0},{3,1},{10,8},{11,9},{18,16},{19,17},{26,24},{27,25}} | collective-permute-start | bytes 3145736 | tf_op jit(solution)/shard_map/ppermute | solution.py:245
  501.1 57.4 %collective-permute-start.39 = (f32[8,2,32,128]{3,2,1,0:T(8,128)}, f32[8,2,32,128]{3,2,1,0:T(8,128)S(1)}, u32[]{:S(2)}, u32[]{:S(2)}) collective-permute-start(f32[8,2,32,128]{3,2,1,0:T(8,128)} %slice_add_fusion.27), channel_id=1, source_target_pairs={{4,6},{5,7},{12,14},{13,15},{20,22},{21,23},{28,30},{29,31}} | collective-permute-start | bytes 786440 | tf_op jit(solution)/shard_map/ppermute | solution.py:245
  504.2 5.9 copy-start.28
  505.3 29.1 %collective-permute-start.40 = (f32[4,2,32,896]{3,2,1,0:T(8,128)S(1)}, f32[4,2,32,896]{3,2,1,0:T(8,128)S(1)}, u32[]{:S(2)}, u32[]{:S(2)}) collective-permute-start(f32[4,2,32,896]{3,2,1,0:T(8,128)S(1)} %copy-done.10), channel_id=1, source_target_pairs={{4,2},{5,3},{12,10},{13,11},{20,18},{21,19},{28,26},{29,27}} | collective-permute-start | bytes 2752520 | tf_op jit(solution)/shard_map/ppermute | solution.py:245
  506.0 32.1 %collective-permute-start.43 = (f32[4,2,32,128]{3,2,1,0:T(8,128)S(1)}, f32[4,2,32,128]{3,2,1,0:T(8,128)S(1)}, u32[]{:S(2)}, u32[]{:S(2)}) collective-permute-start(f32[4,2,32,128]{3,2,1,0:T(8,128)S(1)} %copy-done.32), channel_id=1, source_target_pairs={{4,6},{5,7},{12,14},{13,15},{20,22},{21,23},{28,30},{29,31}} | collective-permute-start | bytes 393224 | tf_op jit(solution)/shard_map/ppermute | solution.py:245
  508.7 19.0 %copy-start.31 = (f32[4,2,32,896]{3,2,1,0:T(8,128)S(1)}, f32[4,2,32,896]{3,2,1,0:T(8,128)}, u32[]{:S(2)}) copy-start(f32[4,2,32,896]{3,2,1,0:T(8,128)} %get-tuple-element.191) | copy-start | bytes 2752516
  512.3 46.2 %collective-permute-start.38 = (f32[8,2,32,512]{3,2,1,0:T(8,128)S(1)}, f32[8,2,32,512]{3,2,1,0:T(8,128)S(1)}, u32[]{:S(2)}, u32[]{:S(2)}) collective-permute-start(f32[8,2,32,512]{3,2,1,0:T(8,128)S(1)} %copy-done.7), channel_id=1, source_target_pairs={{2,0},{3,1},{10,8},{11,9},{18,16},{19,17},{26,24},{27,25}} | collective-permute-start | bytes 3145736 | tf_op jit(solution)/shard_map/ppermute | solution.py:245
  527.7 30.0 %collective-permute-start.46 = (f32[4,2,32,896]{3,2,1,0:T(8,128)S(1)}, f32[4,2,32,896]{3,2,1,0:T(8,128)S(1)}, u32[]{:S(2)}, u32[]{:S(2)}) collective-permute-start(f32[4,2,32,896]{3,2,1,0:T(8,128)S(1)} %copy-done.31), channel_id=1, source_target_pairs={{0,2},{1,3},{8,10},{9,11},{16,18},{17,19},{24,26},{25,27}} | collective-permute-start | bytes 2752520 | tf_op jit(solution)/shard_map/ppermute | solution.py:245
  534.4 20.2 %collective-permute-start.42 = (f32[4,2,32,512]{3,2,1,0:T(8,128)S(1)}, f32[4,2,32,512]{3,2,1,0:T(8,128)S(1)}, u32[]{:S(2)}, u32[]{:S(2)}) collective-permute-start(f32[4,2,32,512]{3,2,1,0:T(8,128)S(1)} %slice_add_fusion.13), channel_id=1, source_target_pairs={{2,0},{3,1},{10,8},{11,9},{18,16},{19,17},{26,24},{27,25}} | collective-permute-start | bytes 1572872 | tf_op jit(solution)/shard_map/ppermute | solution.py:245
  536.8 18.9 %copy-start.30 = (f32[4,2,32,384]{3,2,1,0:T(8,128)S(1)}, f32[4,2,32,384]{3,2,1,0:T(8,128)}, u32[]{:S(2)}) copy-start(f32[4,2,32,384]{3,2,1,0:T(8,128)} %copy-done.29) | copy-start | bytes 1179652
  538.2 23.6 %collective-permute-start.44 = (f32[4,2,32,1152]{3,2,1,0:T(8,128)S(1)}, f32[4,2,32,1152]{3,2,1,0:T(8,128)S(1)}, u32[]{:S(2)}, u32[]{:S(2)}) collective-permute-start(f32[4,2,32,1152]{3,2,1,0:T(8,128)S(1)} %copy-done.21), channel_id=1, source_target_pairs={{6,4},{7,5},{14,12},{15,13},{22,20},{23,21},{30,28},{31,29}} | collective-permute-start | bytes 3538952 | tf_op jit(solution)/shard_map/ppermute | solution.py:245
  557.7 4.0 copy-start.26
  557.8 14.6 %collective-permute-start.47 = (f32[4,2,32,384]{3,2,1,0:T(8,128)S(1)}, f32[4,2,32,384]{3,2,1,0:T(8,128)S(1)}, u32[]{:S(2)}, u32[]{:S(2)}) collective-permute-start(f32[4,2,32,384]{3,2,1,0:T(8,128)S(1)} %slice_add_fusion.18), channel_id=1, source_target_pairs={{2,4},{3,5},{10,12},{11,13},{18,20},{19,21},{26,28},{27,29}} | collective-permute-start | bytes 1179656 | tf_op jit(solution)/shard_map/ppermute | solution.py:245
  561.9 11.2 %collective-permute-start.45 = (f32[4,2,32,896]{3,2,1,0:T(8,128)S(1)}, f32[4,2,32,896]{3,2,1,0:T(8,128)}, u32[]{:S(2)}, u32[]{:S(2)}) collective-permute-start(f32[4,2,32,896]{3,2,1,0:T(8,128)S(1)} %slice_add_fusion.4), channel_id=1, source_target_pairs={{4,2},{5,3},{12,10},{13,11},{20,18},{21,19},{28,26},{29,27}} | collective-permute-start | bytes 2752520 | tf_op jit(solution)/shard_map/ppermute | solution.py:245
  572.4 10.9 %collective-permute-start.49 = (f32[4,2,32,128]{3,2,1,0:T(8,128)S(1)}, f32[4,2,32,128]{3,2,1,0:T(8,128)S(1)}, u32[]{:S(2)}, u32[]{:S(2)}) collective-permute-start(f32[4,2,32,128]{3,2,1,0:T(8,128)S(1)} %slice_add_fusion.34), channel_id=1, source_target_pairs={{4,6},{5,7},{12,14},{13,15},{20,22},{21,23},{28,30},{29,31}} | collective-permute-start | bytes 393224 | tf_op jit(solution)/shard_map/ppermute | solution.py:245
  574.3 15.0 %collective-permute-start.48 = (f32[4,2,32,512]{3,2,1,0:T(8,128)S(1)}, f32[4,2,32,512]{3,2,1,0:T(8,128)S(1)}, u32[]{:S(2)}, u32[]{:S(2)}) collective-permute-start(f32[4,2,32,512]{3,2,1,0:T(8,128)S(1)} %slice_add_fusion.12), channel_id=1, source_target_pairs={{2,0},{3,1},{10,8},{11,9},{18,16},{19,17},{26,24},{27,25}} | collective-permute-start | bytes 1572872 | tf_op jit(solution)/shard_map/ppermute | solution.py:245
  (41 other events, 62.9 us)

commit v3 on v2

--- a/solution.py
+++ b/solution.py
@@ -363,7 +363,7 @@
             send(k + 1)
         waits = []
         for number, chain in enumerate(chains):
-            if k - number < rounds:
+            if 2 <= k - number <= rounds:
                 waits.extend(next(chain))
         near = after(near, *waits) if waits else near
         block = project(plan, side, place, count, own, near, came, legendre, given[k])
@@ -376,16 +376,10 @@
         for state in chain:
             pass
         ends.append(state)
-    parts = []
-    for numbers in (range(len(ends) - 1), range(len(ends) - 1, len(ends))):
-        if len(numbers) == 0:
-            continue
-        blocks = [close(*ends[k], zone, plan, half_degrees, kept[-1]) for k in numbers]
-        place = pieces[numbers[0]][0]
-        count = sum(pieces[k][1] for k in numbers)
-        mine = finish(count, place, jnp.concatenate(blocks, 0))
+    for k, end in enumerate(ends):
+        place, count = pieces[k][:2]
+        mine = finish(count, place, close(*end, zone, plan, half_degrees, kept[-1]))
         result = lax.dynamic_update_slice(result, mine, (place,) + (0,) * 5)
-        parts.append(mine)
     return result[None]
 
 

time: 608 us -> 616 us (1.013)
  starting transfers between devices: 74.5 us -> 111 us
  waiting for transfers between devices: 221 us -> 187 us
  local copies, waits for them, and re-layouts: 19.1 us -> 26.3 us
    ppermute x8, waiting for transfers between devices: 95.1 us -> 55.5 us  [lon_swap(): return lax.ppermute(value, 'lon', [(i, i ^ bit) for i in range(lon_count)])]
    ppermute x6, waiting for transfers between devices: 38.1 us -> 77.5 us  [send(): lax.ppermute(value, 'lat', [(i, i ^ 1) for i in range(lat_count)])]
    ppermute x36, starting transfers between devices: 56.3 us -> 90.9 us  [hop(): return lax.ppermute(value, 'lat', pairs)]
    ppermute x36, waiting for transfers between devices: 88.2 us -> 54.2 us  [hop(): return lax.ppermute(value, 'lat', pairs)]
    select_n x1 -> x6, other arithmetic: 0.16 us -> 10.1 us  [close(): mine = value if mine is None else jnp.where(zone == z, value, mine)]
    dynamic_update_slice x0 -> x5, other arithmetic: none -> 7.88 us  [local(): result = lax.dynamic_update_slice(result, mine, (place,) + (0,) * 5)]
    broadcast_in_dim x1 -> x0, other arithmetic: 7.41 us -> none  [local(): return result[None]]
    unnamed x11 -> x7, other arithmetic: 9.26 us -> 2.46 us
  transfers between devices with their start and end apart: 50 -> 50, of which waited for: 13 -> 11; matrix products, arithmetic and copies ran while one was open for 14% -> 15% of each run, Pallas kernels for 24% -> 25%
where the time goes in v3:
time: 616 us; the launch traced here: 609 us
  Pallas kernels  188 us (31%)
  waiting for transfers between devices  187 us (30%)
  starting transfers between devices  111 us (18%)
  other arithmetic  95.6 us (16%)
  local copies, waits for them, and re-layouts  26.3 us (4%)
    pallas_call x12, Pallas kernels, project(): pl.pallas_call(kernel, grid_spec=pltpu.PrefetchScalarGridSpec(num_scalar_...  95.8 us
    ppermute x36, starting transfers between devices, hop(): return lax.ppermute(value, 'lat', pairs)  90.9 us
    ppermute x6, waiting for transfers between devices, send(): lax.ppermute(value, 'lat', [(i, i ^ 1) for i in range(lat_count)])  77.5 us
    ppermute x8, waiting for transfers between devices, lon_swap(): return lax.ppermute(value, 'lon', [(i, i ^ bit) for i in range(lon_count)])  55.5 us
    ppermute x36, waiting for transfers between devices, hop(): return lax.ppermute(value, 'lat', pairs)  54.2 us
    pallas_call x2, Pallas kernels, fourier(): pl.pallas_call(second_fourier_kernel, grid=(rows // block,), in_specs=[wh...  38.9 us
    pallas_call x2, Pallas kernels, fourier(): pl.pallas_call(first_fourier_kernel, grid=(rows // block,), in_specs=[who...  36.6 us
    add x18, other arithmetic, close(): value = value + came_up[z - 1][..., places[z]:places[z] + width]  23.3 us
  transfers between devices with their start and end apart: 50, of which 11 were waited for; matrix products, arithmetic and copies ran while one was open for 15% of the time, Pallas kernels for 25%

profile of v3, /device:TPU:0, one launch (start us, length us, event | category | flops | bytes accessed | tf_op | source)
XLA Modules:
  0.0 608.7 jit_solution(11811980298247129037)
XLA Ops:
  0.2 2.1 sine_multiply_fusion
  7.5 16.3 %tendencies.1 = (bf16[8,2,256,1024]{3,2,1,0:T(8,128)(2,1)}, bf16[8,2,256,1024]{3,2,1,0:T(8,128)(2,1)}) custom-call(bf16[12,2,2,128,1024]{4,3,2,1,0:T(8,128)(2,1)} %grid_ref.1), custom_call_target="tpu_custom_call" | custom-call | flops 25165824 | bytes 31457280 | tf_op jit(solution)/shard_map/tendencies/pallas_call | solution.py:56
  26.3 1.9 constant_dynamic-update-slice_fusion.6
  33.8 18.2 %fourier_first.2 = f32[512,4096]{1,0:T(8,128)} custom-call(bf16[512,1024]{1,0:T(8,128)(2,1)} %get-tuple-element.202.ph_ref, bf16[512,1024]{1,0:T(8,128)(2,1)} %get-tuple-element.201.pl_ref, bf16[4096,1024]{1,0:T(8,128)(2,1)} %bitcast.188, bf16[4096,1024]{1,0:T(8,128)(2,1)} %bitcast.192), custom_call_target="tpu_custom_call" | custom-call | flops 12884901888 | bytes 25165824 | tf_op jit(solution)/shard_map/fourier_first/pallas_call | solution.py:111
  55.2 18.4 %fourier_first.3 = f32[512,4096]{1,0:T(8,128)} custom-call(bf16[512,1024]{1,0:T(8,128)(2,1)} %get-tuple-element.204.ph_ref, bf16[512,1024]{1,0:T(8,128)(2,1)} %get-tuple-element.203.pl_ref, bf16[4096,1024]{1,0:T(8,128)(2,1)} %bitcast.189, bf16[4096,1024]{1,0:T(8,128)(2,1)} %bitcast.193), custom_call_target="tpu_custom_call" | custom-call | flops 12884901888 | bytes 25165824 | tf_op jit(solution)/shard_map/fourier_first/pallas_call | solution.py:111
  73.6 1.8 fusion
  75.4 19.5 %fourier_second.2 = (f32[64,4096]{1,0:T(8,128)}, f32[64,4096]{1,0:T(8,128)}, f32[128,4096]{1,0:T(8,128)}, f32[64,4096]{1,0:T(8,128)}, f32[64,4096]{1,0:T(8,128)}, /*index=5*/f32[128,4096]{1,0:T(8,128)}) custom-call(bf16[512,1024]{1,0:T(8,128)(2,1)} %get-tuple-element.206.ph_ref, bf16[512,1024]{1,0:T(8,128)(2,1)} %get-tuple-element.205.pl_ref, ...), custom_call_target="tpu_custom_call" | custom-call | flops 12884901888 | bytes 25165824 | tf_op jit(solution)/shard_map/fourier_second/pallas_call | solution.py:120
  94.9 3.0 collective-permute-start.1
  97.9 3.4 fusion.3
  101.4 2.0 collective-permute-start.16
  103.4 18.8 %collective-permute-done.1.refs_5_ = f32[64,4096]{1,0:T(8,128)S(1)} collective-permute-done((f32[64,4096]{1,0:T(8,128)}, f32[64,4096]{1,0:T(8,128)S(1)}, u32[]{:S(2)}, u32[]{:S(2)}) %collective-permute-start.1) | collective-permute-done | bytes 1048608 | tf_op jit(solution)/shard_map/ppermute | solution.py:305
  123.1 6.7 %legendre_sent.6 = f32[4,2,32,1280]{3,2,1,0:T(8,128)} custom-call(s32[1]{0:T(128)} %bitcast.61.refs_0_, s32[6]{0:T(128)} %constant.101.clone.refs_1_, s32[6]{0:T(128)} %constant.102.clone.refs_2_, s32[6]{0:T(128)} %constant.103.clone.refs_3_, f32[64,4096]{1,0:T(8,128)} %get-tuple-element.106.refs_4_, f32[64,4096]{1,0:T(8,128)} %copy-done.4, ...), custom_call_target="tpu_custom_call" | custom-call | flops 201326592 | bytes 3801088 | tf_op jit(solution)/shard_map/legendre_sent/pallas_call | solution.py:222
  129.8 2.0 collective-permute-start.2
  131.8 19.5 %fourier_second.3 = (f32[128,4096]{1,0:T(8,128)}, f32[64,4096]{1,0:T(8,128)}, f32[64,4096]{1,0:T(8,128)}, f32[128,4096]{1,0:T(8,128)}, f32[64,4096]{1,0:T(8,128)}, /*index=5*/f32[64,4096]{1,0:T(8,128)}) custom-call(bf16[512,1024]{1,0:T(8,128)(2,1)} %get-tuple-element.200.ph_ref, bf16[512,1024]{1,0:T(8,128)(2,1)} %get-tuple-element.199.pl_ref, ...), custom_call_target="tpu_custom_call" | custom-call | flops 12884901888 | bytes 25165824 | tf_op jit(solution)/shard_map/fourier_second/pallas_call | solution.py:120
  152.9 36.7 %collective-permute-done.16.refs_5_ = f32[64,4096]{1,0:T(8,128)S(1)} collective-permute-done((f32[64,4096]{1,0:T(8,128)}, f32[64,4096]{1,0:T(8,128)S(1)}, u32[]{:S(2)}, u32[]{:S(2)}) %collective-permute-start.16) | collective-permute-done | bytes 1048608 | tf_op jit(solution)/shard_map/ppermute | solution.py:305
  190.6 6.8 %legendre_sent.8 = f32[4,2,32,1280]{3,2,1,0:T(8,128)} custom-call(s32[1]{0:T(128)} %bitcast.61.refs_0_, s32[6]{0:T(128)} %constant.101.clone.refs_1_, s32[6]{0:T(128)} %constant.102.clone.refs_2_, s32[6]{0:T(128)} %constant.103.clone.refs_3_, f32[64,4096]{1,0:T(8,128)} %get-tuple-element.119.refs_4_, f32[64,4096]{1,0:T(8,128)} %copy-done.3, ...), custom_call_target="tpu_custom_call" | custom-call | flops 201326592 | bytes 3801088 | tf_op jit(solution)/shard_map/legendre_sent/pallas_call | solution.py:222
  197.3 2.0 collective-permute-start.17
  199.3 7.6 %legendre_kept.6 = (f32[4,2,32,1152]{3,2,1,0:T(8,128)}, f32[4,2,32,896]{3,2,1,0:T(8,128)}) custom-call(s32[1]{0:T(128)} %bitcast.refs_0_, s32[6]{0:T(128)} %constant.101.clone.refs_1_, s32[6]{0:T(128)} %constant.102.clone.refs_2_, s32[6]{0:T(128)} %constant.103.clone.refs_3_, f32[64,4096]{1,0:T(8,128)} %get-tuple-element.106.refs_4_, f32[64,4096]{1,0:T(8,128)} %copy-done.4, ...), custom_call_target="tpu_custom_call" | custom-call | flops 201326592 | bytes 3801088 | tf_op jit(solution)/shard_map/legendre_kept/pallas_call | solution.py:222
  206.9 8.7 %legendre_sent.7 = f32[8,2,32,1280]{3,2,1,0:T(8,128)} custom-call(s32[1]{0:T(128)} %bitcast.61.refs_0_, s32[6]{0:T(128)} %constant.101.clone.refs_1_, s32[6]{0:T(128)} %constant.102.clone.refs_2_, s32[6]{0:T(128)} %constant.103.clone.refs_3_, f32[128,4096]{1,0:T(8,128)} %get-tuple-element.115.refs_4_, f32[128,4096]{1,0:T(8,128)} %collective-permute-done.10.refs_5_, ...), custom_call_target="tpu_custom_call" | custom-call | flops 402653184 | bytes 7602176 | tf_op jit(solution)/shard_map/legendre_sent/pallas_call | solution.py:222
  217.3 11.9 %collective-permute-done.17.refs_7_ = f32[4,2,32,1280]{3,2,1,0:T(8,128)S(1)} collective-permute-done((f32[4,2,32,1280]{3,2,1,0:T(8,128)}, f32[4,2,32,1280]{3,2,1,0:T(8,128)S(1)}, u32[]{:S(2)}, u32[]{:S(2)}) %collective-permute-start.17) | collective-permute-done | bytes 1310752 | tf_op jit(solution)/shard_map/ppermute | solution.py:356
  230.2 7.8 %legendre_kept.8 = (f32[4,2,32,1152]{3,2,1,0:T(8,128)}, f32[4,2,32,896]{3,2,1,0:T(8,128)}) custom-call(s32[1]{0:T(128)} %bitcast.refs_0_, s32[6]{0:T(128)} %constant.101.clone.refs_1_, s32[6]{0:T(128)} %constant.102.clone.refs_2_, s32[6]{0:T(128)} %constant.103.clone.refs_3_, f32[64,4096]{1,0:T(8,128)} %get-tuple-element.119.refs_4_, f32[64,4096]{1,0:T(8,128)} %copy-done.3, ...), custom_call_target="tpu_custom_call" | custom-call | flops 201326592 | bytes 3801088 | tf_op jit(solution)/shard_map/legendre_kept/pallas_call | solution.py:222
  239.4 8.7 %legendre_sent.9 = f32[8,2,32,1280]{3,2,1,0:T(8,128)} custom-call(s32[1]{0:T(128)} %bitcast.61.refs_0_, s32[6]{0:T(128)} %constant.101.clone.refs_1_, s32[6]{0:T(128)} %constant.102.clone.refs_2_, s32[6]{0:T(128)} %constant.103.clone.refs_3_, f32[128,4096]{1,0:T(8,128)} %get-tuple-element.125.refs_4_, f32[128,4096]{1,0:T(8,128)} %copy-done, ...), custom_call_target="tpu_custom_call" | custom-call | flops 402653184 | bytes 7602176 | tf_op jit(solution)/shard_map/legendre_sent/pallas_call | solution.py:222
  248.1 2.0 collective-permute-start.21
  250.1 3.5 collective-permute-start.5
  258.0 16.7 %collective-permute-done.5 = f32[4,2,32,896]{3,2,1,0:T(8,128)S(1)} collective-permute-done((f32[4,2,32,896]{3,2,1,0:T(8,128)}, f32[4,2,32,896]{3,2,1,0:T(8,128)S(1)}, u32[]{:S(2)}, u32[]{:S(2)}) %collective-permute-start.5) | collective-permute-done | bytes 917536 | tf_op jit(solution)/shard_map/ppermute | solution.py:245
  277.3 8.1 %collective-permute-done.11.refs_7_ = f32[8,2,32,1280]{3,2,1,0:T(8,128)} collective-permute-done((f32[8,2,32,1280]{3,2,1,0:T(8,128)}, f32[8,2,32,1280]{3,2,1,0:T(8,128)}, u32[]{:S(2)}, u32[]{:S(2)}) %collective-permute-start.11) | collective-permute-done | bytes 2621472 | tf_op jit(solution)/shard_map/ppermute | solution.py:356
  286.2 10.3 %legendre_kept.7 = (f32[8,2,32,1152]{3,2,1,0:T(8,128)}, f32[8,2,32,896]{3,2,1,0:T(8,128)}) custom-call(s32[1]{0:T(128)} %bitcast.refs_0_, s32[6]{0:T(128)} %constant.101.clone.refs_1_, s32[6]{0:T(128)} %constant.102.clone.refs_2_, s32[6]{0:T(128)} %constant.103.clone.refs_3_, f32[128,4096]{1,0:T(8,128)} %get-tuple-element.115.refs_4_, ...), custom_call_target="tpu_custom_call" | custom-call | flops 402653184 | bytes 7602176 | tf_op jit(solution)/shard_map/legendre_kept/pallas_call | solution.py:222
  297.4 2.0 collective-permute-start.36
  299.4 2.1 collective-permute-start.12
  302.2 7.6 %collective-permute-start.14 = (f32[8,2,32,896]{3,2,1,0:T(8,128)}, f32[8,2,32,896]{3,2,1,0:T(8,128)}, u32[]{:S(2)}, u32[]{:S(2)}) collective-permute-start(f32[8,2,32,896]{3,2,1,0:T(8,128)} %get-tuple-element.153), channel_id=1, source_target_pairs={{0,2},{1,3},{8,10},{9,11},{16,18},{17,19},{24,26},{25,27}} | collective-permute-start | bytes 5505032 | tf_op jit(solution)/shard_map/ppermute | solution.py:245
  315.1 24.3 %collective-permute-done.21.refs_7_ = f32[8,2,32,1280]{3,2,1,0:T(8,128)} collective-permute-done((f32[8,2,32,1280]{3,2,1,0:T(8,128)}, f32[8,2,32,1280]{3,2,1,0:T(8,128)}, u32[]{:S(2)}, u32[]{:S(2)}) %collective-permute-start.21) | collective-permute-done | bytes 2621472 | tf_op jit(solution)/shard_map/ppermute | solution.py:356
  340.9 1.9 slice_add_fusion.15
  342.8 10.4 %legendre_kept.9 = (f32[8,2,32,1152]{3,2,1,0:T(8,128)}, f32[8,2,32,896]{3,2,1,0:T(8,128)}) custom-call(s32[1]{0:T(128)} %bitcast.refs_0_, s32[6]{0:T(128)} %constant.101.clone.refs_1_, s32[6]{0:T(128)} %constant.102.clone.refs_2_, s32[6]{0:T(128)} %constant.103.clone.refs_3_, f32[128,4096]{1,0:T(8,128)} %get-tuple-element.125.refs_4_, f32[128,4096]{1,0:T(8,128)} %copy-done, ...), custom_call_target="tpu_custom_call" | custom-call | flops 402653184 | bytes 7602176 | tf_op jit(solution)/shard_map/legendre_kept/pallas_call | solution.py:222
  353.2 2.1 collective-permute-start.22
  355.3 7.5 %collective-permute-start.23 = (f32[8,2,32,896]{3,2,1,0:T(8,128)}, f32[8,2,32,896]{3,2,1,0:T(8,128)}, u32[]{:S(2)}, u32[]{:S(2)}) collective-permute-start(f32[8,2,32,896]{3,2,1,0:T(8,128)} %get-tuple-element.163), channel_id=1, source_target_pairs={{0,2},{1,3},{8,10},{9,11},{16,18},{17,19},{24,26},{25,27}} | collective-permute-start | bytes 5505032 | tf_op jit(solution)/shard_map/ppermute | solution.py:245
  362.7 6.9 %legendre_sent.11 = f32[4,2,32,1280]{3,2,1,0:T(8,128)} custom-call(s32[1]{0:T(128)} %bitcast.61.refs_0_, s32[6]{0:T(128)} %constant.101.clone.refs_1_, s32[6]{0:T(128)} %constant.102.clone.refs_2_, s32[6]{0:T(128)} %constant.103.clone.refs_3_, f32[64,4096]{1,0:T(8,128)} %get-tuple-element.176.refs_4_, f32[64,4096]{1,0:T(8,128)} %copy-done.2, ...), custom_call_target="tpu_custom_call" | custom-call | flops 201326592 | bytes 3801088 | tf_op jit(solution)/shard_map/legendre_sent/pallas_call | solution.py:222
  374.0 1.9 slice_add_fusion.14
  375.9 2.3 slice_add_fusion.9
  381.6 15.9 %collective-permute-done.37.refs_7_ = f32[4,2,32,1280]{3,2,1,0:T(8,128)} collective-permute-done((f32[4,2,32,1280]{3,2,1,0:T(8,128)}, f32[4,2,32,1280]{3,2,1,0:T(8,128)}, u32[]{:S(2)}, u32[]{:S(2)}) %collective-permute-start.37) | collective-permute-done | bytes 1310752 | tf_op jit(solution)/shard_map/ppermute | solution.py:356
  397.4 7.6 %legendre_kept.11 = (f32[4,2,32,1152]{3,2,1,0:T(8,128)}, f32[4,2,32,896]{3,2,1,0:T(8,128)}) custom-call(s32[1]{0:T(128)} %bitcast.refs_0_, s32[6]{0:T(128)} %constant.101.clone.refs_1_, s32[6]{0:T(128)} %constant.102.clone.refs_2_, s32[6]{0:T(128)} %constant.103.clone.refs_3_, f32[64,4096]{1,0:T(8,128)} %get-tuple-element.176.refs_4_, f32[64,4096]{1,0:T(8,128)} %copy-done.2, ...), custom_call_target="tpu_custom_call" | custom-call | flops 201326592 | bytes 3801088 | tf_op jit(solution)/shard_map/legendre_kept/pallas_call | solution.py:222
  405.1 2.3 collective-permute-start.40
  408.5 6.7 %legendre_sent.10 = f32[4,2,32,1280]{3,2,1,0:T(8,128)} custom-call(s32[1]{0:T(128)} %bitcast.61.refs_0_, s32[6]{0:T(128)} %constant.101.clone.refs_1_, s32[6]{0:T(128)} %constant.102.clone.refs_2_, s32[6]{0:T(128)} %constant.103.clone.refs_3_, f32[64,4096]{1,0:T(8,128)} %get-tuple-element.130.refs_4_, f32[64,4096]{1,0:T(8,128)} %copy-done.1, ...), custom_call_target="tpu_custom_call" | custom-call | flops 201326592 | bytes 3801088 | tf_op jit(solution)/shard_map/legendre_sent/pallas_call | solution.py:222
  419.3 3.0 slice_add_fusion
  434.2 17.3 %collective-permute-done.25.refs_7_ = f32[4,2,32,1280]{3,2,1,0:T(8,128)S(1)} collective-permute-done((f32[4,2,32,1280]{3,2,1,0:T(8,128)S(1)}, f32[4,2,32,1280]{3,2,1,0:T(8,128)S(1)}, u32[]{:S(2)}, u32[]{:S(2)}) %collective-permute-start.25) | collective-permute-done | bytes 1310752 | tf_op jit(solution)/shard_map/ppermute | solution.py:356
  452.6 1.9 collective-permute-start.32
  454.5 7.6 %legendre_kept.10 = (f32[4,2,32,1152]{3,2,1,0:T(8,128)}, f32[4,2,32,896]{3,2,1,0:T(8,128)}) custom-call(s32[1]{0:T(128)} %bitcast.refs_0_, s32[6]{0:T(128)} %constant.101.clone.refs_1_, s32[6]{0:T(128)} %constant.102.clone.refs_2_, s32[6]{0:T(128)} %constant.103.clone.refs_3_, f32[64,4096]{1,0:T(8,128)} %get-tuple-element.130.refs_4_, f32[64,4096]{1,0:T(8,128)} %copy-done.1, ...), custom_call_target="tpu_custom_call" | custom-call | flops 201326592 | bytes 3801088 | tf_op jit(solution)/shard_map/legendre_kept/pallas_call | solution.py:222
  471.2 2.1 select_select_fusion.5
  474.5 2.1 slice_add_fusion.24
  477.6 2.1 reshape.675
  479.7 2.3 select_select_fusion.4
  482.0 2.2 reshape.676
  485.7 4.1 pad_bitcast_fusion
  494.0 2.7 slice_add_fusion.2
  498.1 28.7 %collective-permute-start.46 = (f32[4,2,32,896]{3,2,1,0:T(8,128)}, f32[4,2,32,896]{3,2,1,0:T(8,128)}, u32[]{:S(2)}, u32[]{:S(2)}) collective-permute-start(f32[4,2,32,896]{3,2,1,0:T(8,128)} %get-tuple-element.189), channel_id=1, source_target_pairs={{0,2},{1,3},{8,10},{9,11},{16,18},{17,19},{24,26},{25,27}} | collective-permute-start | bytes 2752520 | tf_op jit(solution)/shard_map/ppermute | solution.py:245
  526.7 19.6 %collective-permute-done.42 = f32[4,2,32,512]{3,2,1,0:T(8,128)S(1)} collective-permute-done((f32[4,2,32,512]{3,2,1,0:T(8,128)S(1)}, f32[4,2,32,512]{3,2,1,0:T(8,128)S(1)}, u32[]{:S(2)}, u32[]{:S(2)}) %collective-permute-start.42) | collective-permute-done | bytes 524320 | tf_op jit(solution)/shard_map/ppermute | solution.py:245
  551.9 2.1 reshape.679
  554.9 1.9 slice_add_fusion.18
  559.3 8.3 %collective-permute-done.34 = f32[8,2,32,512]{3,2,1,0:T(8,128)} collective-permute-done((f32[8,2,32,512]{3,2,1,0:T(8,128)}, f32[8,2,32,512]{3,2,1,0:T(8,128)}, u32[]{:S(2)}, u32[]{:S(2)}) %collective-permute-start.34) | collective-permute-done | bytes 1048608 | tf_op jit(solution)/shard_map/ppermute | solution.py:245
  569.1 2.1 slice_add_fusion.16
  572.8 2.6 select_select_fusion.1
  581.6 1.9 select_select_fusion
  584.1 2.0 bitcast_dynamic-update-slice_fusion.1
  588.8 2.0 bitcast_dynamic-update-slice_fusion
  593.8 9.5 %collective-permute-done.48 = f32[4,2,32,512]{3,2,1,0:T(8,128)S(1)} collective-permute-done((f32[4,2,32,512]{3,2,1,0:T(8,128)S(1)}, f32[4,2,32,512]{3,2,1,0:T(8,128)S(1)}, u32[]{:S(2)}, u32[]{:S(2)}) %collective-permute-start.48) | collective-permute-done | bytes 524320 | tf_op jit(solution)/shard_map/ppermute | solution.py:245
  (287 shorter events, 113.1 us)
Async XLA Ops:
  33.8 18.7 %copy-start.47 = (f32[1,4,1024]{2,1,0:T(4,128)S(1)}, f32[1,4,1024]{2,1,0:T(4,128)}, u32[]{:S(2)}) copy-start(f32[1,4,1024]{2,1,0:T(4,128)} %get-tuple-element.271) | copy-start | bytes 49156
  33.8 18.7 %copy-start.48 = (f32[1,4,1024]{2,1,0:T(4,128)S(1)}, f32[1,4,1024]{2,1,0:T(4,128)}, u32[]{:S(2)}) copy-start(f32[1,4,1024]{2,1,0:T(4,128)} %get-tuple-element.272) | copy-start | bytes 49156
  52.0 23.4 %collective-permute-start = (f32[512,4096]{1,0:T(8,128)}, f32[512,4096]{1,0:T(8,128)}, u32[]{:S(2)}, u32[]{:S(2)}) collective-permute-start(f32[512,4096]{1,0:T(8,128)} %fourier_first.2), channel_id=1, source_target_pairs={{0,8},{8,0},{16,24},{24,16},{1,9},{9,1},{17,25},{25,17},{2,10},{10... | collective-permute-start | bytes 25165832 | tf_op jit(solution)/shard_map/ppermute | solution.py:305
  55.2 18.4 %copy-start.11 = (f32[512,1024]{1,0:T(8,128)S(1)}, f32[512,1024]{1,0:T(8,128)}, u32[]{:S(2)}) copy-start(f32[512,1024]{1,0:T(8,128)} %get-tuple-element.297) | copy-start | bytes 6291460
  73.5 58.3 %collective-permute-start.9 = (f32[512,4096]{1,0:T(8,128)}, f32[512,4096]{1,0:T(8,128)}, u32[]{:S(2)}, u32[]{:S(2)}) collective-permute-start(f32[512,4096]{1,0:T(8,128)} %fourier_first.3), channel_id=1, source_target_pairs={{0,8},{8,0},{16,24},{24,16},{1,9},{9,1},{17,25},{25,17},{2,10},{10... | collective-permute-start | bytes 25165832 | tf_op jit(solution)/shard_map/ppermute | solution.py:305
  94.9 27.2 %collective-permute-start.1 = (f32[64,4096]{1,0:T(8,128)}, f32[64,4096]{1,0:T(8,128)S(1)}, u32[]{:S(2)}, u32[]{:S(2)}) collective-permute-start(f32[64,4096]{1,0:T(8,128)} %get-tuple-element.107), channel_id=1, source_target_pairs={{0,16},{8,24},{16,0},{24,8},{1,17},{9,25},{17,1},{25,9},{2,18},{10... | collective-permute-start | bytes 3145736 | tf_op jit(solution)/shard_map/ppermute | solution.py:305
  101.3 105.6 %collective-permute-start.10 = (f32[128,4096]{1,0:T(8,128)}, f32[128,4096]{1,0:T(8,128)}, u32[]{:S(2)}, u32[]{:S(2)}) collective-permute-start(f32[128,4096]{1,0:T(8,128)} %get-tuple-element.114), channel_id=1, source_target_pairs={{0,16},{8,24},{16,0},{24,8},{1,17},{9,25},{17,1},{25,9},{2,18},{10... | collective-permute-start | bytes 6291464 | tf_op jit(solution)/shard_map/ppermute | solution.py:305
  101.4 88.2 %collective-permute-start.16 = (f32[64,4096]{1,0:T(8,128)}, f32[64,4096]{1,0:T(8,128)S(1)}, u32[]{:S(2)}, u32[]{:S(2)}) collective-permute-start(f32[64,4096]{1,0:T(8,128)} %get-tuple-element.120), channel_id=1, source_target_pairs={{0,16},{8,24},{16,0},{24,8},{1,17},{9,25},{17,1},{25,9},{2,18},{10... | collective-permute-start | bytes 3145736 | tf_op jit(solution)/shard_map/ppermute | solution.py:305
  129.8 69.5 %collective-permute-start.2 = (f32[4,2,32,1280]{3,2,1,0:T(8,128)}, f32[4,2,32,1280]{3,2,1,0:T(8,128)}, u32[]{:S(2)}, u32[]{:S(2)}) collective-permute-start(f32[4,2,32,1280]{3,2,1,0:T(8,128)} %legendre_sent.6), channel_id=1, source_target_pairs={{0,1},{1,0},{2,3},{3,2},{4,5},{5,4},{6,7},{7,6},{8,9},{9,8},{10,11... | collective-permute-start | bytes 3932168 | tf_op jit(solution)/shard_map/ppermute | solution.py:356
  151.3 86.8 %collective-permute-start.20 = (f32[128,4096]{1,0:T(8,128)}, f32[128,4096]{1,0:T(8,128)S(1)}, u32[]{:S(2)}, u32[]{:S(2)}) collective-permute-start(f32[128,4096]{1,0:T(8,128)} %get-tuple-element.124), channel_id=1, source_target_pairs={{0,16},{8,24},{16,0},{24,8},{1,17},{9,25},{17,1},{25,9},{2,18},{10... | collective-permute-start | bytes 6291464 | tf_op jit(solution)/shard_map/ppermute | solution.py:305
  197.3 31.9 %collective-permute-start.17 = (f32[4,2,32,1280]{3,2,1,0:T(8,128)}, f32[4,2,32,1280]{3,2,1,0:T(8,128)S(1)}, u32[]{:S(2)}, u32[]{:S(2)}) collective-permute-start(f32[4,2,32,1280]{3,2,1,0:T(8,128)} %legendre_sent.8), channel_id=1, source_target_pairs={{0,1},{1,0},{2,3},{3,2},{4,5},{5,4},{6,7},{7,6},{8,9},{9,8},{10,11... | collective-permute-start | bytes 3932168 | tf_op jit(solution)/shard_map/ppermute | solution.py:356
  215.6 69.9 %collective-permute-start.11 = (f32[8,2,32,1280]{3,2,1,0:T(8,128)}, f32[8,2,32,1280]{3,2,1,0:T(8,128)}, u32[]{:S(2)}, u32[]{:S(2)}) collective-permute-start(f32[8,2,32,1280]{3,2,1,0:T(8,128)} %legendre_sent.7), channel_id=1, source_target_pairs={{0,1},{1,0},{2,3},{3,2},{4,5},{5,4},{6,7},{7,6},{8,9},{9,8},{10,11... | collective-permute-start | bytes 7864328 | tf_op jit(solution)/shard_map/ppermute | solution.py:356
  215.6 39.7 %collective-permute-start.3 = (f32[4,2,32,1152]{3,2,1,0:T(8,128)}, f32[4,2,32,1152]{3,2,1,0:T(8,128)}, u32[]{:S(2)}, u32[]{:S(2)}) collective-permute-start(f32[4,2,32,1152]{3,2,1,0:T(8,128)} %get-tuple-element.135), channel_id=1, source_target_pairs={{6,4},{7,5},{14,12},{15,13},{22,20},{23,21},{30,28},{31,29}} | collective-permute-start | bytes 3538952 | tf_op jit(solution)/shard_map/ppermute | solution.py:245
  238.1 18.6 %copy-start.24 = (f32[4,2,32,1152]{3,2,1,0:T(8,128)S(1)}, f32[4,2,32,1152]{3,2,1,0:T(8,128)}, u32[]{:S(2)}) copy-start(f32[4,2,32,1152]{3,2,1,0:T(8,128)} %get-tuple-element.135) | copy-start | bytes 3538948
  248.1 91.3 %collective-permute-start.21 = (f32[8,2,32,1280]{3,2,1,0:T(8,128)}, f32[8,2,32,1280]{3,2,1,0:T(8,128)}, u32[]{:S(2)}, u32[]{:S(2)}) collective-permute-start(f32[8,2,32,1280]{3,2,1,0:T(8,128)} %legendre_sent.9), channel_id=1, source_target_pairs={{0,1},{1,0},{2,3},{3,2},{4,5},{5,4},{6,7},{7,6},{8,9},{9,8},{10,11... | collective-permute-start | bytes 7864328 | tf_op jit(solution)/shard_map/ppermute | solution.py:356
  250.1 24.5 %collective-permute-start.5 = (f32[4,2,32,896]{3,2,1,0:T(8,128)}, f32[4,2,32,896]{3,2,1,0:T(8,128)S(1)}, u32[]{:S(2)}, u32[]{:S(2)}) collective-permute-start(f32[4,2,32,896]{3,2,1,0:T(8,128)} %get-tuple-element.133), channel_id=1, source_target_pairs={{0,2},{1,3},{8,10},{9,11},{16,18},{17,19},{24,26},{25,27}} | collective-permute-start | bytes 2752520 | tf_op jit(solution)/shard_map/ppermute | solution.py:245
  253.6 45.7 %collective-permute-start.18 = (f32[4,2,32,1152]{3,2,1,0:T(8,128)}, f32[4,2,32,1152]{3,2,1,0:T(8,128)}, u32[]{:S(2)}, u32[]{:S(2)}) collective-permute-start(f32[4,2,32,1152]{3,2,1,0:T(8,128)} %get-tuple-element.145), channel_id=1, source_target_pairs={{6,4},{7,5},{14,12},{15,13},{22,20},{23,21},{30,28},{31,29}} | collective-permute-start | bytes 3538952 | tf_op jit(solution)/shard_map/ppermute | solution.py:245
  255.3 41.1 %collective-permute-start.19 = (f32[4,2,32,896]{3,2,1,0:T(8,128)}, f32[4,2,32,896]{3,2,1,0:T(8,128)S(1)}, u32[]{:S(2)}, u32[]{:S(2)}) collective-permute-start(f32[4,2,32,896]{3,2,1,0:T(8,128)} %get-tuple-element.143), channel_id=1, source_target_pairs={{0,2},{1,3},{8,10},{9,11},{16,18},{17,19},{24,26},{25,27}} | collective-permute-start | bytes 2752520 | tf_op jit(solution)/shard_map/ppermute | solution.py:245
  258.0 82.9 %copy-start.6 = (f32[4,2,32,896]{3,2,1,0:T(8,128)}, f32[4,2,32,896]{3,2,1,0:T(8,128)S(1)}, u32[]{:S(2)}) copy-start(f32[4,2,32,896]{3,2,1,0:T(8,128)S(1)} %slice_add_fusion.7) | copy-start | bytes 2752516
  274.6 36.8 %collective-permute-start.4 = (f32[4,2,32,896]{3,2,1,0:T(8,128)S(1)}, f32[4,2,32,896]{3,2,1,0:T(8,128)}, u32[]{:S(2)}, u32[]{:S(2)}) collective-permute-start(f32[4,2,32,896]{3,2,1,0:T(8,128)S(1)} %slice_add_fusion.7), channel_id=1, source_target_pairs={{4,2},{5,3},{12,10},{13,11},{20,18},{21,19},{28,26},{29,27}} | collective-permute-start | bytes 2752520 | tf_op jit(solution)/shard_map/ppermute | solution.py:245
  277.3 19.1 %copy-start.31 = (f32[4,2,32,384]{3,2,1,0:T(8,128)}, f32[4,2,32,384]{3,2,1,0:T(8,128)S(1)}, u32[]{:S(2)}) copy-start(f32[4,2,32,384]{3,2,1,0:T(8,128)S(1)} %slice_add_fusion.21) | copy-start | bytes 1179652
  285.4 16.0 %collective-permute-start.6 = (f32[4,2,32,384]{3,2,1,0:T(8,128)S(1)}, f32[4,2,32,384]{3,2,1,0:T(8,128)S(1)}, u32[]{:S(2)}, u32[]{:S(2)}) collective-permute-start(f32[4,2,32,384]{3,2,1,0:T(8,128)S(1)} %slice_add_fusion.21), channel_id=1, source_target_pairs={{2,4},{3,5},{10,12},{11,13},{18,20},{19,21},{26,28},{27,29}} | collective-permute-start | bytes 1179656 | tf_op jit(solution)/shard_map/ppermute | solution.py:245
  297.4 55.8 %collective-permute-start.36 = (f32[64,4096]{1,0:T(8,128)}, f32[64,4096]{1,0:T(8,128)S(1)}, u32[]{:S(2)}, u32[]{:S(2)}) collective-permute-start(f32[64,4096]{1,0:T(8,128)} %get-tuple-element.175), channel_id=1, source_target_pairs={{0,16},{8,24},{16,0},{24,8},{1,17},{9,25},{17,1},{25,9},{2,18},{10... | collective-permute-start | bytes 3145736 | tf_op jit(solution)/shard_map/ppermute | solution.py:305
  299.4 78.8 %collective-permute-start.12 = (f32[8,2,32,1152]{3,2,1,0:T(8,128)}, f32[8,2,32,1152]{3,2,1,0:T(8,128)}, u32[]{:S(2)}, u32[]{:S(2)}) collective-permute-start(f32[8,2,32,1152]{3,2,1,0:T(8,128)} %get-tuple-element.155), channel_id=1, source_target_pairs={{6,4},{7,5},{14,12},{15,13},{22,20},{23,21},{30,28},{31,29}} | collective-permute-start | bytes 7077896 | tf_op jit(solution)/shard_map/ppermute | solution.py:245
  302.2 70.1 %collective-permute-start.14 = (f32[8,2,32,896]{3,2,1,0:T(8,128)}, f32[8,2,32,896]{3,2,1,0:T(8,128)}, u32[]{:S(2)}, u32[]{:S(2)}) collective-permute-start(f32[8,2,32,896]{3,2,1,0:T(8,128)} %get-tuple-element.153), channel_id=1, source_target_pairs={{0,2},{1,3},{8,10},{9,11},{16,18},{17,19},{24,26},{25,27}} | collective-permute-start | bytes 5505032 | tf_op jit(solution)/shard_map/ppermute | solution.py:245
  311.4 41.8 %copy-start.7 = (f32[4,2,32,896]{3,2,1,0:T(8,128)}, f32[4,2,32,896]{3,2,1,0:T(8,128)S(1)}, u32[]{:S(2)}) copy-start(f32[4,2,32,896]{3,2,1,0:T(8,128)S(1)} %slice_add_fusion.6) | copy-start | bytes 2752516
  311.4 58.2 %collective-permute-start.26 = (f32[4,2,32,896]{3,2,1,0:T(8,128)S(1)}, f32[4,2,32,896]{3,2,1,0:T(8,128)}, u32[]{:S(2)}, u32[]{:S(2)}) collective-permute-start(f32[4,2,32,896]{3,2,1,0:T(8,128)S(1)} %slice_add_fusion.6), channel_id=1, source_target_pairs={{4,2},{5,3},{12,10},{13,11},{20,18},{21,19},{28,26},{29,27}} | collective-permute-start | bytes 2752520 | tf_op jit(solution)/shard_map/ppermute | solution.py:245
  339.5 15.8 %collective-permute-start.27 = (f32[4,2,32,384]{3,2,1,0:T(8,128)S(1)}, f32[4,2,32,384]{3,2,1,0:T(8,128)}, u32[]{:S(2)}, u32[]{:S(2)}) collective-permute-start(f32[4,2,32,384]{3,2,1,0:T(8,128)S(1)} %slice_add_fusion.20), channel_id=1, source_target_pairs={{2,4},{3,5},{10,12},{11,13},{18,20},{19,21},{26,28},{27,29}} | collective-permute-start | bytes 1179656 | tf_op jit(solution)/shard_map/ppermute | solution.py:245
  353.2 9.6 %copy-start.2 = (f32[64,4096]{1,0:T(8,128)}, f32[64,4096]{1,0:T(8,128)S(1)}, u32[]{:S(2)}) copy-start(f32[64,4096]{1,0:T(8,128)S(1)} %collective-permute-done.36.refs_5_) | copy-start | bytes 3145732
  353.2 65.2 %collective-permute-start.22 = (f32[8,2,32,1152]{3,2,1,0:T(8,128)}, f32[8,2,32,1152]{3,2,1,0:T(8,128)}, u32[]{:S(2)}, u32[]{:S(2)}) collective-permute-start(f32[8,2,32,1152]{3,2,1,0:T(8,128)} %get-tuple-element.165), channel_id=1, source_target_pairs={{6,4},{7,5},{14,12},{15,13},{22,20},{23,21},{30,28},{31,29}} | collective-permute-start | bytes 7077896 | tf_op jit(solution)/shard_map/ppermute | solution.py:245
  355.3 60.9 %collective-permute-start.23 = (f32[8,2,32,896]{3,2,1,0:T(8,128)}, f32[8,2,32,896]{3,2,1,0:T(8,128)}, u32[]{:S(2)}, u32[]{:S(2)}) collective-permute-start(f32[8,2,32,896]{3,2,1,0:T(8,128)} %get-tuple-element.163), channel_id=1, source_target_pairs={{0,2},{1,3},{8,10},{9,11},{16,18},{17,19},{24,26},{25,27}} | collective-permute-start | bytes 5505032 | tf_op jit(solution)/shard_map/ppermute | solution.py:245
  362.7 11.2 %copy-start.8 = (f32[4,2,32,896]{3,2,1,0:T(8,128)S(1)}, f32[4,2,32,896]{3,2,1,0:T(8,128)}, u32[]{:S(2)}) copy-start(f32[4,2,32,896]{3,2,1,0:T(8,128)} %copy-done.7) | copy-start | bytes 2752516
  369.6 27.8 %collective-permute-start.37 = (f32[4,2,32,1280]{3,2,1,0:T(8,128)}, f32[4,2,32,1280]{3,2,1,0:T(8,128)}, u32[]{:S(2)}, u32[]{:S(2)}) collective-permute-start(f32[4,2,32,1280]{3,2,1,0:T(8,128)} %legendre_sent.11), channel_id=1, source_target_pairs={{0,1},{1,0},{2,3},{3,2},{4,5},{5,4},{6,7},{7,6},{8,9},{9,8},{10,11... | collective-permute-start | bytes 3932168 | tf_op jit(solution)/shard_map/ppermute | solution.py:356
  371.2 8.5 %copy-start.12 = (f32[8,2,32,1152]{3,2,1,0:T(8,128)S(1)}, f32[8,2,32,1152]{3,2,1,0:T(8,128)}, u32[]{:S(2)}) copy-start(f32[8,2,32,1152]{3,2,1,0:T(8,128)} %get-tuple-element.155) | copy-start | bytes 7077892
  372.3 35.1 %collective-permute-start.24 = (f32[64,4096]{1,0:T(8,128)}, f32[64,4096]{1,0:T(8,128)S(1)}, u32[]{:S(2)}, u32[]{:S(2)}) collective-permute-start(f32[64,4096]{1,0:T(8,128)} %get-tuple-element.129), channel_id=1, source_target_pairs={{0,16},{8,24},{16,0},{24,8},{1,17},{9,25},{17,1},{25,9},{2,18},{10... | collective-permute-start | bytes 3145736 | tf_op jit(solution)/shard_map/ppermute | solution.py:305
  378.2 44.1 %collective-permute-start.15 = (f32[8,2,32,384]{3,2,1,0:T(8,128)}, f32[8,2,32,384]{3,2,1,0:T(8,128)}, u32[]{:S(2)}, u32[]{:S(2)}) collective-permute-start(f32[8,2,32,384]{3,2,1,0:T(8,128)} %slice_add_fusion.9), channel_id=1, source_target_pairs={{2,4},{3,5},{10,12},{11,13},{18,20},{19,21},{26,28},{27,29}} | collective-permute-start | bytes 2359304 | tf_op jit(solution)/shard_map/ppermute | solution.py:245
  405.1 19.8 %collective-permute-start.40 = (f32[4,2,32,896]{3,2,1,0:T(8,128)}, f32[4,2,32,896]{3,2,1,0:T(8,128)}, u32[]{:S(2)}, u32[]{:S(2)}) collective-permute-start(f32[4,2,32,896]{3,2,1,0:T(8,128)} %get-tuple-element.179), channel_id=1, source_target_pairs={{0,2},{1,3},{8,10},{9,11},{16,18},{17,19},{24,26},{25,27}} | collective-permute-start | bytes 2752520 | tf_op jit(solution)/shard_map/ppermute | solution.py:245
  415.3 17.4 %collective-permute-start.13 = (f32[8,2,32,896]{3,2,1,0:T(8,128)S(1)}, f32[8,2,32,896]{3,2,1,0:T(8,128)S(1)}, u32[]{:S(2)}, u32[]{:S(2)}) collective-permute-start(f32[8,2,32,896]{3,2,1,0:T(8,128)S(1)} %slice_add_fusion.1), channel_id=1, source_target_pairs={{4,2},{5,3},{12,10},{13,11},{20,18},{21,19},{28,26},{29,27}} | collective-permute-start | bytes 5505032 | tf_op jit(solution)/shard_map/ppermute | solution.py:245
  416.2 12.8 %collective-permute-start.38 = (f32[4,2,32,1152]{3,2,1,0:T(8,128)}, f32[4,2,32,1152]{3,2,1,0:T(8,128)S(1)}, u32[]{:S(2)}, u32[]{:S(2)}) collective-permute-start(f32[4,2,32,1152]{3,2,1,0:T(8,128)} %get-tuple-element.181), channel_id=1, source_target_pairs={{6,4},{7,5},{14,12},{15,13},{22,20},{23,21},{30,28},{31,29}} | collective-permute-start | bytes 3538952 | tf_op jit(solution)/shard_map/ppermute | solution.py:245
  418.4 9.1 %collective-permute-start.33 = (f32[8,2,32,384]{3,2,1,0:T(8,128)S(1)}, f32[8,2,32,384]{3,2,1,0:T(8,128)S(1)}, u32[]{:S(2)}, u32[]{:S(2)}) collective-permute-start(f32[8,2,32,384]{3,2,1,0:T(8,128)S(1)} %slice_add_fusion.8), channel_id=1, source_target_pairs={{2,4},{3,5},{10,12},{11,13},{18,20},{19,21},{26,28},{27,29}} | collective-permute-start | bytes 2359304 | tf_op jit(solution)/shard_map/ppermute | solution.py:245
  422.3 8.0 %copy-start.26 = (f32[4,2,32,1152]{3,2,1,0:T(8,128)S(1)}, f32[4,2,32,1152]{3,2,1,0:T(8,128)}, u32[]{:S(2)}) copy-start(f32[4,2,32,1152]{3,2,1,0:T(8,128)} %get-tuple-element.181) | copy-start | bytes 3538948
  422.3 39.8 %collective-permute-start.8 = (f32[4,2,32,128]{3,2,1,0:T(8,128)S(1)}, f32[4,2,32,128]{3,2,1,0:T(8,128)S(1)}, u32[]{:S(2)}, u32[]{:S(2)}) collective-permute-start(f32[4,2,32,128]{3,2,1,0:T(8,128)S(1)} %slice_add_fusion.37), channel_id=1, source_target_pairs={{4,6},{5,7},{12,14},{13,15},{20,22},{21,23},{28,30},{29,31}} | collective-permute-start | bytes 393224 | tf_op jit(solution)/shard_map/ppermute | solution.py:245
  424.9 26.6 %collective-permute-start.25 = (f32[4,2,32,1280]{3,2,1,0:T(8,128)S(1)}, f32[4,2,32,1280]{3,2,1,0:T(8,128)S(1)}, u32[]{:S(2)}, u32[]{:S(2)}) collective-permute-start(f32[4,2,32,1280]{3,2,1,0:T(8,128)S(1)} %copy-done.21), channel_id=1, source_target_pairs={{0,1},{1,0},{2,3},{3,2},{4,5},{5,4},{6,7},{7,6},{8,9},{9,8},{10,11... | collective-permute-start | bytes 3932168 | tf_op jit(solution)/shard_map/ppermute | solution.py:356
  427.5 3.8 collective-permute-start.41
  429.0 34.6 %collective-permute-start.7 = (f32[4,2,32,512]{3,2,1,0:T(8,128)}, f32[4,2,32,512]{3,2,1,0:T(8,128)}, u32[]{:S(2)}, u32[]{:S(2)}) collective-permute-start(f32[4,2,32,512]{3,2,1,0:T(8,128)} %slice_add_fusion.15), channel_id=1, source_target_pairs={{2,0},{3,1},{10,8},{11,9},{18,16},{19,17},{26,24},{27,25}} | collective-permute-start | bytes 1572872 | tf_op jit(solution)/shard_map/ppermute | solution.py:245
  431.3 20.2 %copy-start.36 = (f32[4,2,32,384]{3,2,1,0:T(8,128)}, f32[4,2,32,384]{3,2,1,0:T(8,128)S(1)}, u32[]{:S(2)}) copy-start(f32[4,2,32,384]{3,2,1,0:T(8,128)S(1)} %collective-permute-done.41) | copy-start | bytes 1179652
  431.4 35.2 %collective-permute-start.28 = (f32[4,2,32,512]{3,2,1,0:T(8,128)}, f32[4,2,32,512]{3,2,1,0:T(8,128)}, u32[]{:S(2)}, u32[]{:S(2)}) collective-permute-start(f32[4,2,32,512]{3,2,1,0:T(8,128)} %slice_add_fusion.14), channel_id=1, source_target_pairs={{2,0},{3,1},{10,8},{11,9},{18,16},{19,17},{26,24},{27,25}} | collective-permute-start | bytes 1572872 | tf_op jit(solution)/shard_map/ppermute | solution.py:245
  432.7 32.3 %collective-permute-start.29 = (f32[4,2,32,128]{3,2,1,0:T(8,128)S(1)}, f32[4,2,32,128]{3,2,1,0:T(8,128)}, u32[]{:S(2)}, u32[]{:S(2)}) collective-permute-start(f32[4,2,32,128]{3,2,1,0:T(8,128)S(1)} %slice_add_fusion.36), channel_id=1, source_target_pairs={{4,6},{5,7},{12,14},{13,15},{20,22},{21,23},{28,30},{29,31}} | collective-permute-start | bytes 393224 | tf_op jit(solution)/shard_map/ppermute | solution.py:245
  452.6 40.0 %collective-permute-start.32 = (f32[8,2,32,896]{3,2,1,0:T(8,128)}, f32[8,2,32,896]{3,2,1,0:T(8,128)}, u32[]{:S(2)}, u32[]{:S(2)}) collective-permute-start(f32[8,2,32,896]{3,2,1,0:T(8,128)} %slice_add_fusion), channel_id=1, source_target_pairs={{4,2},{5,3},{12,10},{13,11},{20,18},{21,19},{28,26},{29,27}} | collective-permute-start | bytes 5505032 | tf_op jit(solution)/shard_map/ppermute | solution.py:245
  462.1 94.7 %collective-permute-start.31 = (f32[8,2,32,128]{3,2,1,0:T(8,128)}, f32[8,2,32,128]{3,2,1,0:T(8,128)}, u32[]{:S(2)}, u32[]{:S(2)}) collective-permute-start(f32[8,2,32,128]{3,2,1,0:T(8,128)} %slice_add_fusion.27), channel_id=1, source_target_pairs={{4,6},{5,7},{12,14},{13,15},{20,22},{21,23},{28,30},{29,31}} | collective-permute-start | bytes 786440 | tf_op jit(solution)/shard_map/ppermute | solution.py:245
  463.6 95.7 %collective-permute-start.35 = (f32[8,2,32,128]{3,2,1,0:T(8,128)}, f32[8,2,32,128]{3,2,1,0:T(8,128)}, u32[]{:S(2)}, u32[]{:S(2)}) collective-permute-start(f32[8,2,32,128]{3,2,1,0:T(8,128)} %slice_add_fusion.26), channel_id=1, source_target_pairs={{4,6},{5,7},{12,14},{13,15},{20,22},{21,23},{28,30},{29,31}} | collective-permute-start | bytes 786440 | tf_op jit(solution)/shard_map/ppermute | solution.py:245
  465.0 24.8 %collective-permute-start.39 = (f32[4,2,32,896]{3,2,1,0:T(8,128)}, f32[4,2,32,896]{3,2,1,0:T(8,128)}, u32[]{:S(2)}, u32[]{:S(2)}) collective-permute-start(f32[4,2,32,896]{3,2,1,0:T(8,128)} %slice_add_fusion.5), channel_id=1, source_target_pairs={{4,2},{5,3},{12,10},{13,11},{20,18},{21,19},{28,26},{29,27}} | collective-permute-start | bytes 2752520 | tf_op jit(solution)/shard_map/ppermute | solution.py:245
  466.6 31.5 %collective-permute-start.43 = (f32[4,2,32,128]{3,2,1,0:T(8,128)S(1)}, f32[4,2,32,128]{3,2,1,0:T(8,128)}, u32[]{:S(2)}, u32[]{:S(2)}) collective-permute-start(f32[4,2,32,128]{3,2,1,0:T(8,128)S(1)} %slice_add_fusion.35), channel_id=1, source_target_pairs={{4,6},{5,7},{12,14},{13,15},{20,22},{21,23},{28,30},{29,31}} | collective-permute-start | bytes 393224 | tf_op jit(solution)/shard_map/ppermute | solution.py:245
  489.8 68.4 %collective-permute-start.30 = (f32[8,2,32,512]{3,2,1,0:T(8,128)S(1)}, f32[8,2,32,512]{3,2,1,0:T(8,128)}, u32[]{:S(2)}, u32[]{:S(2)}) collective-permute-start(f32[8,2,32,512]{3,2,1,0:T(8,128)S(1)} %slice_add_fusion.3), channel_id=1, source_target_pairs={{2,0},{3,1},{10,8},{11,9},{18,16},{19,17},{26,24},{27,25}} | collective-permute-start | bytes 3145736 | tf_op jit(solution)/shard_map/ppermute | solution.py:245
  492.6 55.0 %copy-start.37 = (f32[4,2,32,384]{3,2,1,0:T(8,128)S(1)}, f32[4,2,32,384]{3,2,1,0:T(8,128)}, u32[]{:S(2)}) copy-start(f32[4,2,32,384]{3,2,1,0:T(8,128)} %copy-done.36) | copy-start | bytes 1179652
  492.6 53.7 %collective-permute-start.42 = (f32[4,2,32,512]{3,2,1,0:T(8,128)S(1)}, f32[4,2,32,512]{3,2,1,0:T(8,128)S(1)}, u32[]{:S(2)}, u32[]{:S(2)}) collective-permute-start(f32[4,2,32,512]{3,2,1,0:T(8,128)S(1)} %slice_add_fusion.13), channel_id=1, source_target_pairs={{2,0},{3,1},{10,8},{11,9},{18,16},{19,17},{26,24},{27,25}} | collective-permute-start | bytes 1572872 | tf_op jit(solution)/shard_map/ppermute | solution.py:245
  498.1 56.0 %collective-permute-start.46 = (f32[4,2,32,896]{3,2,1,0:T(8,128)}, f32[4,2,32,896]{3,2,1,0:T(8,128)}, u32[]{:S(2)}, u32[]{:S(2)}) collective-permute-start(f32[4,2,32,896]{3,2,1,0:T(8,128)} %get-tuple-element.189), channel_id=1, source_target_pairs={{0,2},{1,3},{8,10},{9,11},{16,18},{17,19},{24,26},{25,27}} | collective-permute-start | bytes 2752520 | tf_op jit(solution)/shard_map/ppermute | solution.py:245
  546.3 21.3 %collective-permute-start.34 = (f32[8,2,32,512]{3,2,1,0:T(8,128)}, f32[8,2,32,512]{3,2,1,0:T(8,128)}, u32[]{:S(2)}, u32[]{:S(2)}) collective-permute-start(f32[8,2,32,512]{3,2,1,0:T(8,128)} %slice_add_fusion.2), channel_id=1, source_target_pairs={{2,0},{3,1},{10,8},{11,9},{18,16},{19,17},{26,24},{27,25}} | collective-permute-start | bytes 3145736 | tf_op jit(solution)/shard_map/ppermute | solution.py:245
  554.0 15.1 %copy-start.30 = (f32[8,2,32,384]{3,2,1,0:T(8,128)S(1)}, f32[8,2,32,384]{3,2,1,0:T(8,128)}, u32[]{:S(2)}) copy-start(f32[8,2,32,384]{3,2,1,0:T(8,128)} %copy-done.29) | copy-start | bytes 2359300
  554.0 21.4 %collective-permute-start.44 = (f32[4,2,32,1152]{3,2,1,0:T(8,128)}, f32[4,2,32,1152]{3,2,1,0:T(8,128)S(1)}, u32[]{:S(2)}, u32[]{:S(2)}) collective-permute-start(f32[4,2,32,1152]{3,2,1,0:T(8,128)} %get-tuple-element.191), channel_id=1, source_target_pairs={{6,4},{7,5},{14,12},{15,13},{22,20},{23,21},{30,28},{31,29}} | collective-permute-start | bytes 3538952 | tf_op jit(solution)/shard_map/ppermute | solution.py:245
  556.8 34.0 %collective-permute-start.47 = (f32[4,2,32,384]{3,2,1,0:T(8,128)}, f32[4,2,32,384]{3,2,1,0:T(8,128)}, u32[]{:S(2)}, u32[]{:S(2)}) collective-permute-start(f32[4,2,32,384]{3,2,1,0:T(8,128)} %slice_add_fusion.18), channel_id=1, source_target_pairs={{2,4},{3,5},{10,12},{11,13},{18,20},{19,21},{26,28},{27,29}} | collective-permute-start | bytes 1179656 | tf_op jit(solution)/shard_map/ppermute | solution.py:245
  576.4 9.7 %collective-permute-start.45 = (f32[4,2,32,896]{3,2,1,0:T(8,128)}, f32[4,2,32,896]{3,2,1,0:T(8,128)}, u32[]{:S(2)}, u32[]{:S(2)}) collective-permute-start(f32[4,2,32,896]{3,2,1,0:T(8,128)} %slice_add_fusion.4), channel_id=1, source_target_pairs={{4,2},{5,3},{12,10},{13,11},{20,18},{21,19},{28,26},{29,27}} | collective-permute-start | bytes 2752520 | tf_op jit(solution)/shard_map/ppermute | solution.py:245
  587.5 15.8 %collective-permute-start.48 = (f32[4,2,32,512]{3,2,1,0:T(8,128)S(1)}, f32[4,2,32,512]{3,2,1,0:T(8,128)S(1)}, u32[]{:S(2)}, u32[]{:S(2)}) collective-permute-start(f32[4,2,32,512]{3,2,1,0:T(8,128)S(1)} %slice_add_fusion.12), channel_id=1, source_target_pairs={{2,0},{3,1},{10,8},{11,9},{18,16},{19,17},{26,24},{27,25}} | collective-permute-start | bytes 1572872 | tf_op jit(solution)/shard_map/ppermute | solution.py:245
  591.8 2.0 collective-permute-start.49
  (45 other events, 158.3 us)

commit v4 on v3

--- a/solution.py
+++ b/solution.py
@@ -335,17 +335,7 @@
                 bit //= 2
             pieces.append((place, count, near, lon_swap(far, bit)))
 
-    def finish(count, place, mine):
-        mine = mine.reshape(count, 2, 2, 8, levels, half_degrees).transpose(0, 3, 4, 2, 1, 5)
-        wavenumber = lon + lon_count * (lat * own + place + lax.iota(jnp.int32, count))
-        degree = (
-            2 * lax.iota(jnp.int32, half_degrees)[None, None, :]
-            + lax.iota(jnp.int32, 2)[None, :, None]
-        )
-        inside = wavenumber[:, None, None] + degree < waves
-        return jnp.where(inside[:, None, None, None, :, :], mine, jnp.zeros((), jnp.float32))
-
-    result = jnp.zeros((own, 8, levels, 2, 2, half_degrees), jnp.float32)
+    result = None
     given, chains, kept = [None] * len(pieces), [], []
 
     def send(k):
@@ -378,8 +368,9 @@
         ends.append(state)
     for k, end in enumerate(ends):
         place, count = pieces[k][:2]
-        mine = finish(count, place, close(*end, zone, plan, half_degrees, kept[-1]))
-        result = lax.dynamic_update_slice(result, mine, (place,) + (0,) * 5)
+        base = lon + lon_count * (lat * own + place)
+        shape = (own, 8, levels, 2, 2, half_degrees)
+        result = close(end, kept[-1], zone, base, lon_count, waves, plan, place, shape, result)
     return result[None]
 
 
@@ -398,25 +389,91 @@
     yield downs, ups, came_down, came_up
 
 
-def close(downs, ups, came_down, came_up, zone, plan, half_degrees, last):
+def close_kernel(zones, tiles, stride, waves, fresh, zone_ref, base_ref, *refs):
+    refs = refs if fresh else refs[1:]
+    hops = zones - 1
+    downs, came_down = refs[:hops], refs[hops : 2 * hops]
+    up, came_up = refs[2 * hops], refs[2 * hops + 1 : 3 * hops + 1]
+    out_ref, total = refs[-2:]
+    tile = pl.program_id(0)
+    for z in range(zones):
+        @pl.when((zone_ref[0] == z) & (tile < tiles[z]))
+        def _():
+            if z == hops:
+                value = up[...]
+            else:
+                value = downs[hops - 1 - z][...] + came_down[hops - 1 - z][...]
+            if z > 0:
+                value = value + came_up[z - 1][...]
+            total[...] = value
+
+        @pl.when((zone_ref[0] == z) & (tile >= tiles[z]))
+        def _():
+            total[...] = jnp.zeros_like(total)
+
+    count, _, rows, width = total.shape
+    batch = rows // 2
+    fields, levels = out_ref.shape[1:3]
+    lane = tile * width + lax.broadcasted_iota(jnp.int32, (batch, width), 1)
+    for r in range(count):
+        for e in range(2):
+            inside = 2 * lane + (base_ref[0] + stride * r + e) < waves
+            for c in range(2):
+                value = total[r, e, c * batch : (c + 1) * batch]
+                value = jnp.where(inside, value, jnp.zeros_like(value))
+                out_ref[r, :, :, c, e, :] = value.reshape(fields, levels, width)
+
+
+def close(end, last, zone, base, stride, waves, plan, place, shape, result):
     widths, places, _ = plan[:3]
     zones = len(widths)
-    downs, ups, came_down, came_up, _ = lax.optimization_barrier(
-        (downs, ups, came_down, came_up, last)
-    )
-    mine = None
-    for z in range(zones):
-        width = widths[z]
-        if z == zones - 1:
-            value = ups[0][..., :width]
-        else:
-            k = zones - 2 - z
-            value = downs[k][..., :width] + came_down[k][..., :width]
-        if z > 0:
-            value = value + came_up[z - 1][..., places[z] : places[z] + width]
-        value = jnp.pad(value, ((0, 0), (0, 0), (0, 0), (0, half_degrees - width)))
-        mine = value if mine is None else jnp.where(zone == z, value, mine)
-    return mine
+    hops = zones - 1
+    downs, ups, came_down, came_up, _ = lax.optimization_barrier((*end, last))
+    arrays = [*downs, *came_down, ups[0], *came_up]
+    users = [hops - 1 - k for k in range(hops)] * 2 + [hops] + [k + 1 for k in range(hops)]
+    starts = [0] * (2 * hops + 1) + [places[k + 1] // LANES for k in range(hops)]
+    count, _, rows, _ = arrays[0].shape
+
+    def spec(user, start):
+        most = start + widths[user] // LANES - 1
+
+        def index(tile, zone_ref, base_ref):
+            return (0, 0, 0, jnp.where(zone_ref[0] == user, jnp.minimum(start + tile, most), 0))
+
+        return pl.BlockSpec((count, 2, rows, LANES), index)
+
+    in_specs = [spec(user, start) for user, start in zip(users, starts)]
+    scalars = [zone.astype(jnp.int32).reshape(1), base.astype(jnp.int32).reshape(1)]
+    aliases = {}
+    if result is not None:
+        in_specs = [pl.BlockSpec(memory_space=pl.ANY)] + in_specs
+        arrays = [result] + arrays
+        aliases = {2: 0}
+    fresh = result is None
+    tiles = [width // LANES for width in widths]
+
+    def kernel(*refs):
+        close_kernel(zones, tiles, stride, waves, fresh, *refs)
+
+    block = (count,) + shape[1:-1] + (LANES,)
+    return pl.pallas_call(
+        kernel,
+        grid_spec=pltpu.PrefetchScalarGridSpec(
+            num_scalar_prefetch=2,
+            grid=(shape[-1] // LANES,),
+            in_specs=in_specs,
+            out_specs=pl.BlockSpec(block, lambda tile, *_: (place // count, 0, 0, 0, 0, tile)),
+            scratch_shapes=[pltpu.VMEM((count, 2, rows, LANES), jnp.float32)],
+        ),
+        out_shape=jax.ShapeDtypeStruct(shape, jnp.float32),
+        input_output_aliases=aliases,
+        cost_estimate=pl.CostEstimate(
+            flops=count * 2 * rows * shape[-1],
+            bytes_accessed=16 * count * 2 * rows * shape[-1],
+            transcendentals=0,
+        ),
+        name="close",
+    )(*scalars, *arrays)
 
 
 def solution(mesh):

time: 616 us -> 581 us (0.943)
  other arithmetic: 95.6 us -> 51.6 us
  Pallas kernels: 188 us -> 214 us
  local copies, waits for them, and re-layouts: 26.3 us -> 13.3 us
  starting transfers between devices: 111 us -> 104 us
    pallas_call x0 -> x6, Pallas kernels: none -> 26.1 us  [close(): pl.pallas_call(kernel, grid_spec=pltpu.PrefetchScalarGridSpec(num_scalar_...]
    ppermute x8, waiting for transfers between devices: 55.5 us -> 32.1 us  [lon_swap(): return lax.ppermute(value, 'lon', [(i, i ^ bit) for i in range(lon_count)])]
    add x22 -> x0, other arithmetic: 23.3 us -> none  [the longest x18 23.3 us: close(): value = value + came_up[z - 1][..., places[z]:places[z] + width]]
    ppermute x36, waiting for transfers between devices: 54.2 us -> 74.5 us  [hop(): return lax.ppermute(value, 'lat', pairs)]
    select_n x7 -> x0, other arithmetic: 11.6 us -> none  [the longest x6 10.1 us: close(): mine = value if mine is None else jnp.where(zone == z, value, mine)]
    ppermute x6, waiting for transfers between devices: 77.5 us -> 86.9 us  [send(): lax.ppermute(value, 'lat', [(i, i ^ 1) for i in range(lat_count)])]
    reshape x6 -> x0, local copies, waits for them, and re-layouts: 8.01 us -> none  [finish(): mine.reshape(count, 2, 2, 8, levels, half_degrees)]
    dynamic_update_slice x5 -> x0, other arithmetic: 7.88 us -> none  [local(): result = lax.dynamic_update_slice(result, mine, (place,) + (0,) * 5)]
  transfers between devices with their start and end apart: 50 -> 50, of which waited for: 11 -> 12; matrix products, arithmetic and copies ran while one was open for 15% -> 7% of each run, Pallas kernels for 25% -> 30%
where the time goes in v4:
time: 581 us; the launch traced here: 577 us
  Pallas kernels  214 us (37%)
  waiting for transfers between devices  193 us (33%)
  starting transfers between devices  104 us (18%)
  other arithmetic  51.6 us (9%)
  local copies, waits for them, and re-layouts  13.3 us (2%)
    pallas_call x12, Pallas kernels, project(): pl.pallas_call(kernel, grid_spec=pltpu.PrefetchScalarGridSpec(num_scalar_...  95.6 us
    ppermute x6, waiting for transfers between devices, send(): lax.ppermute(value, 'lat', [(i, i ^ 1) for i in range(lat_count)])  86.9 us
    ppermute x36, starting transfers between devices, hop(): return lax.ppermute(value, 'lat', pairs)  85.3 us
    ppermute x36, waiting for transfers between devices, hop(): return lax.ppermute(value, 'lat', pairs)  74.5 us
    pallas_call x2, Pallas kernels, fourier(): pl.pallas_call(second_fourier_kernel, grid=(rows // block,), in_specs=[wh...  39.2 us
    pallas_call x2, Pallas kernels, fourier(): pl.pallas_call(first_fourier_kernel, grid=(rows // block,), in_specs=[who...  36.7 us
    ppermute x8, waiting for transfers between devices, lon_swap(): return lax.ppermute(value, 'lon', [(i, i ^ bit) for i in range(lon_count)])  32.1 us
    pallas_call x6, Pallas kernels, close(): pl.pallas_call(kernel, grid_spec=pltpu.PrefetchScalarGridSpec(num_scalar_...  26.1 us
  transfers between devices with their start and end apart: 50, of which 12 were waited for; matrix products, arithmetic and copies ran while one was open for 7% of the time, Pallas kernels for 30%

profile of v4, /device:TPU:0, one launch (start us, length us, event | category | flops | bytes accessed | tf_op | source)
XLA Modules:
  0.0 577.4 jit_solution(6749631773664781097)
XLA Ops:
  0.2 2.1 sine_multiply_fusion
  7.4 16.0 %tendencies.1 = (bf16[8,2,256,1024]{3,2,1,0:T(8,128)(2,1)}, bf16[8,2,256,1024]{3,2,1,0:T(8,128)(2,1)}) custom-call(bf16[12,2,2,128,1024]{4,3,2,1,0:T(8,128)(2,1)} %grid_ref.1), custom_call_target="tpu_custom_call" | custom-call | flops 25165824 | bytes 31457280 | tf_op jit(solution)/shard_map/tendencies/pallas_call | solution.py:56
  26.0 1.9 constant_dynamic-update-slice_fusion.6
  31.7 1.8 fusion.2
  33.5 18.2 %fourier_first.2 = f32[512,4096]{1,0:T(8,128)} custom-call(bf16[512,1024]{1,0:T(8,128)(2,1)} %get-tuple-element.202.ph_ref, bf16[512,1024]{1,0:T(8,128)(2,1)} %get-tuple-element.201.pl_ref, bf16[4096,1024]{1,0:T(8,128)(2,1)} %bitcast.160, bf16[4096,1024]{1,0:T(8,128)(2,1)} %bitcast.164), custom_call_target="tpu_custom_call" | custom-call | flops 12884901888 | bytes 25165824 | tf_op jit(solution)/shard_map/fourier_first/pallas_call | solution.py:111
  53.1 1.8 fusion.1
  54.9 18.4 %fourier_first.3 = f32[512,4096]{1,0:T(8,128)} custom-call(bf16[512,1024]{1,0:T(8,128)(2,1)} %get-tuple-element.204.ph_ref, bf16[512,1024]{1,0:T(8,128)(2,1)} %get-tuple-element.203.pl_ref, bf16[4096,1024]{1,0:T(8,128)(2,1)} %bitcast.161, bf16[4096,1024]{1,0:T(8,128)(2,1)} %bitcast.165), custom_call_target="tpu_custom_call" | custom-call | flops 12884901888 | bytes 25165824 | tf_op jit(solution)/shard_map/fourier_first/pallas_call | solution.py:111
  73.4 1.8 fusion
  75.3 19.7 %fourier_second.2 = (f32[64,4096]{1,0:T(8,128)}, f32[64,4096]{1,0:T(8,128)}, f32[128,4096]{1,0:T(8,128)}, f32[64,4096]{1,0:T(8,128)}, f32[64,4096]{1,0:T(8,128)}, /*index=5*/f32[128,4096]{1,0:T(8,128)}) custom-call(bf16[512,1024]{1,0:T(8,128)(2,1)} %get-tuple-element.206.ph_ref, bf16[512,1024]{1,0:T(8,128)(2,1)} %get-tuple-element.205.pl_ref, ...), custom_call_target="tpu_custom_call" | custom-call | flops 12884901888 | bytes 25165824 | tf_op jit(solution)/shard_map/fourier_second/pallas_call | solution.py:120
  94.9 3.0 collective-permute-start.1
  98.0 1.8 fusion.3
  99.8 1.9 collective-permute-start.16
  101.8 20.3 %collective-permute-done.1.refs_5_ = f32[64,4096]{1,0:T(8,128)S(1)} collective-permute-done((f32[64,4096]{1,0:T(8,128)}, f32[64,4096]{1,0:T(8,128)S(1)}, u32[]{:S(2)}, u32[]{:S(2)}) %collective-permute-start.1) | collective-permute-done | bytes 1048608 | tf_op jit(solution)/shard_map/ppermute | solution.py:305
  123.1 6.7 %legendre_sent.6 = f32[4,2,32,1280]{3,2,1,0:T(8,128)} custom-call(s32[1]{0:T(128)} %bitcast.68.refs_0_, s32[6]{0:T(128)} %constant.87.clone.refs_1_, s32[6]{0:T(128)} %constant.88.clone.refs_2_, s32[6]{0:T(128)} %constant.89.clone.refs_3_, f32[64,4096]{1,0:T(8,128)} %get-tuple-element.106.refs_4_, f32[64,4096]{1,0:T(8,128)} %copy-done.9, ...), custom_call_target="tpu_custom_call" | custom-call | flops 201326592 | bytes 3801088 | tf_op jit(solution)/shard_map/legendre_sent/pallas_call | solution.py:222
  129.9 2.0 collective-permute-start.2
  131.9 19.5 %fourier_second.3 = (f32[128,4096]{1,0:T(8,128)}, f32[64,4096]{1,0:T(8,128)}, f32[64,4096]{1,0:T(8,128)}, f32[128,4096]{1,0:T(8,128)}, f32[64,4096]{1,0:T(8,128)}, /*index=5*/f32[64,4096]{1,0:T(8,128)}) custom-call(bf16[512,1024]{1,0:T(8,128)(2,1)} %get-tuple-element.200.ph_ref, bf16[512,1024]{1,0:T(8,128)(2,1)} %get-tuple-element.199.pl_ref, ...), custom_call_target="tpu_custom_call" | custom-call | flops 12884901888 | bytes 25165824 | tf_op jit(solution)/shard_map/fourier_second/pallas_call | solution.py:120
  152.9 6.7 %collective-permute-done.2.refs_7_ = f32[4,2,32,1280]{3,2,1,0:T(8,128)} collective-permute-done((f32[4,2,32,1280]{3,2,1,0:T(8,128)}, f32[4,2,32,1280]{3,2,1,0:T(8,128)}, u32[]{:S(2)}, u32[]{:S(2)}) %collective-permute-start.2) | collective-permute-done | bytes 1310752 | tf_op jit(solution)/shard_map/ppermute | solution.py:346
  159.6 7.6 %legendre_kept.6 = (f32[4,2,32,1152]{3,2,1,0:T(8,128)}, f32[4,2,32,896]{3,2,1,0:T(8,128)}) custom-call(s32[1]{0:T(128)} %bitcast.7.refs_0_, s32[6]{0:T(128)} %constant.87.clone.refs_1_, s32[6]{0:T(128)} %constant.88.clone.refs_2_, s32[6]{0:T(128)} %constant.89.clone.refs_3_, f32[64,4096]{1,0:T(8,128)} %get-tuple-element.106.refs_4_, f32[64,4096]{1,0:T(8,128)} %copy-done.9, ...), custom_call_target="tpu_custom_call" | custom-call | flops 201326592 | bytes 3801088 | tf_op jit(solution)/shard_map/legendre_kept/pallas_call | solution.py:222
  167.2 8.7 %legendre_sent.7 = f32[8,2,32,1280]{3,2,1,0:T(8,128)} custom-call(s32[1]{0:T(128)} %bitcast.68.refs_0_, s32[6]{0:T(128)} %constant.87.clone.refs_1_, s32[6]{0:T(128)} %constant.88.clone.refs_2_, s32[6]{0:T(128)} %constant.89.clone.refs_3_, f32[128,4096]{1,0:T(8,128)} %get-tuple-element.115.refs_4_, f32[128,4096]{1,0:T(8,128)} %collective-permute-done.10.refs_5_, ...), custom_call_target="tpu_custom_call" | custom-call | flops 402653184 | bytes 7602176 | tf_op jit(solution)/shard_map/legendre_sent/pallas_call | solution.py:222
  175.9 1.9 collective-permute-start.11
  177.8 11.7 %collective-permute-done.16.refs_5_ = f32[64,4096]{1,0:T(8,128)S(1)} collective-permute-done((f32[64,4096]{1,0:T(8,128)}, f32[64,4096]{1,0:T(8,128)S(1)}, u32[]{:S(2)}, u32[]{:S(2)}) %collective-permute-start.16) | collective-permute-done | bytes 1048608 | tf_op jit(solution)/shard_map/ppermute | solution.py:305
  190.5 6.8 %legendre_sent.8 = f32[4,2,32,1280]{3,2,1,0:T(8,128)} custom-call(s32[1]{0:T(128)} %bitcast.68.refs_0_, s32[6]{0:T(128)} %constant.87.clone.refs_1_, s32[6]{0:T(128)} %constant.88.clone.refs_2_, s32[6]{0:T(128)} %constant.89.clone.refs_3_, f32[64,4096]{1,0:T(8,128)} %get-tuple-element.119.refs_4_, f32[64,4096]{1,0:T(8,128)} %copy-done.8, ...), custom_call_target="tpu_custom_call" | custom-call | flops 201326592 | bytes 3801088 | tf_op jit(solution)/shard_map/legendre_sent/pallas_call | solution.py:222
  197.3 2.0 collective-permute-start.17
  201.0 3.5 collective-permute-start.5
  204.5 57.3 %collective-permute-done.17.refs_7_ = f32[4,2,32,1280]{3,2,1,0:T(8,128)} collective-permute-done((f32[4,2,32,1280]{3,2,1,0:T(8,128)}, f32[4,2,32,1280]{3,2,1,0:T(8,128)}, u32[]{:S(2)}, u32[]{:S(2)}) %collective-permute-start.17) | collective-permute-done | bytes 1310752 | tf_op jit(solution)/shard_map/ppermute | solution.py:346
  261.8 7.8 %legendre_kept.8 = (f32[4,2,32,1152]{3,2,1,0:T(8,128)}, f32[4,2,32,896]{3,2,1,0:T(8,128)}) custom-call(s32[1]{0:T(128)} %bitcast.7.refs_0_, s32[6]{0:T(128)} %constant.87.clone.refs_1_, s32[6]{0:T(128)} %constant.88.clone.refs_2_, s32[6]{0:T(128)} %constant.89.clone.refs_3_, f32[64,4096]{1,0:T(8,128)} %get-tuple-element.119.refs_4_, f32[64,4096]{1,0:T(8,128)} %copy-done.8, ...), custom_call_target="tpu_custom_call" | custom-call | flops 201326592 | bytes 3801088 | tf_op jit(solution)/shard_map/legendre_kept/pallas_call | solution.py:222
  270.9 8.7 %legendre_sent.9 = f32[8,2,32,1280]{3,2,1,0:T(8,128)} custom-call(s32[1]{0:T(128)} %bitcast.68.refs_0_, s32[6]{0:T(128)} %constant.87.clone.refs_1_, s32[6]{0:T(128)} %constant.88.clone.refs_2_, s32[6]{0:T(128)} %constant.89.clone.refs_3_, f32[128,4096]{1,0:T(8,128)} %get-tuple-element.125.refs_4_, f32[128,4096]{1,0:T(8,128)} %copy-done.1, ...), custom_call_target="tpu_custom_call" | custom-call | flops 402653184 | bytes 7602176 | tf_op jit(solution)/shard_map/legendre_sent/pallas_call | solution.py:222
  282.8 4.4 collective-permute-start.19
  287.2 1.8 slice_add_fusion.17
  290.5 10.2 %legendre_kept.7 = (f32[8,2,32,1152]{3,2,1,0:T(8,128)}, f32[8,2,32,896]{3,2,1,0:T(8,128)}) custom-call(s32[1]{0:T(128)} %bitcast.7.refs_0_, s32[6]{0:T(128)} %constant.87.clone.refs_1_, s32[6]{0:T(128)} %constant.88.clone.refs_2_, s32[6]{0:T(128)} %constant.89.clone.refs_3_, f32[128,4096]{1,0:T(8,128)} %get-tuple-element.115.refs_4_, ...), custom_call_target="tpu_custom_call" | custom-call | flops 402653184 | bytes 7602176 | tf_op jit(solution)/shard_map/legendre_kept/pallas_call | solution.py:222
  305.7 1.9 slice_add_fusion.16
  307.6 6.2 %collective-permute-start.14 = (f32[8,2,32,896]{3,2,1,0:T(8,128)}, f32[8,2,32,896]{3,2,1,0:T(8,128)}, u32[]{:S(2)}, u32[]{:S(2)}) collective-permute-start(f32[8,2,32,896]{3,2,1,0:T(8,128)} %get-tuple-element.159.refs_9_), channel_id=1, source_target_pairs={{0,2},{1,3},{8,10},{9,11},{16,18},{17,19},{24,26},{25,27}} | collective-permute-start | bytes 5505032 | tf_op jit(solution)/shard_map/ppermute | solution.py:245
  313.8 2.5 slice_add_fusion.6.refs_4_
  319.5 17.1 %collective-permute-done.21.refs_7_ = f32[8,2,32,1280]{3,2,1,0:T(8,128)} collective-permute-done((f32[8,2,32,1280]{3,2,1,0:T(8,128)}, f32[8,2,32,1280]{3,2,1,0:T(8,128)}, u32[]{:S(2)}, u32[]{:S(2)}) %collective-permute-start.21) | collective-permute-done | bytes 2621472 | tf_op jit(solution)/shard_map/ppermute | solution.py:346
  336.5 10.4 %legendre_kept.9 = (f32[8,2,32,1152]{3,2,1,0:T(8,128)}, f32[8,2,32,896]{3,2,1,0:T(8,128)}) custom-call(s32[1]{0:T(128)} %bitcast.7.refs_0_, s32[6]{0:T(128)} %constant.87.clone.refs_1_, s32[6]{0:T(128)} %constant.88.clone.refs_2_, s32[6]{0:T(128)} %constant.89.clone.refs_3_, f32[128,4096]{1,0:T(8,128)} %get-tuple-element.125.refs_4_, f32[128,4096]{1,0:T(8,128)} %copy-done.1, ...), custom_call_target="tpu_custom_call" | custom-call | flops 402653184 | bytes 7602176 | tf_op jit(solution)/shard_map/legendre_kept/pallas_call | solution.py:222
  346.9 4.2 collective-permute-start.23
  351.1 2.1 collective-permute-start.22
  357.8 2.3 slice_add_fusion.1.refs_4_
  360.1 2.0 collective-permute-start.13
  362.1 6.7 %legendre_sent.11 = f32[4,2,32,1280]{3,2,1,0:T(8,128)} custom-call(s32[1]{0:T(128)} %bitcast.68.refs_0_, s32[6]{0:T(128)} %constant.87.clone.refs_1_, s32[6]{0:T(128)} %constant.88.clone.refs_2_, s32[6]{0:T(128)} %constant.89.clone.refs_3_, f32[64,4096]{1,0:T(8,128)} %get-tuple-element.176.refs_4_, f32[64,4096]{1,0:T(8,128)} %collective-permute-done.36.refs_5_, ...), custom_call_target="tpu_custom_call" | custom-call | flops 201326592 | bytes 3801088 | tf_op jit(solution)/shard_map/legendre_sent/pallas_call | solution.py:222
  371.9 6.7 %legendre_sent.10 = f32[4,2,32,1280]{3,2,1,0:T(8,128)} custom-call(s32[1]{0:T(128)} %bitcast.68.refs_0_, s32[6]{0:T(128)} %constant.87.clone.refs_1_, s32[6]{0:T(128)} %constant.88.clone.refs_2_, s32[6]{0:T(128)} %constant.89.clone.refs_3_, f32[64,4096]{1,0:T(8,128)} %get-tuple-element.130.refs_4_, f32[64,4096]{1,0:T(8,128)} %collective-permute-done.24.refs_5_, ...), custom_call_target="tpu_custom_call" | custom-call | flops 201326592 | bytes 3801088 | tf_op jit(solution)/shard_map/legendre_sent/pallas_call | solution.py:222
  378.6 2.4 slice_add_fusion.9
  381.6 5.9 %collective-permute-done.23.refs_10_ = f32[8,2,32,896]{3,2,1,0:T(8,128)} collective-permute-done((f32[8,2,32,896]{3,2,1,0:T(8,128)}, f32[8,2,32,896]{3,2,1,0:T(8,128)}, u32[]{:S(2)}, u32[]{:S(2)}) %collective-permute-start.23) | collective-permute-done | bytes 1835040 | tf_op jit(solution)/shard_map/ppermute | solution.py:245
  389.1 1.9 slice_add_fusion.12.refs_5_
  391.1 2.4 slice_add_fusion.8
  393.4 3.0 slice_add_fusion.refs_4_
  396.4 1.9 collective-permute-start.32
  398.4 2.4 collective-permute-done.37.refs_7_
  400.8 7.6 %legendre_kept.11 = (f32[4,2,32,1152]{3,2,1,0:T(8,128)}, f32[4,2,32,896]{3,2,1,0:T(8,128)}) custom-call(s32[1]{0:T(128)} %bitcast.7.refs_0_, s32[6]{0:T(128)} %constant.87.clone.refs_1_, s32[6]{0:T(128)} %constant.88.clone.refs_2_, s32[6]{0:T(128)} %constant.89.clone.refs_3_, f32[64,4096]{1,0:T(8,128)} %get-tuple-element.176.refs_4_, ...), custom_call_target="tpu_custom_call" | custom-call | flops 201326592 | bytes 3801088 | tf_op jit(solution)/shard_map/legendre_kept/pallas_call | solution.py:222
  410.1 7.4 %collective-permute-start.40 = (f32[4,2,32,896]{3,2,1,0:T(8,128)}, f32[4,2,32,896]{3,2,1,0:T(8,128)}, u32[]{:S(2)}, u32[]{:S(2)}) collective-permute-start(f32[4,2,32,896]{3,2,1,0:T(8,128)} %get-tuple-element.185.refs_9_), channel_id=1, source_target_pairs={{0,2},{1,3},{8,10},{9,11},{16,18},{17,19},{24,26},{25,27}} | collective-permute-start | bytes 2752520 | tf_op jit(solution)/shard_map/ppermute | solution.py:245
  417.5 1.8 slice_add_fusion.19
  420.7 3.4 collective-permute-done.25.refs_7_
  424.1 7.7 %legendre_kept.10 = (f32[4,2,32,1152]{3,2,1,0:T(8,128)}, f32[4,2,32,896]{3,2,1,0:T(8,128)}) custom-call(s32[1]{0:T(128)} %bitcast.7.refs_0_, s32[6]{0:T(128)} %constant.87.clone.refs_1_, s32[6]{0:T(128)} %constant.88.clone.refs_2_, s32[6]{0:T(128)} %constant.89.clone.refs_3_, f32[64,4096]{1,0:T(8,128)} %get-tuple-element.130.refs_4_, ...), custom_call_target="tpu_custom_call" | custom-call | flops 201326592 | bytes 3801088 | tf_op jit(solution)/shard_map/legendre_kept/pallas_call | solution.py:222
  440.4 24.6 %collective-permute-start.46 = (f32[4,2,32,896]{3,2,1,0:T(8,128)S(1)}, f32[4,2,32,896]{3,2,1,0:T(8,128)S(1)}, u32[]{:S(2)}, u32[]{:S(2)}) collective-permute-start(f32[4,2,32,896]{3,2,1,0:T(8,128)S(1)} %copy-done.27), channel_id=1, source_target_pairs={{0,2},{1,3},{8,10},{9,11},{16,18},{17,19},{24,26},{25,27}} | collective-permute-start | bytes 2752520 | tf_op jit(solution)/shard_map/ppermute | solution.py:245
  466.0 9.2 %collective-permute-done.7.refs_7_ = f32[4,2,32,512]{3,2,1,0:T(8,128)S(1)} collective-permute-done((f32[4,2,32,512]{3,2,1,0:T(8,128)S(1)}, f32[4,2,32,512]{3,2,1,0:T(8,128)S(1)}, u32[]{:S(2)}, u32[]{:S(2)}) %collective-permute-start.7) | collective-permute-done | bytes 524320 | tf_op jit(solution)/shard_map/ppermute | solution.py:245
  477.3 2.8 slice_add_fusion.2.refs_5_
  480.9 8.7 %collective-permute-done.28.refs_8_ = f32[4,2,32,512]{3,2,1,0:T(8,128)S(1)} collective-permute-done((f32[4,2,32,512]{3,2,1,0:T(8,128)S(1)}, f32[4,2,32,512]{3,2,1,0:T(8,128)S(1)}, u32[]{:S(2)}, u32[]{:S(2)}) %collective-permute-start.28) | collective-permute-done | bytes 524320 | tf_op jit(solution)/shard_map/ppermute | solution.py:245
  498.6 49.5 %collective-permute-done.42.refs_8_ = f32[4,2,32,512]{3,2,1,0:T(8,128)S(1)} collective-permute-done((f32[4,2,32,512]{3,2,1,0:T(8,128)S(1)}, f32[4,2,32,512]{3,2,1,0:T(8,128)S(1)}, u32[]{:S(2)}, u32[]{:S(2)}) %collective-permute-start.42) | collective-permute-done | bytes 524320 | tf_op jit(solution)/shard_map/ppermute | solution.py:245
  549.7 4.4 close.6.refs_2_
  554.1 4.1 close.7.refs_2_
  558.2 4.8 close.8.refs_2_
  563.7 4.7 close.9.refs_2_
  568.4 4.1 close.10.refs_2_
  573.3 4.1 close.11
  (263 shorter events, 68.9 us)
Async XLA Ops:
  51.7 23.5 %collective-permute-start = (f32[512,4096]{1,0:T(8,128)}, f32[512,4096]{1,0:T(8,128)}, u32[]{:S(2)}, u32[]{:S(2)}) collective-permute-start(f32[512,4096]{1,0:T(8,128)} %fourier_first.2), channel_id=1, source_target_pairs={{0,8},{8,0},{16,24},{24,16},{1,9},{9,1},{17,25},{25,17},{2,10},{10... | collective-permute-start | bytes 25165832 | tf_op jit(solution)/shard_map/ppermute | solution.py:305
  73.3 58.5 %collective-permute-start.9 = (f32[512,4096]{1,0:T(8,128)}, f32[512,4096]{1,0:T(8,128)}, u32[]{:S(2)}, u32[]{:S(2)}) collective-permute-start(f32[512,4096]{1,0:T(8,128)} %fourier_first.3), channel_id=1, source_target_pairs={{0,8},{8,0},{16,24},{24,16},{1,9},{9,1},{17,25},{25,17},{2,10},{10... | collective-permute-start | bytes 25165832 | tf_op jit(solution)/shard_map/ppermute | solution.py:305
  94.9 27.2 %collective-permute-start.1 = (f32[64,4096]{1,0:T(8,128)}, f32[64,4096]{1,0:T(8,128)S(1)}, u32[]{:S(2)}, u32[]{:S(2)}) collective-permute-start(f32[64,4096]{1,0:T(8,128)} %get-tuple-element.107), channel_id=1, source_target_pairs={{0,16},{8,24},{16,0},{24,8},{1,17},{9,25},{17,1},{25,9},{2,18},{10... | collective-permute-start | bytes 3145736 | tf_op jit(solution)/shard_map/ppermute | solution.py:305
  97.9 69.3 %collective-permute-start.10 = (f32[128,4096]{1,0:T(8,128)}, f32[128,4096]{1,0:T(8,128)}, u32[]{:S(2)}, u32[]{:S(2)}) collective-permute-start(f32[128,4096]{1,0:T(8,128)} %get-tuple-element.114), channel_id=1, source_target_pairs={{0,16},{8,24},{16,0},{24,8},{1,17},{9,25},{17,1},{25,9},{2,18},{10... | collective-permute-start | bytes 6291464 | tf_op jit(solution)/shard_map/ppermute | solution.py:305
  99.8 89.7 %collective-permute-start.16 = (f32[64,4096]{1,0:T(8,128)}, f32[64,4096]{1,0:T(8,128)S(1)}, u32[]{:S(2)}, u32[]{:S(2)}) collective-permute-start(f32[64,4096]{1,0:T(8,128)} %get-tuple-element.120), channel_id=1, source_target_pairs={{0,16},{8,24},{16,0},{24,8},{1,17},{9,25},{17,1},{25,9},{2,18},{10... | collective-permute-start | bytes 3145736 | tf_op jit(solution)/shard_map/ppermute | solution.py:305
  129.9 29.8 %collective-permute-start.2 = (f32[4,2,32,1280]{3,2,1,0:T(8,128)}, f32[4,2,32,1280]{3,2,1,0:T(8,128)}, u32[]{:S(2)}, u32[]{:S(2)}) collective-permute-start(f32[4,2,32,1280]{3,2,1,0:T(8,128)} %legendre_sent.6), channel_id=1, source_target_pairs={{0,1},{1,0},{2,3},{3,2},{4,5},{5,4},{6,7},{7,6},{8,9},{9,8},{10,11... | collective-permute-start | bytes 3932168 | tf_op jit(solution)/shard_map/ppermute | solution.py:346
  151.4 118.2 %collective-permute-start.20 = (f32[128,4096]{1,0:T(8,128)}, f32[128,4096]{1,0:T(8,128)S(1)}, u32[]{:S(2)}, u32[]{:S(2)}) collective-permute-start(f32[128,4096]{1,0:T(8,128)} %get-tuple-element.124), channel_id=1, source_target_pairs={{0,16},{8,24},{16,0},{24,8},{1,17},{9,25},{17,1},{25,9},{2,18},{10... | collective-permute-start | bytes 6291464 | tf_op jit(solution)/shard_map/ppermute | solution.py:305
  175.9 114.6 %collective-permute-start.11 = (f32[8,2,32,1280]{3,2,1,0:T(8,128)}, f32[8,2,32,1280]{3,2,1,0:T(8,128)}, u32[]{:S(2)}, u32[]{:S(2)}) collective-permute-start(f32[8,2,32,1280]{3,2,1,0:T(8,128)} %legendre_sent.7), channel_id=1, source_target_pairs={{0,1},{1,0},{2,3},{3,2},{4,5},{5,4},{6,7},{7,6},{8,9},{9,8},{10,11... | collective-permute-start | bytes 7864328 | tf_op jit(solution)/shard_map/ppermute | solution.py:346
  197.3 64.5 %collective-permute-start.17 = (f32[4,2,32,1280]{3,2,1,0:T(8,128)}, f32[4,2,32,1280]{3,2,1,0:T(8,128)}, u32[]{:S(2)}, u32[]{:S(2)}) collective-permute-start(f32[4,2,32,1280]{3,2,1,0:T(8,128)} %legendre_sent.8), channel_id=1, source_target_pairs={{0,1},{1,0},{2,3},{3,2},{4,5},{5,4},{6,7},{7,6},{8,9},{9,8},{10,11... | collective-permute-start | bytes 3932168 | tf_op jit(solution)/shard_map/ppermute | solution.py:346
  199.3 89.7 %collective-permute-start.3 = (f32[4,2,32,1152]{3,2,1,0:T(8,128)}, f32[4,2,32,1152]{3,2,1,0:T(8,128)}, u32[]{:S(2)}, u32[]{:S(2)}) collective-permute-start(f32[4,2,32,1152]{3,2,1,0:T(8,128)} %get-tuple-element.133.refs_2_), channel_id=1, source_target_pairs={{6,4},{7,5},{14,12},{15,13},{22,20},{23,21},{30,28},{31,29}} | collective-permute-start | bytes 3538952 | tf_op jit(solution)/shard_map/ppermute | solution.py:245
  201.0 81.8 %collective-permute-start.5 = (f32[4,2,32,896]{3,2,1,0:T(8,128)}, f32[4,2,32,896]{3,2,1,0:T(8,128)S(1)}, u32[]{:S(2)}, u32[]{:S(2)}) collective-permute-start(f32[4,2,32,896]{3,2,1,0:T(8,128)} %get-tuple-element.139.refs_8_), channel_id=1, source_target_pairs={{0,2},{1,3},{8,10},{9,11},{16,18},{17,19},{24,26},{25,27}} | collective-permute-start | bytes 2752520 | tf_op jit(solution)/shard_map/ppermute | solution.py:245
  279.6 56.9 %collective-permute-start.21 = (f32[8,2,32,1280]{3,2,1,0:T(8,128)}, f32[8,2,32,1280]{3,2,1,0:T(8,128)}, u32[]{:S(2)}, u32[]{:S(2)}) collective-permute-start(f32[8,2,32,1280]{3,2,1,0:T(8,128)} %legendre_sent.9), channel_id=1, source_target_pairs={{0,1},{1,0},{2,3},{3,2},{4,5},{5,4},{6,7},{7,6},{8,9},{9,8},{10,11... | collective-permute-start | bytes 7864328 | tf_op jit(solution)/shard_map/ppermute | solution.py:346
  281.1 23.0 %collective-permute-start.18 = (f32[4,2,32,1152]{3,2,1,0:T(8,128)}, f32[4,2,32,1152]{3,2,1,0:T(8,128)}, u32[]{:S(2)}, u32[]{:S(2)}) collective-permute-start(f32[4,2,32,1152]{3,2,1,0:T(8,128)} %get-tuple-element.143.refs_3_), channel_id=1, source_target_pairs={{6,4},{7,5},{14,12},{15,13},{22,20},{23,21},{30,28},{31,29}} | collective-permute-start | bytes 3538952 | tf_op jit(solution)/shard_map/ppermute | solution.py:245
  282.8 20.6 %collective-permute-start.19 = (f32[4,2,32,896]{3,2,1,0:T(8,128)}, f32[4,2,32,896]{3,2,1,0:T(8,128)}, u32[]{:S(2)}, u32[]{:S(2)}) collective-permute-start(f32[4,2,32,896]{3,2,1,0:T(8,128)} %get-tuple-element.149.refs_9_), channel_id=1, source_target_pairs={{0,2},{1,3},{8,10},{9,11},{16,18},{17,19},{24,26},{25,27}} | collective-permute-start | bytes 2752520 | tf_op jit(solution)/shard_map/ppermute | solution.py:245
  300.8 53.8 %collective-permute-start.12 = (f32[8,2,32,1152]{3,2,1,0:T(8,128)}, f32[8,2,32,1152]{3,2,1,0:T(8,128)S(1)}, u32[]{:S(2)}, u32[]{:S(2)}) collective-permute-start(f32[8,2,32,1152]{3,2,1,0:T(8,128)} %get-tuple-element.153.refs_3_), channel_id=1, source_target_pairs={{6,4},{7,5},{14,12},{15,13},{22,20},{23,21},{30,28},{31,29}} | collective-permute-start | bytes 7077896 | tf_op jit(solution)/shard_map/ppermute | solution.py:245
  301.6 6.0 %collective-permute-start.6 = (f32[4,2,32,384]{3,2,1,0:T(8,128)}, f32[4,2,32,384]{3,2,1,0:T(8,128)S(1)}, u32[]{:S(2)}, u32[]{:S(2)}) collective-permute-start(f32[4,2,32,384]{3,2,1,0:T(8,128)} %slice_add_fusion.17), channel_id=1, source_target_pairs={{2,4},{3,5},{10,12},{11,13},{18,20},{19,21},{26,28},{27,29}} | collective-permute-start | bytes 1179656 | tf_op jit(solution)/shard_map/ppermute | solution.py:245
  303.4 14.5 %collective-permute-start.4 = (f32[4,2,32,896]{3,2,1,0:T(8,128)S(1)}, f32[4,2,32,896]{3,2,1,0:T(8,128)S(1)}, u32[]{:S(2)}, u32[]{:S(2)}) collective-permute-start(f32[4,2,32,896]{3,2,1,0:T(8,128)S(1)} %slice_add_fusion.7.refs_3_), channel_id=1, source_target_pairs={{4,2},{5,3},{12,10},{13,11},{20,18},{21,19},{28,26},{29,27}} | collective-permute-start | bytes 2752520 | tf_op jit(solution)/shard_map/ppermute | solution.py:245
  304.1 47.0 %collective-permute-start.24 = (f32[64,4096]{1,0:T(8,128)}, f32[64,4096]{1,0:T(8,128)}, u32[]{:S(2)}, u32[]{:S(2)}) collective-permute-start(f32[64,4096]{1,0:T(8,128)} %get-tuple-element.129), channel_id=1, source_target_pairs={{0,16},{8,24},{16,0},{24,8},{1,17},{9,25},{17,1},{25,9},{2,18},{10... | collective-permute-start | bytes 3145736 | tf_op jit(solution)/shard_map/ppermute | solution.py:305
  307.6 61.2 %collective-permute-start.14 = (f32[8,2,32,896]{3,2,1,0:T(8,128)}, f32[8,2,32,896]{3,2,1,0:T(8,128)}, u32[]{:S(2)}, u32[]{:S(2)}) collective-permute-start(f32[8,2,32,896]{3,2,1,0:T(8,128)} %get-tuple-element.159.refs_9_), channel_id=1, source_target_pairs={{0,2},{1,3},{8,10},{9,11},{16,18},{17,19},{24,26},{25,27}} | collective-permute-start | bytes 5505032 | tf_op jit(solution)/shard_map/ppermute | solution.py:245
  317.9 35.3 %collective-permute-start.36 = (f32[64,4096]{1,0:T(8,128)}, f32[64,4096]{1,0:T(8,128)}, u32[]{:S(2)}, u32[]{:S(2)}) collective-permute-start(f32[64,4096]{1,0:T(8,128)} %get-tuple-element.175), channel_id=1, source_target_pairs={{0,16},{8,24},{16,0},{24,8},{1,17},{9,25},{17,1},{25,9},{2,18},{10... | collective-permute-start | bytes 3145736 | tf_op jit(solution)/shard_map/ppermute | solution.py:305
  346.9 40.7 %collective-permute-start.23 = (f32[8,2,32,896]{3,2,1,0:T(8,128)}, f32[8,2,32,896]{3,2,1,0:T(8,128)}, u32[]{:S(2)}, u32[]{:S(2)}) collective-permute-start(f32[8,2,32,896]{3,2,1,0:T(8,128)} %get-tuple-element.169.refs_9_), channel_id=1, source_target_pairs={{0,2},{1,3},{8,10},{9,11},{16,18},{17,19},{24,26},{25,27}} | collective-permute-start | bytes 5505032 | tf_op jit(solution)/shard_map/ppermute | solution.py:245
  351.1 42.3 %collective-permute-start.22 = (f32[8,2,32,1152]{3,2,1,0:T(8,128)}, f32[8,2,32,1152]{3,2,1,0:T(8,128)}, u32[]{:S(2)}, u32[]{:S(2)}) collective-permute-start(f32[8,2,32,1152]{3,2,1,0:T(8,128)} %get-tuple-element.163.refs_3_), channel_id=1, source_target_pairs={{6,4},{7,5},{14,12},{15,13},{22,20},{23,21},{30,28},{31,29}} | collective-permute-start | bytes 7077896 | tf_op jit(solution)/shard_map/ppermute | solution.py:245
  353.2 6.9 %collective-permute-start.27 = (f32[4,2,32,384]{3,2,1,0:T(8,128)}, f32[4,2,32,384]{3,2,1,0:T(8,128)}, u32[]{:S(2)}, u32[]{:S(2)}) collective-permute-start(f32[4,2,32,384]{3,2,1,0:T(8,128)} %slice_add_fusion.16), channel_id=1, source_target_pairs={{2,4},{3,5},{10,12},{11,13},{18,20},{19,21},{26,28},{27,29}} | collective-permute-start | bytes 1179656 | tf_op jit(solution)/shard_map/ppermute | solution.py:245
  356.1 24.9 %collective-permute-start.26 = (f32[4,2,32,896]{3,2,1,0:T(8,128)S(1)}, f32[4,2,32,896]{3,2,1,0:T(8,128)}, u32[]{:S(2)}, u32[]{:S(2)}) collective-permute-start(f32[4,2,32,896]{3,2,1,0:T(8,128)S(1)} %copy-done.5), channel_id=1, source_target_pairs={{4,2},{5,3},{12,10},{13,11},{20,18},{21,19},{28,26},{29,27}} | collective-permute-start | bytes 2752520 | tf_op jit(solution)/shard_map/ppermute | solution.py:245
  360.1 59.2 %copy-start = (f32[8,2,32,896]{3,2,1,0:T(8,128)}, f32[8,2,32,896]{3,2,1,0:T(8,128)S(1)}, u32[]{:S(2)}) copy-start(f32[8,2,32,896]{3,2,1,0:T(8,128)S(1)} %slice_add_fusion.1.refs_4_) | copy-start | bytes 5505028
  360.1 59.2 %collective-permute-start.13 = (f32[8,2,32,896]{3,2,1,0:T(8,128)S(1)}, f32[8,2,32,896]{3,2,1,0:T(8,128)}, u32[]{:S(2)}, u32[]{:S(2)}) collective-permute-start(f32[8,2,32,896]{3,2,1,0:T(8,128)S(1)} %slice_add_fusion.1.refs_4_), channel_id=1, source_target_pairs={{4,2},{5,3},{12,10},{13,11},{20,18},{21,19},{28,26},{29,27}} | collective-permute-start | bytes 5505032 | tf_op jit(solution)/shard_map/ppermute | solution.py:245
  368.8 32.0 %collective-permute-start.37 = (f32[4,2,32,1280]{3,2,1,0:T(8,128)}, f32[4,2,32,1280]{3,2,1,0:T(8,128)}, u32[]{:S(2)}, u32[]{:S(2)}) collective-permute-start(f32[4,2,32,1280]{3,2,1,0:T(8,128)} %legendre_sent.11), channel_id=1, source_target_pairs={{0,1},{1,0},{2,3},{3,2},{4,5},{5,4},{6,7},{7,6},{8,9},{9,8},{10,11... | collective-permute-start | bytes 3932168 | tf_op jit(solution)/shard_map/ppermute | solution.py:346
  381.1 43.1 %collective-permute-start.25 = (f32[4,2,32,1280]{3,2,1,0:T(8,128)}, f32[4,2,32,1280]{3,2,1,0:T(8,128)}, u32[]{:S(2)}, u32[]{:S(2)}) collective-permute-start(f32[4,2,32,1280]{3,2,1,0:T(8,128)} %legendre_sent.10), channel_id=1, source_target_pairs={{0,1},{1,0},{2,3},{3,2},{4,5},{5,4},{6,7},{7,6},{8,9},{9,8},{10,11... | collective-permute-start | bytes 3932168 | tf_op jit(solution)/shard_map/ppermute | solution.py:346
  387.6 22.5 %collective-permute-start.15 = (f32[8,2,32,384]{3,2,1,0:T(8,128)}, f32[8,2,32,384]{3,2,1,0:T(8,128)}, u32[]{:S(2)}, u32[]{:S(2)}) collective-permute-start(f32[8,2,32,384]{3,2,1,0:T(8,128)} %slice_add_fusion.9), channel_id=1, source_target_pairs={{2,4},{3,5},{10,12},{11,13},{18,20},{19,21},{26,28},{27,29}} | collective-permute-start | bytes 2359304 | tf_op jit(solution)/shard_map/ppermute | solution.py:245
  396.4 80.1 %collective-permute-start.32 = (f32[8,2,32,896]{3,2,1,0:T(8,128)}, f32[8,2,32,896]{3,2,1,0:T(8,128)}, u32[]{:S(2)}, u32[]{:S(2)}) collective-permute-start(f32[8,2,32,896]{3,2,1,0:T(8,128)} %slice_add_fusion.refs_4_), channel_id=1, source_target_pairs={{4,2},{5,3},{12,10},{13,11},{20,18},{21,19},{28,26},{29,27}} | collective-permute-start | bytes 5505032 | tf_op jit(solution)/shard_map/ppermute | solution.py:245
  408.4 27.5 %collective-permute-start.38 = (f32[4,2,32,1152]{3,2,1,0:T(8,128)}, f32[4,2,32,1152]{3,2,1,0:T(8,128)}, u32[]{:S(2)}, u32[]{:S(2)}) collective-permute-start(f32[4,2,32,1152]{3,2,1,0:T(8,128)} %get-tuple-element.179.refs_3_), channel_id=1, source_target_pairs={{6,4},{7,5},{14,12},{15,13},{22,20},{23,21},{30,28},{31,29}} | collective-permute-start | bytes 3538952 | tf_op jit(solution)/shard_map/ppermute | solution.py:245
  410.1 23.9 %collective-permute-start.40 = (f32[4,2,32,896]{3,2,1,0:T(8,128)}, f32[4,2,32,896]{3,2,1,0:T(8,128)}, u32[]{:S(2)}, u32[]{:S(2)}) collective-permute-start(f32[4,2,32,896]{3,2,1,0:T(8,128)} %get-tuple-element.185.refs_9_), channel_id=1, source_target_pairs={{0,2},{1,3},{8,10},{9,11},{16,18},{17,19},{24,26},{25,27}} | collective-permute-start | bytes 2752520 | tf_op jit(solution)/shard_map/ppermute | solution.py:245
  420.7 68.9 %copy-start.10 = (f32[8,2,32,512]{3,2,1,0:T(8,128)}, f32[8,2,32,512]{3,2,1,0:T(8,128)S(1)}, u32[]{:S(2)}) copy-start(f32[8,2,32,512]{3,2,1,0:T(8,128)S(1)} %slice_add_fusion.3.refs_5_) | copy-start | bytes 3145732
  431.8 8.5 %collective-permute-start.44 = (f32[4,2,32,1152]{3,2,1,0:T(8,128)}, f32[4,2,32,1152]{3,2,1,0:T(8,128)S(1)}, u32[]{:S(2)}, u32[]{:S(2)}) collective-permute-start(f32[4,2,32,1152]{3,2,1,0:T(8,128)} %get-tuple-element.189.refs_3_), channel_id=1, source_target_pairs={{6,4},{7,5},{14,12},{15,13},{22,20},{23,21},{30,28},{31,29}} | collective-permute-start | bytes 3538952 | tf_op jit(solution)/shard_map/ppermute | solution.py:245
  432.7 5.4 collective-permute-start.8
  434.0 5.0 collective-permute-start.29
  435.9 29.3 %collective-permute-start.41 = (f32[4,2,32,384]{3,2,1,0:T(8,128)S(1)}, f32[4,2,32,384]{3,2,1,0:T(8,128)S(1)}, u32[]{:S(2)}, u32[]{:S(2)}) collective-permute-start(f32[4,2,32,384]{3,2,1,0:T(8,128)S(1)} %slice_add_fusion.15), channel_id=1, source_target_pairs={{2,4},{3,5},{10,12},{11,13},{18,20},{19,21},{26,28},{27,29}} | collective-permute-start | bytes 1179656 | tf_op jit(solution)/shard_map/ppermute | solution.py:245
  438.1 42.7 %copy-start.6 = (f32[4,2,32,896]{3,2,1,0:T(8,128)}, f32[4,2,32,896]{3,2,1,0:T(8,128)S(1)}, u32[]{:S(2)}) copy-start(f32[4,2,32,896]{3,2,1,0:T(8,128)S(1)} %slice_add_fusion.5.refs_4_) | copy-start | bytes 2752516
  438.1 37.1 %copy-start.20 = (f32[4,2,32,512]{3,2,1,0:T(8,128)S(1)}, f32[4,2,32,512]{3,2,1,0:T(8,128)}, u32[]{:S(2)}) copy-start(f32[4,2,32,512]{3,2,1,0:T(8,128)} %slice_add_fusion.12.refs_5_) | copy-start | bytes 1572868
  438.1 38.4 %copy-start.30 = (f32[8,2,32,384]{3,2,1,0:T(8,128)S(1)}, f32[8,2,32,384]{3,2,1,0:T(8,128)}, u32[]{:S(2)}) copy-start(f32[8,2,32,384]{3,2,1,0:T(8,128)} %slice_add_fusion.8) | copy-start | bytes 2359300
  438.1 41.9 %collective-permute-start.39 = (f32[4,2,32,896]{3,2,1,0:T(8,128)S(1)}, f32[4,2,32,896]{3,2,1,0:T(8,128)S(1)}, u32[]{:S(2)}, u32[]{:S(2)}) collective-permute-start(f32[4,2,32,896]{3,2,1,0:T(8,128)S(1)} %slice_add_fusion.5.refs_4_), channel_id=1, source_target_pairs={{4,2},{5,3},{12,10},{13,11},{20,18},{21,19},{28,26},{29,27}} | collective-permute-start | bytes 2752520 | tf_op jit(solution)/shard_map/ppermute | solution.py:245
  439.0 41.1 %copy-start.41 = (f32[4,2,32,128]{3,2,1,0:T(8,128)}, f32[4,2,32,128]{3,2,1,0:T(8,128)S(1)}, u32[]{:S(2)}) copy-start(f32[4,2,32,128]{3,2,1,0:T(8,128)S(1)} %collective-permute-done.29.refs_12_) | copy-start | bytes 393220
  439.0 36.2 %collective-permute-start.7 = (f32[4,2,32,512]{3,2,1,0:T(8,128)S(1)}, f32[4,2,32,512]{3,2,1,0:T(8,128)S(1)}, u32[]{:S(2)}, u32[]{:S(2)}) collective-permute-start(f32[4,2,32,512]{3,2,1,0:T(8,128)S(1)} %copy-done.19), channel_id=1, source_target_pairs={{2,0},{3,1},{10,8},{11,9},{18,16},{19,17},{26,24},{27,25}} | collective-permute-start | bytes 1572872 | tf_op jit(solution)/shard_map/ppermute | solution.py:245
  440.3 39.7 %copy-start.12 = (f32[4,2,32,1152]{3,2,1,0:T(8,128)}, f32[4,2,32,1152]{3,2,1,0:T(8,128)S(1)}, u32[]{:S(2)}) copy-start(f32[4,2,32,1152]{3,2,1,0:T(8,128)S(1)} %collective-permute-done.44.refs_6_) | copy-start | bytes 3538948
  440.4 50.5 %collective-permute-start.46 = (f32[4,2,32,896]{3,2,1,0:T(8,128)S(1)}, f32[4,2,32,896]{3,2,1,0:T(8,128)S(1)}, u32[]{:S(2)}, u32[]{:S(2)}) collective-permute-start(f32[4,2,32,896]{3,2,1,0:T(8,128)S(1)} %copy-done.27), channel_id=1, source_target_pairs={{0,2},{1,3},{8,10},{9,11},{16,18},{17,19},{24,26},{25,27}} | collective-permute-start | bytes 2752520 | tf_op jit(solution)/shard_map/ppermute | solution.py:245
  465.1 29.1 %collective-permute-start.45 = (f32[4,2,32,896]{3,2,1,0:T(8,128)S(1)}, f32[4,2,32,896]{3,2,1,0:T(8,128)S(1)}, u32[]{:S(2)}, u32[]{:S(2)}) collective-permute-start(f32[4,2,32,896]{3,2,1,0:T(8,128)S(1)} %slice_add_fusion.4.refs_4_), channel_id=1, source_target_pairs={{4,2},{5,3},{12,10},{13,11},{20,18},{21,19},{28,26},{29,27}} | collective-permute-start | bytes 2752520 | tf_op jit(solution)/shard_map/ppermute | solution.py:245
  475.2 14.3 %collective-permute-start.28 = (f32[4,2,32,512]{3,2,1,0:T(8,128)S(1)}, f32[4,2,32,512]{3,2,1,0:T(8,128)S(1)}, u32[]{:S(2)}, u32[]{:S(2)}) collective-permute-start(f32[4,2,32,512]{3,2,1,0:T(8,128)S(1)} %copy-done.20), channel_id=1, source_target_pairs={{2,0},{3,1},{10,8},{11,9},{18,16},{19,17},{26,24},{27,25}} | collective-permute-start | bytes 1572872 | tf_op jit(solution)/shard_map/ppermute | solution.py:245
  476.6 15.7 %collective-permute-start.33 = (f32[8,2,32,384]{3,2,1,0:T(8,128)S(1)}, f32[8,2,32,384]{3,2,1,0:T(8,128)S(1)}, u32[]{:S(2)}, u32[]{:S(2)}) collective-permute-start(f32[8,2,32,384]{3,2,1,0:T(8,128)S(1)} %copy-done.30), channel_id=1, source_target_pairs={{2,4},{3,5},{10,12},{11,13},{18,20},{19,21},{26,28},{27,29}} | collective-permute-start | bytes 2359304 | tf_op jit(solution)/shard_map/ppermute | solution.py:245
  480.1 12.8 %collective-permute-start.31 = (f32[8,2,32,128]{3,2,1,0:T(8,128)S(1)}, f32[8,2,32,128]{3,2,1,0:T(8,128)S(1)}, u32[]{:S(2)}, u32[]{:S(2)}) collective-permute-start(f32[8,2,32,128]{3,2,1,0:T(8,128)S(1)} %copy-done.40), channel_id=1, source_target_pairs={{4,6},{5,7},{12,14},{13,15},{20,22},{21,23},{28,30},{29,31}} | collective-permute-start | bytes 786440 | tf_op jit(solution)/shard_map/ppermute | solution.py:245
  480.9 73.1 %copy-start.21 = (f32[4,2,32,512]{3,2,1,0:T(8,128)}, f32[4,2,32,512]{3,2,1,0:T(8,128)S(1)}, u32[]{:S(2)}) copy-start(f32[4,2,32,512]{3,2,1,0:T(8,128)S(1)} %slice_add_fusion.11.refs_5_) | copy-start | bytes 1572868
  489.6 58.5 %copy-start.37 = (f32[4,2,32,512]{3,2,1,0:T(8,128)}, f32[4,2,32,512]{3,2,1,0:T(8,128)S(1)}, u32[]{:S(2)}) copy-start(f32[4,2,32,512]{3,2,1,0:T(8,128)S(1)} %collective-permute-done.28.refs_8_) | copy-start | bytes 1572868
  489.6 68.6 %collective-permute-start.30 = (f32[8,2,32,512]{3,2,1,0:T(8,128)S(1)}, f32[8,2,32,512]{3,2,1,0:T(8,128)}, u32[]{:S(2)}, u32[]{:S(2)}) collective-permute-start(f32[8,2,32,512]{3,2,1,0:T(8,128)S(1)} %slice_add_fusion.3.refs_5_), channel_id=1, source_target_pairs={{2,0},{3,1},{10,8},{11,9},{18,16},{19,17},{26,24},{27,25}} | collective-permute-start | bytes 3145736 | tf_op jit(solution)/shard_map/ppermute | solution.py:245
  490.9 57.2 %copy-start.28 = (f32[4,2,32,896]{3,2,1,0:T(8,128)}, f32[4,2,32,896]{3,2,1,0:T(8,128)S(1)}, u32[]{:S(2)}) copy-start(f32[4,2,32,896]{3,2,1,0:T(8,128)S(1)} %collective-permute-done.46.refs_10_) | copy-start | bytes 2752516
  490.9 72.1 %collective-permute-start.34 = (f32[8,2,32,512]{3,2,1,0:T(8,128)}, f32[8,2,32,512]{3,2,1,0:T(8,128)}, u32[]{:S(2)}, u32[]{:S(2)}) collective-permute-start(f32[8,2,32,512]{3,2,1,0:T(8,128)} %slice_add_fusion.2.refs_5_), channel_id=1, source_target_pairs={{2,0},{3,1},{10,8},{11,9},{18,16},{19,17},{26,24},{27,25}} | collective-permute-start | bytes 3145736 | tf_op jit(solution)/shard_map/ppermute | solution.py:245
  492.3 55.9 %copy-start.29 = (f32[8,2,32,384]{3,2,1,0:T(8,128)}, f32[8,2,32,384]{3,2,1,0:T(8,128)S(1)}, u32[]{:S(2)}) copy-start(f32[8,2,32,384]{3,2,1,0:T(8,128)S(1)} %collective-permute-done.33.refs_11_) | copy-start | bytes 2359300
  492.3 2.8 collective-permute-start.43
  493.0 55.1 %collective-permute-start.42 = (f32[4,2,32,512]{3,2,1,0:T(8,128)S(1)}, f32[4,2,32,512]{3,2,1,0:T(8,128)S(1)}, u32[]{:S(2)}, u32[]{:S(2)}) collective-permute-start(f32[4,2,32,512]{3,2,1,0:T(8,128)S(1)} %slice_add_fusion.11.refs_5_), channel_id=1, source_target_pairs={{2,0},{3,1},{10,8},{11,9},{18,16},{19,17},{26,24},{27,25}} | collective-permute-start | bytes 1572872 | tf_op jit(solution)/shard_map/ppermute | solution.py:245
  494.3 3.0 collective-permute-start.47
  495.1 59.0 %copy-start.22 = (f32[4,2,32,512]{3,2,1,0:T(8,128)}, f32[4,2,32,512]{3,2,1,0:T(8,128)S(1)}, u32[]{:S(2)}) copy-start(f32[4,2,32,512]{3,2,1,0:T(8,128)S(1)} %slice_add_fusion.10.refs_5_) | copy-start | bytes 1572868
  495.2 58.8 %copy-start.42 = (f32[4,2,32,128]{3,2,1,0:T(8,128)}, f32[4,2,32,128]{3,2,1,0:T(8,128)S(1)}, u32[]{:S(2)}) copy-start(f32[4,2,32,128]{3,2,1,0:T(8,128)S(1)} %collective-permute-done.43.refs_12_) | copy-start | bytes 393220
  495.2 77.3 %collective-permute-start.48 = (f32[4,2,32,512]{3,2,1,0:T(8,128)S(1)}, f32[4,2,32,512]{3,2,1,0:T(8,128)S(1)}, u32[]{:S(2)}, u32[]{:S(2)}) collective-permute-start(f32[4,2,32,512]{3,2,1,0:T(8,128)S(1)} %slice_add_fusion.10.refs_5_), channel_id=1, source_target_pairs={{2,0},{3,1},{10,8},{11,9},{18,16},{19,17},{26,24},{27,25}} | collective-permute-start | bytes 1572872 | tf_op jit(solution)/shard_map/ppermute | solution.py:245
  497.2 50.9 %copy-start.33 = (f32[4,2,32,384]{3,2,1,0:T(8,128)}, f32[4,2,32,384]{3,2,1,0:T(8,128)S(1)}, u32[]{:S(2)}) copy-start(f32[4,2,32,384]{3,2,1,0:T(8,128)S(1)} %collective-permute-done.47.refs_11_) | copy-start | bytes 1179652
  497.2 65.7 %collective-permute-start.35 = (f32[8,2,32,128]{3,2,1,0:T(8,128)}, f32[8,2,32,128]{3,2,1,0:T(8,128)S(1)}, u32[]{:S(2)}, u32[]{:S(2)}) collective-permute-start(f32[8,2,32,128]{3,2,1,0:T(8,128)} %slice_add_fusion.18), channel_id=1, source_target_pairs={{4,6},{5,7},{12,14},{13,15},{20,22},{21,23},{28,30},{29,31}} | collective-permute-start | bytes 786440 | tf_op jit(solution)/shard_map/ppermute | solution.py:245
  549.0 23.5 %collective-permute-start.49 = (f32[4,2,32,128]{3,2,1,0:T(8,128)}, f32[4,2,32,128]{3,2,1,0:T(8,128)S(1)}, u32[]{:S(2)}, u32[]{:S(2)}) collective-permute-start(f32[4,2,32,128]{3,2,1,0:T(8,128)} %slice_add_fusion.20), channel_id=1, source_target_pairs={{4,6},{5,7},{12,14},{13,15},{20,22},{21,23},{28,30},{29,31}} | collective-permute-start | bytes 393224 | tf_op jit(solution)/shard_map/ppermute | solution.py:245
  (52 other events, 410.3 us)

commit v5 on v4

--- a/solution.py
+++ b/solution.py
@@ -11,7 +11,7 @@
 
 ADIABATIC = 0.286
 LANES = 128
-SPLIT = ((1, 1, 2), (2, 1, 1))
+SPLIT = ((1, 1), (2,), (2, 1, 1))
 ROWS_CONTRACTED = (((1,), (1,)), ((), ()))
 
 
@@ -272,8 +272,8 @@
 
     longitude = lon * longitudes + lax.iota(jnp.int32, longitudes)
 
-    def table(wavenumbers, scale):
-        product = wavenumbers[..., None] * longitude % nlon
+    def table(wavenumbers, scale, turn=0):
+        product = (wavenumbers[..., None] * longitude + jnp.asarray(turn)[..., None]) % nlon
         angles = product.astype(jnp.float32) * (2.0 * math.pi / nlon)
         return jnp.cos(angles) * scale, jnp.sin(angles) * scale
 
@@ -281,28 +281,6 @@
     coarse = table(lon_count * own * bands.reshape(-1), 1.0)
     keep = list(range(lon_count - 2, -1, -2))
     halves = [keep[: len(keep) // 2], keep[len(keep) // 2 :]]
-
-    steps = lon_count * lax.iota(jnp.int32, own)
-    rels = jnp.stack([lon ^ rel for rel in range(lon_count)])
-    cos, sin = table(rels[:, None] + steps, 1.0 / math.sqrt(nlon))
-
-    def phases(bit, chunks):
-        blocks = []
-        for some in halves:
-            for place, count in chunks:
-                def fine(values):
-                    return jnp.stack([values[rel | bit, place : place + count] for rel in some])
-
-                first = jnp.concatenate([fine(cos), -fine(sin)], 1)[:, None]
-                second = jnp.concatenate([fine(sin), fine(cos)], 1)[:, None]
-                both = coarse[0][:, None] * first - coarse[1][:, None] * second
-                blocks.append(both.reshape(-1, longitudes))
-        both = jnp.concatenate(blocks, 0)
-        top = lax.reduce_precision(both, 8, 7)
-        return top.astype(jnp.bfloat16), (both - top).astype(jnp.bfloat16)
-
-    def lon_swap(value, bit):
-        return lax.ppermute(value, "lon", [(i, i ^ bit) for i in range(lon_count)])
 
     groups, place = [], 0
     for group in sizes(own):
@@ -312,19 +290,53 @@
             place += count
         groups.append(chunks)
 
-    swapped, before = [], None
-    for chunks in groups:
-        here = tendencies if before is None else (after(tendencies[0], before), tendencies[1])
-        ready = phases(1, chunks)
-        before = fourier(ready, here)
-        swapped.append(lon_swap(before, 1))
-    pieces = []
-    for chunks, came in zip(groups, swapped):
+    spots = [
+        (start + r, part)
+        for chunks in groups
+        for start, count in chunks
+        for part in range(2)
+        for r in range(count)
+    ]
+    steps = jnp.asarray(np.array([lon_count * r for r, _ in spots], np.int32))
+    quarters = jnp.asarray(np.array([part * (nlon // 4) for _, part in spots], np.int32))
+    rels = jnp.stack([lon ^ rel for rel in range(lon_count)])
+    cos, sin = table(rels[:, None] + steps, 1.0 / math.sqrt(nlon), quarters)
+
+    def phases(bit, chunks):
+        blocks = []
+        for some in halves:
+            for place, count in chunks:
+                rows = slice(2 * place, 2 * (place + count))
+                for rel in some:
+                    first, second = cos[rel | bit, rows], sin[rel | bit, rows]
+                    both = coarse[0][:, None] * first - coarse[1][:, None] * second
+                    blocks.append(both.reshape(-1, longitudes))
+        both = jnp.concatenate(blocks, 0)
+        top = lax.reduce_precision(both, 8, 7)
+        return top.astype(jnp.bfloat16), (both - top).astype(jnp.bfloat16)
+
+    def lon_swap(value, bit):
+        return lax.ppermute(value, "lon", [(i, i ^ bit) for i in range(lon_count)])
+
+    given, chains, kept, pieces, swapped = [], [], [], [], []
+    before = []
+
+    def held():
+        if not before:
+            return tendencies
+        return after(tendencies[0], before[-1]), tendencies[1]
+
+    def first(number):
+        ready = phases(1, groups[number])
+        before.append(fourier(ready, held()))
+        swapped.append(lon_swap(before[-1], 1))
+
+    def second(number):
+        chunks = groups[number]
         parts = [len(keep) // 2 * 4 * zones * count for _, count in chunks] * 2
-        here = (after(tendencies[0], before), tendencies[1])
         ready = phases(0, chunks)
-        blocks = fourier(ready, here, came, parts)
-        before = blocks[-1]
+        blocks = fourier(ready, held(), swapped[number], parts)
+        before.append(blocks[-1])
         for k, (place, count) in enumerate(chunks):
             far, near = blocks[k], blocks[len(chunks) + k]
             bit = lon_count // 2
@@ -335,21 +347,31 @@
                 bit //= 2
             pieces.append((place, count, near, lon_swap(far, bit)))
 
-    result = None
-    given, chains, kept = [None] * len(pieces), [], []
-
     def send(k):
         place, count, near, came = pieces[k]
-        if k > 1:
+        if k > 1 and len(kept) > k - 2:
             near = after(near, *kept[k - 2])
+        else:
+            near = after(near, before[-1])
         (value,) = project(plan, 1 - side, place, count, own, near, came, legendre)
-        given[k] = lax.ppermute(value, "lat", [(i, i ^ 1) for i in range(lat_count)])
-
+        before.append(value)
+        given.append(lax.ppermute(value, "lat", [(i, i ^ 1) for i in range(lat_count)]))
+
+    first(0)
+    second(0)
+    for number in range(1, len(groups)):
+        first(number)
+    send(0)
+    for number in range(1, len(groups)):
+        second(number)
+        if number == 1 and len(pieces) > 1:
+            send(1)
+    result = None
     rounds = max(zones - 1, 1)
     for k, (place, count, near, came) in enumerate(pieces):
         if k == 0:
-            send(0)
-        if k + 1 < len(pieces):
+            near = after(near, before[-1])
+        if len(given) == k + 1 and k + 1 < len(pieces):
             send(k + 1)
         waits = []
         for number, chain in enumerate(chains):

time: 581 us -> 590 us (1.015)
  Pallas kernels: 214 us -> 230 us
  starting transfers between devices: 104 us -> 94.9 us
  waiting for transfers between devices: 193 us -> 200 us
    ppermute x6, waiting for transfers between devices: 86.9 us -> 103 us  [send(): lax.ppermute(value, 'lat', [(i, i ^ 1) for i in range(lat_count)])]
    pallas_call x2 -> x3, Pallas kernels: 39.2 us -> 47.8 us  [fourier(): pl.pallas_call(second_fourier_kernel, grid=(rows // block,), in_specs=[wh...]
    pallas_call x2 -> x3, Pallas kernels: 36.7 us -> 44.9 us  [fourier(): pl.pallas_call(first_fourier_kernel, grid=(rows // block,), in_specs=[who...]
    ppermute x36, starting transfers between devices: 85.3 us -> 77.3 us  [hop(): return lax.ppermute(value, 'lat', pairs)]
    ppermute x8 -> x9, waiting for transfers between devices: 32.1 us -> 27.2 us  [lon_swap(): return lax.ppermute(value, 'lon', [(i, i ^ bit) for i in range(lon_count)])]
  transfers between devices with their start and end apart: 50 -> 51, of which waited for: 12 -> 10; matrix products, arithmetic and copies ran while one was open for 7% -> 7% of each run, Pallas kernels for 30% -> 24%
where the time goes in v5:
time: 590 us; the launch traced here: 586 us
  Pallas kernels  230 us (39%)
  waiting for transfers between devices  200 us (34%)
  starting transfers between devices  94.9 us (16%)
  other arithmetic  50.6 us (9%)
  local copies, waits for them, and re-layouts  9.33 us (2%)
    ppermute x6, waiting for transfers between devices, send(): lax.ppermute(value, 'lat', [(i, i ^ 1) for i in range(lat_count)])  103 us
    pallas_call x12, Pallas kernels, project(): pl.pallas_call(kernel, grid_spec=pltpu.PrefetchScalarGridSpec(num_scalar_...  95.4 us
    ppermute x36, starting transfers between devices, hop(): return lax.ppermute(value, 'lat', pairs)  77.3 us
    ppermute x36, waiting for transfers between devices, hop(): return lax.ppermute(value, 'lat', pairs)  70.3 us
    pallas_call x3, Pallas kernels, fourier(): pl.pallas_call(second_fourier_kernel, grid=(rows // block,), in_specs=[wh...  47.8 us
    pallas_call x3, Pallas kernels, fourier(): pl.pallas_call(first_fourier_kernel, grid=(rows // block,), in_specs=[who...  44.9 us
    ppermute x9, waiting for transfers between devices, lon_swap(): return lax.ppermute(value, 'lon', [(i, i ^ bit) for i in range(lon_count)])  27.2 us
    pallas_call x6, Pallas kernels, close(): pl.pallas_call(kernel, grid_spec=pltpu.PrefetchScalarGridSpec(num_scalar_...  25.8 us
  transfers between devices with their start and end apart: 51, of which 10 were waited for; matrix products, arithmetic and copies ran while one was open for 7% of the time, Pallas kernels for 24%

profile of v5, /device:TPU:0, one launch (start us, length us, event | category | flops | bytes accessed | tf_op | source)
XLA Modules:
  0.0 586.4 jit_solution(16928750672048346346)
XLA Ops:
  0.8 4.9 cosine_multiply_fusion
  7.6 16.1 %tendencies.1 = (bf16[8,2,256,1024]{3,2,1,0:T(8,128)(2,1)}, bf16[8,2,256,1024]{3,2,1,0:T(8,128)(2,1)}) custom-call(bf16[12,2,2,128,1024]{4,3,2,1,0:T(8,128)(2,1)} %grid_ref.1), custom_call_target="tpu_custom_call" | custom-call | flops 25165824 | bytes 31457280 | tf_op jit(solution)/shard_map/tendencies/pallas_call | solution.py:56
  23.8 1.9 subtract_bitcast_fusion.3
  26.9 13.4 %fourier_first.3 = f32[256,4096]{1,0:T(8,128)} custom-call(bf16[256,1024]{1,0:T(8,128)(2,1)} %get-tuple-element.266.ph_ref, bf16[256,1024]{1,0:T(8,128)(2,1)} %get-tuple-element.265.pl_ref, bf16[4096,1024]{1,0:T(8,128)(2,1)} %bitcast.160, bf16[4096,1024]{1,0:T(8,128)(2,1)} %bitcast.166), custom_call_target="tpu_custom_call" | custom-call | flops 6442450944 | bytes 20971520 | tf_op jit(solution)/shard_map/fourier_first/pallas_call | solution.py:111
  45.7 1.8 fusion.1
  47.8 14.1 %fourier_second.3 = (f32[64,4096]{1,0:T(8,128)}, f32[64,4096]{1,0:T(8,128)}, f32[64,4096]{1,0:T(8,128)}, f32[64,4096]{1,0:T(8,128)}) custom-call(bf16[256,1024]{1,0:T(8,128)(2,1)} %get-tuple-element.268.ph_ref, bf16[256,1024]{1,0:T(8,128)(2,1)} %get-tuple-element.267.pl_ref, bf16[4096,1024]{1,0:T(8,128)(2,1)} %bitcast.161, bf16[4096,1024]{1,0:T(8,128)(2,1)} %bitcast.167, ...), custom_call_target="tpu_custom_call" | custom-call | flops 6442450944 | bytes 20971520 | tf_op jit(solution)/shard_map/fourier_second/pallas_call | solution.py:120
  62.0 13.4 %fourier_first.4 = f32[256,4096]{1,0:T(8,128)} custom-call(bf16[256,1024]{1,0:T(8,128)(2,1)} %get-tuple-element.214.ph_ref, bf16[256,1024]{1,0:T(8,128)(2,1)} %get-tuple-element.213.pl_ref, bf16[4096,1024]{1,0:T(8,128)(2,1)} %bitcast.162, bf16[4096,1024]{1,0:T(8,128)(2,1)} %bitcast.168), custom_call_target="tpu_custom_call" | custom-call | flops 6442450944 | bytes 20971520 | tf_op jit(solution)/shard_map/fourier_first/pallas_call | solution.py:111
  75.3 18.2 %fourier_first.5 = f32[512,4096]{1,0:T(8,128)} custom-call(bf16[512,1024]{1,0:T(8,128)(2,1)} %get-tuple-element.210.ph_ref, bf16[512,1024]{1,0:T(8,128)(2,1)} %get-tuple-element.209.pl_ref, bf16[4096,1024]{1,0:T(8,128)(2,1)} %bitcast.163, bf16[4096,1024]{1,0:T(8,128)(2,1)} %bitcast.169), custom_call_target="tpu_custom_call" | custom-call | flops 12884901888 | bytes 25165824 | tf_op jit(solution)/shard_map/fourier_first/pallas_call | solution.py:111
  94.1 2.9 collective-permute-start.1
  99.0 22.2 %collective-permute-done.1.refs_5_ = f32[64,4096]{1,0:T(8,128)S(1)} collective-permute-done((f32[64,4096]{1,0:T(8,128)}, f32[64,4096]{1,0:T(8,128)S(1)}, u32[]{:S(2)}, u32[]{:S(2)}) %collective-permute-start.1) | collective-permute-done | bytes 1048608 | tf_op jit(solution)/shard_map/ppermute | solution.py:319
  122.2 6.7 %legendre_sent.6 = f32[4,2,32,1280]{3,2,1,0:T(8,128)} custom-call(s32[1]{0:T(128)} %bitcast.56.refs_0_, s32[6]{0:T(128)} %constant.92.clone.refs_1_, s32[6]{0:T(128)} %constant.93.clone.refs_2_, s32[6]{0:T(128)} %constant.94.clone.refs_3_, f32[64,4096]{1,0:T(8,128)} %get-tuple-element.122.refs_4_, f32[64,4096]{1,0:T(8,128)} %copy-done.10, ...), custom_call_target="tpu_custom_call" | custom-call | flops 201326592 | bytes 3801088 | tf_op jit(solution)/shard_map/legendre_sent/pallas_call | solution.py:222
  129.0 14.2 %fourier_second.4 = (f32[128,4096]{1,0:T(8,128)}, f32[128,4096]{1,0:T(8,128)}) custom-call(bf16[256,1024]{1,0:T(8,128)(2,1)} %get-tuple-element.264.ph_ref, bf16[256,1024]{1,0:T(8,128)(2,1)} %get-tuple-element.263.pl_ref, bf16[4096,1024]{1,0:T(8,128)(2,1)} %bitcast.164, bf16[4096,1024]{1,0:T(8,128)(2,1)} %bitcast.170, ...), custom_call_target="tpu_custom_call" | custom-call | flops 6442450944 | bytes 20971520 | tf_op jit(solution)/shard_map/fourier_second/pallas_call | solution.py:120
  143.2 2.0 collective-permute-start.12
  149.0 3.4 fusion
  153.4 6.7 %legendre_sent.7 = f32[4,2,32,1280]{3,2,1,0:T(8,128)} custom-call(s32[1]{0:T(128)} %bitcast.56.refs_0_, s32[6]{0:T(128)} %constant.92.clone.refs_1_, s32[6]{0:T(128)} %constant.93.clone.refs_2_, s32[6]{0:T(128)} %constant.94.clone.refs_3_, f32[64,4096]{1,0:T(8,128)} %get-tuple-element.118.refs_4_, f32[64,4096]{1,0:T(8,128)} %copy-done.9, ...), custom_call_target="tpu_custom_call" | custom-call | flops 201326592 | bytes 3801088 | tf_op jit(solution)/shard_map/legendre_sent/pallas_call | solution.py:222
  160.1 19.5 %fourier_second.5 = (f32[128,4096]{1,0:T(8,128)}, f32[64,4096]{1,0:T(8,128)}, f32[64,4096]{1,0:T(8,128)}, f32[128,4096]{1,0:T(8,128)}, f32[64,4096]{1,0:T(8,128)}, /*index=5*/f32[64,4096]{1,0:T(8,128)}) custom-call(bf16[512,1024]{1,0:T(8,128)(2,1)} %get-tuple-element.212.ph_ref, bf16[512,1024]{1,0:T(8,128)(2,1)} %get-tuple-element.211.pl_ref, ...), custom_call_target="tpu_custom_call" | custom-call | flops 12884901888 | bytes 25165824 | tf_op jit(solution)/shard_map/fourier_second/pallas_call | solution.py:120
  181.3 7.7 %legendre_kept.6 = (f32[4,2,32,1152]{3,2,1,0:T(8,128)}, f32[4,2,32,896]{3,2,1,0:T(8,128)}) custom-call(s32[1]{0:T(128)} %bitcast.7.refs_0_, s32[6]{0:T(128)} %constant.92.clone.refs_1_, s32[6]{0:T(128)} %constant.93.clone.refs_2_, s32[6]{0:T(128)} %constant.94.clone.refs_3_, f32[64,4096]{1,0:T(8,128)} %get-tuple-element.122.refs_4_, f32[64,4096]{1,0:T(8,128)} %copy-done.10, ...), custom_call_target="tpu_custom_call" | custom-call | flops 201326592 | bytes 3801088 | tf_op jit(solution)/shard_map/legendre_kept/pallas_call | solution.py:222
  189.0 3.1 collective-permute-done.12.refs_5_
  192.0 8.7 %legendre_sent.8 = f32[8,2,32,1280]{3,2,1,0:T(8,128)} custom-call(s32[1]{0:T(128)} %bitcast.56.refs_0_, s32[6]{0:T(128)} %constant.92.clone.refs_1_, s32[6]{0:T(128)} %constant.93.clone.refs_2_, s32[6]{0:T(128)} %constant.94.clone.refs_3_, f32[128,4096]{1,0:T(8,128)} %get-tuple-element.127.refs_4_, f32[128,4096]{1,0:T(8,128)} %collective-permute-done.12.refs_5_, ...), custom_call_target="tpu_custom_call" | custom-call | flops 402653184 | bytes 7602176 | tf_op jit(solution)/shard_map/legendre_sent/pallas_call | solution.py:222
  200.7 2.0 collective-permute-start.13
  202.7 1.7 collective-permute-start.6
  204.4 4.9 collective-permute-start.8
  209.3 74.7 %collective-permute-done.18.refs_7_ = f32[4,2,32,1280]{3,2,1,0:T(8,128)} collective-permute-done((f32[4,2,32,1280]{3,2,1,0:T(8,128)}, f32[4,2,32,1280]{3,2,1,0:T(8,128)}, u32[]{:S(2)}, u32[]{:S(2)}) %collective-permute-start.18) | collective-permute-done | bytes 1310752 | tf_op jit(solution)/shard_map/ppermute | solution.py:358
  284.0 7.6 %legendre_kept.8 = (f32[4,2,32,1152]{3,2,1,0:T(8,128)}, f32[4,2,32,896]{3,2,1,0:T(8,128)}) custom-call(s32[1]{0:T(128)} %bitcast.7.refs_0_, s32[6]{0:T(128)} %constant.92.clone.refs_1_, s32[6]{0:T(128)} %constant.93.clone.refs_2_, s32[6]{0:T(128)} %constant.94.clone.refs_3_, f32[64,4096]{1,0:T(8,128)} %get-tuple-element.118.refs_4_, f32[64,4096]{1,0:T(8,128)} %copy-done.9, ...), custom_call_target="tpu_custom_call" | custom-call | flops 201326592 | bytes 3801088 | tf_op jit(solution)/shard_map/legendre_kept/pallas_call | solution.py:222
  291.7 1.7 collective-permute-start.19
  293.4 3.8 collective-permute-start.20
  297.2 8.7 %legendre_sent.9 = f32[8,2,32,1280]{3,2,1,0:T(8,128)} custom-call(s32[1]{0:T(128)} %bitcast.56.refs_0_, s32[6]{0:T(128)} %constant.92.clone.refs_1_, s32[6]{0:T(128)} %constant.93.clone.refs_2_, s32[6]{0:T(128)} %constant.94.clone.refs_3_, f32[128,4096]{1,0:T(8,128)} %get-tuple-element.135.refs_4_, f32[128,4096]{1,0:T(8,128)} %copy-done.2, ...), custom_call_target="tpu_custom_call" | custom-call | flops 402653184 | bytes 7602176 | tf_op jit(solution)/shard_map/legendre_sent/pallas_call | solution.py:222
  307.4 1.9 slice_add_fusion.17
  310.8 1.6 slice_add_fusion.7.refs_3_
  312.4 10.3 %legendre_kept.7 = (f32[8,2,32,1152]{3,2,1,0:T(8,128)}, f32[8,2,32,896]{3,2,1,0:T(8,128)}) custom-call(s32[1]{0:T(128)} %bitcast.7.refs_0_, s32[6]{0:T(128)} %constant.92.clone.refs_1_, s32[6]{0:T(128)} %constant.93.clone.refs_2_, s32[6]{0:T(128)} %constant.94.clone.refs_3_, f32[128,4096]{1,0:T(8,128)} %get-tuple-element.127.refs_4_, ...), custom_call_target="tpu_custom_call" | custom-call | flops 402653184 | bytes 7602176 | tf_op jit(solution)/shard_map/legendre_kept/pallas_call | solution.py:222
  324.2 2.5 collective-permute-start.16
  326.8 1.5 collective-permute-done.37.refs_5_
  329.0 2.5 slice_add_fusion.6.refs_4_
  331.5 1.6 collective-permute-start.27
  333.1 1.9 slice_add_fusion.16
  337.3 21.5 %collective-permute-done.22.refs_7_ = f32[8,2,32,1280]{3,2,1,0:T(8,128)} collective-permute-done((f32[8,2,32,1280]{3,2,1,0:T(8,128)}, f32[8,2,32,1280]{3,2,1,0:T(8,128)}, u32[]{:S(2)}, u32[]{:S(2)}) %collective-permute-start.22) | collective-permute-done | bytes 2621472 | tf_op jit(solution)/shard_map/ppermute | solution.py:358
  361.3 6.7 %legendre_sent.11 = f32[4,2,32,1280]{3,2,1,0:T(8,128)} custom-call(s32[1]{0:T(128)} %bitcast.56.refs_0_, s32[6]{0:T(128)} %constant.92.clone.refs_1_, s32[6]{0:T(128)} %constant.93.clone.refs_2_, s32[6]{0:T(128)} %constant.94.clone.refs_3_, f32[64,4096]{1,0:T(8,128)} %get-tuple-element.186.refs_4_, f32[64,4096]{1,0:T(8,128)} %collective-permute-done.37.refs_5_, ...), custom_call_target="tpu_custom_call" | custom-call | flops 201326592 | bytes 3801088 | tf_op jit(solution)/shard_map/legendre_sent/pallas_call | solution.py:222
  368.0 10.3 %legendre_kept.9 = (f32[8,2,32,1152]{3,2,1,0:T(8,128)}, f32[8,2,32,896]{3,2,1,0:T(8,128)}) custom-call(s32[1]{0:T(128)} %bitcast.7.refs_0_, s32[6]{0:T(128)} %constant.92.clone.refs_1_, s32[6]{0:T(128)} %constant.93.clone.refs_2_, s32[6]{0:T(128)} %constant.94.clone.refs_3_, f32[128,4096]{1,0:T(8,128)} %get-tuple-element.135.refs_4_, f32[128,4096]{1,0:T(8,128)} %copy-done.2, ...), custom_call_target="tpu_custom_call" | custom-call | flops 402653184 | bytes 7602176 | tf_op jit(solution)/shard_map/legendre_kept/pallas_call | solution.py:222
  379.8 2.0 collective-permute-start.23
  383.3 2.6 collective-permute-start.24
  385.9 2.3 slice_add_fusion.1.refs_4_
  388.2 2.0 collective-permute-start.15
  392.4 1.6 slice_add_fusion.22
  394.1 6.7 %legendre_sent.10 = f32[4,2,32,1280]{3,2,1,0:T(8,128)} custom-call(s32[1]{0:T(128)} %bitcast.56.refs_0_, s32[6]{0:T(128)} %constant.92.clone.refs_1_, s32[6]{0:T(128)} %constant.93.clone.refs_2_, s32[6]{0:T(128)} %constant.94.clone.refs_3_, f32[64,4096]{1,0:T(8,128)} %get-tuple-element.140.refs_4_, f32[64,4096]{1,0:T(8,128)} %collective-permute-done.25.refs_5_, ...), custom_call_target="tpu_custom_call" | custom-call | flops 201326592 | bytes 3801088 | tf_op jit(solution)/shard_map/legendre_sent/pallas_call | solution.py:222
  400.8 6.4 %collective-permute-done.38.refs_7_ = f32[4,2,32,1280]{3,2,1,0:T(8,128)} collective-permute-done((f32[4,2,32,1280]{3,2,1,0:T(8,128)}, f32[4,2,32,1280]{3,2,1,0:T(8,128)}, u32[]{:S(2)}, u32[]{:S(2)}) %collective-permute-start.38) | collective-permute-done | bytes 1310752 | tf_op jit(solution)/shard_map/ppermute | solution.py:358
  408.8 2.1 slice_add_fusion.12.refs_5_
  410.8 7.6 %legendre_kept.11 = (f32[4,2,32,1152]{3,2,1,0:T(8,128)}, f32[4,2,32,896]{3,2,1,0:T(8,128)}) custom-call(s32[1]{0:T(128)} %bitcast.7.refs_0_, s32[6]{0:T(128)} %constant.92.clone.refs_1_, s32[6]{0:T(128)} %constant.93.clone.refs_2_, s32[6]{0:T(128)} %constant.94.clone.refs_3_, f32[64,4096]{1,0:T(8,128)} %get-tuple-element.186.refs_4_, ...), custom_call_target="tpu_custom_call" | custom-call | flops 201326592 | bytes 3801088 | tf_op jit(solution)/shard_map/legendre_kept/pallas_call | solution.py:222
  418.5 1.7 collective-permute-start.39
  420.9 4.8 collective-permute-start.41
  425.7 2.4 slice_add_fusion.8
  428.1 2.5 slice_add_fusion.3.refs_5_
  430.6 1.8 slice_add_fusion.refs_4_
  432.4 7.6 %legendre_kept.10 = (f32[4,2,32,1152]{3,2,1,0:T(8,128)}, f32[4,2,32,896]{3,2,1,0:T(8,128)}) custom-call(s32[1]{0:T(128)} %bitcast.7.refs_0_, s32[6]{0:T(128)} %constant.92.clone.refs_1_, s32[6]{0:T(128)} %constant.93.clone.refs_2_, s32[6]{0:T(128)} %constant.94.clone.refs_3_, f32[64,4096]{1,0:T(8,128)} %get-tuple-element.140.refs_4_, ...), custom_call_target="tpu_custom_call" | custom-call | flops 201326592 | bytes 3801088 | tf_op jit(solution)/shard_map/legendre_kept/pallas_call | solution.py:222
  441.8 1.6 slice_add_fusion.5.refs_4_
  448.2 25.3 %collective-permute-start.47 = (f32[4,2,32,896]{3,2,1,0:T(8,128)S(1)}, f32[4,2,32,896]{3,2,1,0:T(8,128)S(1)}, u32[]{:S(2)}, u32[]{:S(2)}) collective-permute-start(f32[4,2,32,896]{3,2,1,0:T(8,128)S(1)} %copy-done.22), channel_id=1, source_target_pairs={{0,2},{1,3},{8,10},{9,11},{16,18},{17,19},{24,26},{25,27}} | collective-permute-start | bytes 2752520 | tf_op jit(solution)/shard_map/ppermute | solution.py:245
  474.3 4.0 collective-permute-done.29.refs_8_
  482.2 35.5 %collective-permute-done.10.refs_7_ = f32[4,2,32,512]{3,2,1,0:T(8,128)S(1)} collective-permute-done((f32[4,2,32,512]{3,2,1,0:T(8,128)S(1)}, f32[4,2,32,512]{3,2,1,0:T(8,128)S(1)}, u32[]{:S(2)}, u32[]{:S(2)}) %collective-permute-start.10) | collective-permute-done | bytes 524320 | tf_op jit(solution)/shard_map/ppermute | solution.py:245
  527.4 30.7 %collective-permute-done.43.refs_8_ = f32[4,2,32,512]{3,2,1,0:T(8,128)S(1)} collective-permute-done((f32[4,2,32,512]{3,2,1,0:T(8,128)S(1)}, f32[4,2,32,512]{3,2,1,0:T(8,128)S(1)}, u32[]{:S(2)}, u32[]{:S(2)}) %collective-permute-start.43) | collective-permute-done | bytes 524320 | tf_op jit(solution)/shard_map/ppermute | solution.py:245
  559.5 4.1 close.6.refs_2_
  563.5 4.1 close.7.refs_2_
  567.7 4.8 close.8.refs_2_
  573.5 4.7 close.9.refs_2_
  578.1 4.1 close.10.refs_2_
  582.2 4.1 close.11
  (233 shorter events, 59.7 us)
Async XLA Ops:
  40.2 7.6 %collective-permute-start = (f32[256,4096]{1,0:T(8,128)}, f32[256,4096]{1,0:T(8,128)}, u32[]{:S(2)}, u32[]{:S(2)}) collective-permute-start(f32[256,4096]{1,0:T(8,128)} %fourier_first.3), channel_id=1, source_target_pairs={{0,8},{8,0},{16,24},{24,16},{1,9},{9,1},{17,25},{25,17},{2,10},{10... | collective-permute-start | bytes 12582920 | tf_op jit(solution)/shard_map/ppermute | solution.py:319
  93.6 66.6 %collective-permute-start.4 = (f32[512,4096]{1,0:T(8,128)}, f32[512,4096]{1,0:T(8,128)}, u32[]{:S(2)}, u32[]{:S(2)}) collective-permute-start(f32[512,4096]{1,0:T(8,128)} %fourier_first.5), channel_id=1, source_target_pairs={{0,8},{8,0},{16,24},{24,16},{1,9},{9,1},{17,25},{25,17},{2,10},{10... | collective-permute-start | bytes 25165832 | tf_op jit(solution)/shard_map/ppermute | solution.py:319
  94.0 35.0 %collective-permute-start.2 = (f32[256,4096]{1,0:T(8,128)}, f32[256,4096]{1,0:T(8,128)}, u32[]{:S(2)}, u32[]{:S(2)}) collective-permute-start(f32[256,4096]{1,0:T(8,128)} %fourier_first.4), channel_id=1, source_target_pairs={{0,8},{8,0},{16,24},{24,16},{1,9},{9,1},{17,25},{25,17},{2,10},{10... | collective-permute-start | bytes 12582920 | tf_op jit(solution)/shard_map/ppermute | solution.py:319
  94.1 27.1 %collective-permute-start.1 = (f32[64,4096]{1,0:T(8,128)}, f32[64,4096]{1,0:T(8,128)S(1)}, u32[]{:S(2)}, u32[]{:S(2)}) collective-permute-start(f32[64,4096]{1,0:T(8,128)} %get-tuple-element.115), channel_id=1, source_target_pairs={{0,16},{8,24},{16,0},{24,8},{1,17},{9,25},{17,1},{25,9},{2,18},{10... | collective-permute-start | bytes 3145736 | tf_op jit(solution)/shard_map/ppermute | solution.py:319
  99.0 53.4 %collective-permute-start.3 = (f32[64,4096]{1,0:T(8,128)}, f32[64,4096]{1,0:T(8,128)S(1)}, u32[]{:S(2)}, u32[]{:S(2)}) collective-permute-start(f32[64,4096]{1,0:T(8,128)} %get-tuple-element.119), channel_id=1, source_target_pairs={{0,16},{8,24},{16,0},{24,8},{1,17},{9,25},{17,1},{25,9},{2,18},{10... | collective-permute-start | bytes 3145736 | tf_op jit(solution)/shard_map/ppermute | solution.py:319
  143.2 48.8 %collective-permute-start.12 = (f32[128,4096]{1,0:T(8,128)}, f32[128,4096]{1,0:T(8,128)}, u32[]{:S(2)}, u32[]{:S(2)}) collective-permute-start(f32[128,4096]{1,0:T(8,128)} %get-tuple-element.126), channel_id=1, source_target_pairs={{0,16},{8,24},{16,0},{24,8},{1,17},{9,25},{17,1},{25,9},{2,18},{10... | collective-permute-start | bytes 6291464 | tf_op jit(solution)/shard_map/ppermute | solution.py:319
  147.5 32.6 %collective-permute-start.5 = (f32[4,2,32,1280]{3,2,1,0:T(8,128)}, f32[4,2,32,1280]{3,2,1,0:T(8,128)S(1)}, u32[]{:S(2)}, u32[]{:S(2)}) collective-permute-start(f32[4,2,32,1280]{3,2,1,0:T(8,128)} %legendre_sent.6), channel_id=1, source_target_pairs={{0,1},{1,0},{2,3},{3,2},{4,5},{5,4},{6,7},{7,6},{8,9},{9,8},{10,11... | collective-permute-start | bytes 3932168 | tf_op jit(solution)/shard_map/ppermute | solution.py:358
  179.6 113.7 %collective-permute-start.21 = (f32[128,4096]{1,0:T(8,128)}, f32[128,4096]{1,0:T(8,128)S(1)}, u32[]{:S(2)}, u32[]{:S(2)}) collective-permute-start(f32[128,4096]{1,0:T(8,128)} %get-tuple-element.134), channel_id=1, source_target_pairs={{0,16},{8,24},{16,0},{24,8},{1,17},{9,25},{17,1},{25,9},{2,18},{10... | collective-permute-start | bytes 6291464 | tf_op jit(solution)/shard_map/ppermute | solution.py:319
  200.7 111.7 %collective-permute-start.13 = (f32[8,2,32,1280]{3,2,1,0:T(8,128)}, f32[8,2,32,1280]{3,2,1,0:T(8,128)}, u32[]{:S(2)}, u32[]{:S(2)}) collective-permute-start(f32[8,2,32,1280]{3,2,1,0:T(8,128)} %legendre_sent.8), channel_id=1, source_target_pairs={{0,1},{1,0},{2,3},{3,2},{4,5},{5,4},{6,7},{7,6},{8,9},{9,8},{10,11... | collective-permute-start | bytes 7864328 | tf_op jit(solution)/shard_map/ppermute | solution.py:358
  202.7 81.4 %collective-permute-start.18 = (f32[4,2,32,1280]{3,2,1,0:T(8,128)}, f32[4,2,32,1280]{3,2,1,0:T(8,128)}, u32[]{:S(2)}, u32[]{:S(2)}) collective-permute-start(f32[4,2,32,1280]{3,2,1,0:T(8,128)} %legendre_sent.7), channel_id=1, source_target_pairs={{0,1},{1,0},{2,3},{3,2},{4,5},{5,4},{6,7},{7,6},{8,9},{9,8},{10,11... | collective-permute-start | bytes 3932168 | tf_op jit(solution)/shard_map/ppermute | solution.py:358
  202.7 106.6 %collective-permute-start.6 = (f32[4,2,32,1152]{3,2,1,0:T(8,128)S(1)}, f32[4,2,32,1152]{3,2,1,0:T(8,128)}, u32[]{:S(2)}, u32[]{:S(2)}) collective-permute-start(f32[4,2,32,1152]{3,2,1,0:T(8,128)S(1)} %copy-done.12), channel_id=1, source_target_pairs={{6,4},{7,5},{14,12},{15,13},{22,20},{23,21},{30,28},{31,29}} | collective-permute-start | bytes 3538952 | tf_op jit(solution)/shard_map/ppermute | solution.py:245
  204.4 101.5 %collective-permute-start.8 = (f32[4,2,32,896]{3,2,1,0:T(8,128)}, f32[4,2,32,896]{3,2,1,0:T(8,128)}, u32[]{:S(2)}, u32[]{:S(2)}) collective-permute-start(f32[4,2,32,896]{3,2,1,0:T(8,128)} %get-tuple-element.149.refs_8_), channel_id=1, source_target_pairs={{0,2},{1,3},{8,10},{9,11},{16,18},{17,19},{24,26},{25,27}} | collective-permute-start | bytes 2752520 | tf_op jit(solution)/shard_map/ppermute | solution.py:245
  291.7 32.6 %collective-permute-start.19 = (f32[4,2,32,1152]{3,2,1,0:T(8,128)}, f32[4,2,32,1152]{3,2,1,0:T(8,128)}, u32[]{:S(2)}, u32[]{:S(2)}) collective-permute-start(f32[4,2,32,1152]{3,2,1,0:T(8,128)} %get-tuple-element.153.refs_3_), channel_id=1, source_target_pairs={{6,4},{7,5},{14,12},{15,13},{22,20},{23,21},{30,28},{31,29}} | collective-permute-start | bytes 3538952 | tf_op jit(solution)/shard_map/ppermute | solution.py:245
  293.4 30.1 %collective-permute-start.20 = (f32[4,2,32,896]{3,2,1,0:T(8,128)}, f32[4,2,32,896]{3,2,1,0:T(8,128)}, u32[]{:S(2)}, u32[]{:S(2)}) collective-permute-start(f32[4,2,32,896]{3,2,1,0:T(8,128)} %get-tuple-element.159.refs_9_), channel_id=1, source_target_pairs={{0,2},{1,3},{8,10},{9,11},{16,18},{17,19},{24,26},{25,27}} | collective-permute-start | bytes 2752520 | tf_op jit(solution)/shard_map/ppermute | solution.py:245
  305.9 53.0 %collective-permute-start.22 = (f32[8,2,32,1280]{3,2,1,0:T(8,128)}, f32[8,2,32,1280]{3,2,1,0:T(8,128)}, u32[]{:S(2)}, u32[]{:S(2)}) collective-permute-start(f32[8,2,32,1280]{3,2,1,0:T(8,128)} %legendre_sent.9), channel_id=1, source_target_pairs={{0,1},{1,0},{2,3},{3,2},{4,5},{5,4},{6,7},{7,6},{8,9},{9,8},{10,11... | collective-permute-start | bytes 7864328 | tf_op jit(solution)/shard_map/ppermute | solution.py:358
  309.3 19.0 %collective-permute-start.37 = (f32[64,4096]{1,0:T(8,128)}, f32[64,4096]{1,0:T(8,128)}, u32[]{:S(2)}, u32[]{:S(2)}) collective-permute-start(f32[64,4096]{1,0:T(8,128)} %get-tuple-element.185), channel_id=1, source_target_pairs={{0,16},{8,24},{16,0},{24,8},{1,17},{9,25},{17,1},{25,9},{2,18},{10... | collective-permute-start | bytes 3145736 | tf_op jit(solution)/shard_map/ppermute | solution.py:319
  312.4 48.0 %copy-start.5 = (f32[4,2,32,896]{3,2,1,0:T(8,128)}, f32[4,2,32,896]{3,2,1,0:T(8,128)S(1)}, u32[]{:S(2)}) copy-start(f32[4,2,32,896]{3,2,1,0:T(8,128)S(1)} %slice_add_fusion.7.refs_3_) | copy-start | bytes 2752516
  322.7 59.2 %collective-permute-start.14 = (f32[8,2,32,1152]{3,2,1,0:T(8,128)}, f32[8,2,32,1152]{3,2,1,0:T(8,128)S(1)}, u32[]{:S(2)}, u32[]{:S(2)}) collective-permute-start(f32[8,2,32,1152]{3,2,1,0:T(8,128)} %get-tuple-element.163.refs_3_), channel_id=1, source_target_pairs={{6,4},{7,5},{14,12},{15,13},{22,20},{23,21},{30,28},{31,29}} | collective-permute-start | bytes 7077896 | tf_op jit(solution)/shard_map/ppermute | solution.py:245
  323.5 11.5 %collective-permute-start.7 = (f32[4,2,32,896]{3,2,1,0:T(8,128)S(1)}, f32[4,2,32,896]{3,2,1,0:T(8,128)S(1)}, u32[]{:S(2)}, u32[]{:S(2)}) collective-permute-start(f32[4,2,32,896]{3,2,1,0:T(8,128)S(1)} %slice_add_fusion.7.refs_3_), channel_id=1, source_target_pairs={{4,2},{5,3},{12,10},{13,11},{20,18},{21,19},{28,26},{29,27}} | collective-permute-start | bytes 2752520 | tf_op jit(solution)/shard_map/ppermute | solution.py:245
  324.2 64.0 %collective-permute-start.16 = (f32[8,2,32,896]{3,2,1,0:T(8,128)}, f32[8,2,32,896]{3,2,1,0:T(8,128)}, u32[]{:S(2)}, u32[]{:S(2)}) collective-permute-start(f32[8,2,32,896]{3,2,1,0:T(8,128)} %get-tuple-element.169.refs_9_), channel_id=1, source_target_pairs={{0,2},{1,3},{8,10},{9,11},{16,18},{17,19},{24,26},{25,27}} | collective-permute-start | bytes 5505032 | tf_op jit(solution)/shard_map/ppermute | solution.py:245
  328.3 3.2 collective-permute-start.9
  331.5 48.3 %collective-permute-start.27 = (f32[4,2,32,896]{3,2,1,0:T(8,128)}, f32[4,2,32,896]{3,2,1,0:T(8,128)}, u32[]{:S(2)}, u32[]{:S(2)}) collective-permute-start(f32[4,2,32,896]{3,2,1,0:T(8,128)} %slice_add_fusion.6.refs_4_), channel_id=1, source_target_pairs={{4,2},{5,3},{12,10},{13,11},{20,18},{21,19},{28,26},{29,27}} | collective-permute-start | bytes 2752520 | tf_op jit(solution)/shard_map/ppermute | solution.py:245
  335.0 43.3 %collective-permute-start.28 = (f32[4,2,32,384]{3,2,1,0:T(8,128)}, f32[4,2,32,384]{3,2,1,0:T(8,128)}, u32[]{:S(2)}, u32[]{:S(2)}) collective-permute-start(f32[4,2,32,384]{3,2,1,0:T(8,128)} %slice_add_fusion.16), channel_id=1, source_target_pairs={{2,4},{3,5},{10,12},{11,13},{18,20},{19,21},{26,28},{27,29}} | collective-permute-start | bytes 1179656 | tf_op jit(solution)/shard_map/ppermute | solution.py:245
  358.9 32.8 %collective-permute-start.25 = (f32[64,4096]{1,0:T(8,128)}, f32[64,4096]{1,0:T(8,128)}, u32[]{:S(2)}, u32[]{:S(2)}) collective-permute-start(f32[64,4096]{1,0:T(8,128)} %get-tuple-element.139), channel_id=1, source_target_pairs={{0,16},{8,24},{16,0},{24,8},{1,17},{9,25},{17,1},{25,9},{2,18},{10... | collective-permute-start | bytes 3145736 | tf_op jit(solution)/shard_map/ppermute | solution.py:319
  378.3 28.9 %collective-permute-start.38 = (f32[4,2,32,1280]{3,2,1,0:T(8,128)}, f32[4,2,32,1280]{3,2,1,0:T(8,128)}, u32[]{:S(2)}, u32[]{:S(2)}) collective-permute-start(f32[4,2,32,1280]{3,2,1,0:T(8,128)} %legendre_sent.11), channel_id=1, source_target_pairs={{0,1},{1,0},{2,3},{3,2},{4,5},{5,4},{6,7},{7,6},{8,9},{9,8},{10,11... | collective-permute-start | bytes 3932168 | tf_op jit(solution)/shard_map/ppermute | solution.py:358
  379.8 50.8 %collective-permute-start.23 = (f32[8,2,32,1152]{3,2,1,0:T(8,128)}, f32[8,2,32,1152]{3,2,1,0:T(8,128)}, u32[]{:S(2)}, u32[]{:S(2)}) collective-permute-start(f32[8,2,32,1152]{3,2,1,0:T(8,128)} %get-tuple-element.173.refs_3_), channel_id=1, source_target_pairs={{6,4},{7,5},{14,12},{15,13},{22,20},{23,21},{30,28},{31,29}} | collective-permute-start | bytes 7077896 | tf_op jit(solution)/shard_map/ppermute | solution.py:245
  383.3 37.6 %collective-permute-start.24 = (f32[8,2,32,896]{3,2,1,0:T(8,128)}, f32[8,2,32,896]{3,2,1,0:T(8,128)}, u32[]{:S(2)}, u32[]{:S(2)}) collective-permute-start(f32[8,2,32,896]{3,2,1,0:T(8,128)} %get-tuple-element.179.refs_9_), channel_id=1, source_target_pairs={{0,2},{1,3},{8,10},{9,11},{16,18},{17,19},{24,26},{25,27}} | collective-permute-start | bytes 5505032 | tf_op jit(solution)/shard_map/ppermute | solution.py:245
  388.2 39.9 %copy-start = (f32[8,2,32,896]{3,2,1,0:T(8,128)}, f32[8,2,32,896]{3,2,1,0:T(8,128)S(1)}, u32[]{:S(2)}) copy-start(f32[8,2,32,896]{3,2,1,0:T(8,128)S(1)} %slice_add_fusion.1.refs_4_) | copy-start | bytes 5505028
  388.2 39.9 %collective-permute-start.15 = (f32[8,2,32,896]{3,2,1,0:T(8,128)S(1)}, f32[8,2,32,896]{3,2,1,0:T(8,128)}, u32[]{:S(2)}, u32[]{:S(2)}) collective-permute-start(f32[8,2,32,896]{3,2,1,0:T(8,128)S(1)} %slice_add_fusion.1.refs_4_), channel_id=1, source_target_pairs={{4,2},{5,3},{12,10},{13,11},{20,18},{21,19},{28,26},{29,27}} | collective-permute-start | bytes 5505032 | tf_op jit(solution)/shard_map/ppermute | solution.py:245
  391.7 26.8 %collective-permute-start.17 = (f32[8,2,32,384]{3,2,1,0:T(8,128)S(1)}, f32[8,2,32,384]{3,2,1,0:T(8,128)S(1)}, u32[]{:S(2)}, u32[]{:S(2)}) collective-permute-start(f32[8,2,32,384]{3,2,1,0:T(8,128)S(1)} %slice_add_fusion.9), channel_id=1, source_target_pairs={{2,4},{3,5},{10,12},{11,13},{18,20},{19,21},{26,28},{27,29}} | collective-permute-start | bytes 2359304 | tf_op jit(solution)/shard_map/ppermute | solution.py:245
  407.2 25.2 %collective-permute-start.26 = (f32[4,2,32,1280]{3,2,1,0:T(8,128)}, f32[4,2,32,1280]{3,2,1,0:T(8,128)}, u32[]{:S(2)}, u32[]{:S(2)}) collective-permute-start(f32[4,2,32,1280]{3,2,1,0:T(8,128)} %legendre_sent.10), channel_id=1, source_target_pairs={{0,1},{1,0},{2,3},{3,2},{4,5},{5,4},{6,7},{7,6},{8,9},{9,8},{10,11... | collective-permute-start | bytes 3932168 | tf_op jit(solution)/shard_map/ppermute | solution.py:358
  418.5 23.3 %collective-permute-start.39 = (f32[4,2,32,1152]{3,2,1,0:T(8,128)}, f32[4,2,32,1152]{3,2,1,0:T(8,128)}, u32[]{:S(2)}, u32[]{:S(2)}) collective-permute-start(f32[4,2,32,1152]{3,2,1,0:T(8,128)} %get-tuple-element.189.refs_3_), channel_id=1, source_target_pairs={{6,4},{7,5},{14,12},{15,13},{22,20},{23,21},{30,28},{31,29}} | collective-permute-start | bytes 3538952 | tf_op jit(solution)/shard_map/ppermute | solution.py:245
  420.9 24.0 %collective-permute-start.41 = (f32[4,2,32,896]{3,2,1,0:T(8,128)}, f32[4,2,32,896]{3,2,1,0:T(8,128)}, u32[]{:S(2)}, u32[]{:S(2)}) collective-permute-start(f32[4,2,32,896]{3,2,1,0:T(8,128)} %get-tuple-element.195.refs_9_), channel_id=1, source_target_pairs={{0,2},{1,3},{8,10},{9,11},{16,18},{17,19},{24,26},{25,27}} | collective-permute-start | bytes 2752520 | tf_op jit(solution)/shard_map/ppermute | solution.py:245
  432.4 49.5 %copy-start.1 = (f32[8,2,32,896]{3,2,1,0:T(8,128)}, f32[8,2,32,896]{3,2,1,0:T(8,128)S(1)}, u32[]{:S(2)}) copy-start(f32[8,2,32,896]{3,2,1,0:T(8,128)S(1)} %slice_add_fusion.refs_4_) | copy-start | bytes 5505028
  440.1 8.0 %collective-permute-start.45 = (f32[4,2,32,1152]{3,2,1,0:T(8,128)}, f32[4,2,32,1152]{3,2,1,0:T(8,128)S(1)}, u32[]{:S(2)}, u32[]{:S(2)}) collective-permute-start(f32[4,2,32,1152]{3,2,1,0:T(8,128)} %get-tuple-element.199.refs_3_), channel_id=1, source_target_pairs={{6,4},{7,5},{14,12},{15,13},{22,20},{23,21},{30,28},{31,29}} | collective-permute-start | bytes 3538952 | tf_op jit(solution)/shard_map/ppermute | solution.py:245
  441.0 40.2 %collective-permute-start.33 = (f32[8,2,32,896]{3,2,1,0:T(8,128)S(1)}, f32[8,2,32,896]{3,2,1,0:T(8,128)S(1)}, u32[]{:S(2)}, u32[]{:S(2)}) collective-permute-start(f32[8,2,32,896]{3,2,1,0:T(8,128)S(1)} %slice_add_fusion.refs_4_), channel_id=1, source_target_pairs={{4,2},{5,3},{12,10},{13,11},{20,18},{21,19},{28,26},{29,27}} | collective-permute-start | bytes 5505032 | tf_op jit(solution)/shard_map/ppermute | solution.py:245
  443.3 35.7 %collective-permute-start.40 = (f32[4,2,32,896]{3,2,1,0:T(8,128)S(1)}, f32[4,2,32,896]{3,2,1,0:T(8,128)S(1)}, u32[]{:S(2)}, u32[]{:S(2)}) collective-permute-start(f32[4,2,32,896]{3,2,1,0:T(8,128)S(1)} %slice_add_fusion.5.refs_4_), channel_id=1, source_target_pairs={{4,2},{5,3},{12,10},{13,11},{20,18},{21,19},{28,26},{29,27}} | collective-permute-start | bytes 2752520 | tf_op jit(solution)/shard_map/ppermute | solution.py:245
  444.2 2.6 collective-permute-start.30
  446.1 27.5 %collective-permute-start.42 = (f32[4,2,32,384]{3,2,1,0:T(8,128)S(1)}, f32[4,2,32,384]{3,2,1,0:T(8,128)S(1)}, u32[]{:S(2)}, u32[]{:S(2)}) collective-permute-start(f32[4,2,32,384]{3,2,1,0:T(8,128)S(1)} %slice_add_fusion.15), channel_id=1, source_target_pairs={{2,4},{3,5},{10,12},{11,13},{18,20},{19,21},{26,28},{27,29}} | collective-permute-start | bytes 1179656 | tf_op jit(solution)/shard_map/ppermute | solution.py:245
  446.8 31.6 %collective-permute-start.29 = (f32[4,2,32,512]{3,2,1,0:T(8,128)S(1)}, f32[4,2,32,512]{3,2,1,0:T(8,128)S(1)}, u32[]{:S(2)}, u32[]{:S(2)}) collective-permute-start(f32[4,2,32,512]{3,2,1,0:T(8,128)S(1)} %copy-done.19), channel_id=1, source_target_pairs={{2,0},{3,1},{10,8},{11,9},{18,16},{19,17},{26,24},{27,25}} | collective-permute-start | bytes 1572872 | tf_op jit(solution)/shard_map/ppermute | solution.py:245
  448.2 71.5 %collective-permute-start.47 = (f32[4,2,32,896]{3,2,1,0:T(8,128)S(1)}, f32[4,2,32,896]{3,2,1,0:T(8,128)S(1)}, u32[]{:S(2)}, u32[]{:S(2)}) collective-permute-start(f32[4,2,32,896]{3,2,1,0:T(8,128)S(1)} %copy-done.22), channel_id=1, source_target_pairs={{0,2},{1,3},{8,10},{9,11},{16,18},{17,19},{24,26},{25,27}} | collective-permute-start | bytes 2752520 | tf_op jit(solution)/shard_map/ppermute | solution.py:245
  473.5 49.6 %copy-start.7 = (f32[4,2,32,896]{3,2,1,0:T(8,128)}, f32[4,2,32,896]{3,2,1,0:T(8,128)S(1)}, u32[]{:S(2)}) copy-start(f32[4,2,32,896]{3,2,1,0:T(8,128)S(1)} %slice_add_fusion.4.refs_4_) | copy-start | bytes 2752516
  473.6 48.8 %collective-permute-start.46 = (f32[4,2,32,896]{3,2,1,0:T(8,128)S(1)}, f32[4,2,32,896]{3,2,1,0:T(8,128)S(1)}, u32[]{:S(2)}, u32[]{:S(2)}) collective-permute-start(f32[4,2,32,896]{3,2,1,0:T(8,128)S(1)} %slice_add_fusion.4.refs_4_), channel_id=1, source_target_pairs={{4,2},{5,3},{12,10},{13,11},{20,18},{21,19},{28,26},{29,27}} | collective-permute-start | bytes 2752520 | tf_op jit(solution)/shard_map/ppermute | solution.py:245
  478.4 2.1 collective-permute-start.11
  479.1 38.6 %collective-permute-start.10 = (f32[4,2,32,512]{3,2,1,0:T(8,128)S(1)}, f32[4,2,32,512]{3,2,1,0:T(8,128)S(1)}, u32[]{:S(2)}, u32[]{:S(2)}) collective-permute-start(f32[4,2,32,512]{3,2,1,0:T(8,128)S(1)} %copy-done.18), channel_id=1, source_target_pairs={{2,0},{3,1},{10,8},{11,9},{18,16},{19,17},{26,24},{27,25}} | collective-permute-start | bytes 1572872 | tf_op jit(solution)/shard_map/ppermute | solution.py:245
  480.5 40.6 %copy-start.20 = (f32[4,2,32,512]{3,2,1,0:T(8,128)}, f32[4,2,32,512]{3,2,1,0:T(8,128)S(1)}, u32[]{:S(2)}) copy-start(f32[4,2,32,512]{3,2,1,0:T(8,128)S(1)} %slice_add_fusion.11.refs_5_) | copy-start | bytes 1572868
  480.5 39.2 %copy-start.40 = (f32[4,2,32,128]{3,2,1,0:T(8,128)}, f32[4,2,32,128]{3,2,1,0:T(8,128)S(1)}, u32[]{:S(2)}) copy-start(f32[4,2,32,128]{3,2,1,0:T(8,128)S(1)} %collective-permute-done.11.refs_11_) | copy-start | bytes 393220
  480.5 37.8 %collective-permute-start.32 = (f32[8,2,32,128]{3,2,1,0:T(8,128)S(1)}, f32[8,2,32,128]{3,2,1,0:T(8,128)S(1)}, u32[]{:S(2)}, u32[]{:S(2)}) collective-permute-start(f32[8,2,32,128]{3,2,1,0:T(8,128)S(1)} %copy-done.37), channel_id=1, source_target_pairs={{4,6},{5,7},{12,14},{13,15},{20,22},{21,23},{28,30},{29,31}} | collective-permute-start | bytes 786440 | tf_op jit(solution)/shard_map/ppermute | solution.py:245
  481.2 39.8 %copy-start.8 = (f32[8,2,32,896]{3,2,1,0:T(8,128)}, f32[8,2,32,896]{3,2,1,0:T(8,128)S(1)}, u32[]{:S(2)}) copy-start(f32[8,2,32,896]{3,2,1,0:T(8,128)S(1)} %collective-permute-done.33.refs_7_) | copy-start | bytes 5505028
  481.2 42.1 %collective-permute-start.34 = (f32[8,2,32,384]{3,2,1,0:T(8,128)S(1)}, f32[8,2,32,384]{3,2,1,0:T(8,128)S(1)}, u32[]{:S(2)}, u32[]{:S(2)}) collective-permute-start(f32[8,2,32,384]{3,2,1,0:T(8,128)S(1)} %copy-done.26), channel_id=1, source_target_pairs={{2,4},{3,5},{10,12},{11,13},{18,20},{19,21},{26,28},{27,29}} | collective-permute-start | bytes 2359304 | tf_op jit(solution)/shard_map/ppermute | solution.py:245
  482.2 81.3 %copy-start.11 = (f32[8,2,32,512]{3,2,1,0:T(8,128)}, f32[8,2,32,512]{3,2,1,0:T(8,128)S(1)}, u32[]{:S(2)}) copy-start(f32[8,2,32,512]{3,2,1,0:T(8,128)S(1)} %slice_add_fusion.2.refs_5_) | copy-start | bytes 3145732
  517.7 40.4 %copy-start.35 = (f32[4,2,32,512]{3,2,1,0:T(8,128)}, f32[4,2,32,512]{3,2,1,0:T(8,128)S(1)}, u32[]{:S(2)}) copy-start(f32[4,2,32,512]{3,2,1,0:T(8,128)S(1)} %collective-permute-done.10.refs_7_) | copy-start | bytes 1572868
  517.7 3.4 collective-permute-start.44
  518.3 39.8 %copy-start.36 = (f32[8,2,32,128]{3,2,1,0:T(8,128)}, f32[8,2,32,128]{3,2,1,0:T(8,128)S(1)}, u32[]{:S(2)}) copy-start(f32[8,2,32,128]{3,2,1,0:T(8,128)S(1)} %collective-permute-done.32.refs_12_) | copy-start | bytes 786436
  518.4 49.3 %collective-permute-start.31 = (f32[8,2,32,512]{3,2,1,0:T(8,128)}, f32[8,2,32,512]{3,2,1,0:T(8,128)}, u32[]{:S(2)}, u32[]{:S(2)}) collective-permute-start(f32[8,2,32,512]{3,2,1,0:T(8,128)} %slice_add_fusion.3.refs_5_), channel_id=1, source_target_pairs={{2,0},{3,1},{10,8},{11,9},{18,16},{19,17},{26,24},{27,25}} | collective-permute-start | bytes 3145736 | tf_op jit(solution)/shard_map/ppermute | solution.py:245
  519.7 38.4 %copy-start.23 = (f32[4,2,32,896]{3,2,1,0:T(8,128)}, f32[4,2,32,896]{3,2,1,0:T(8,128)S(1)}, u32[]{:S(2)}) copy-start(f32[4,2,32,896]{3,2,1,0:T(8,128)S(1)} %collective-permute-done.47.refs_10_) | copy-start | bytes 2752516
  519.7 52.8 %collective-permute-start.35 = (f32[8,2,32,512]{3,2,1,0:T(8,128)S(1)}, f32[8,2,32,512]{3,2,1,0:T(8,128)S(1)}, u32[]{:S(2)}, u32[]{:S(2)}) collective-permute-start(f32[8,2,32,512]{3,2,1,0:T(8,128)S(1)} %slice_add_fusion.2.refs_5_), channel_id=1, source_target_pairs={{2,0},{3,1},{10,8},{11,9},{18,16},{19,17},{26,24},{27,25}} | collective-permute-start | bytes 3145736 | tf_op jit(solution)/shard_map/ppermute | solution.py:245
  521.1 37.0 %collective-permute-start.43 = (f32[4,2,32,512]{3,2,1,0:T(8,128)S(1)}, f32[4,2,32,512]{3,2,1,0:T(8,128)S(1)}, u32[]{:S(2)}, u32[]{:S(2)}) collective-permute-start(f32[4,2,32,512]{3,2,1,0:T(8,128)S(1)} %slice_add_fusion.11.refs_5_), channel_id=1, source_target_pairs={{2,0},{3,1},{10,8},{11,9},{18,16},{19,17},{26,24},{27,25}} | collective-permute-start | bytes 1572872 | tf_op jit(solution)/shard_map/ppermute | solution.py:245
  522.4 2.9 collective-permute-start.48
  523.3 40.2 %copy-start.21 = (f32[4,2,32,512]{3,2,1,0:T(8,128)}, f32[4,2,32,512]{3,2,1,0:T(8,128)S(1)}, u32[]{:S(2)}) copy-start(f32[4,2,32,512]{3,2,1,0:T(8,128)S(1)} %slice_add_fusion.10.refs_5_) | copy-start | bytes 1572868
  523.3 49.1 %collective-permute-start.49 = (f32[4,2,32,512]{3,2,1,0:T(8,128)S(1)}, f32[4,2,32,512]{3,2,1,0:T(8,128)}, u32[]{:S(2)}, u32[]{:S(2)}) collective-permute-start(f32[4,2,32,512]{3,2,1,0:T(8,128)S(1)} %slice_add_fusion.10.refs_5_), channel_id=1, source_target_pairs={{2,0},{3,1},{10,8},{11,9},{18,16},{19,17},{26,24},{27,25}} | collective-permute-start | bytes 1572872 | tf_op jit(solution)/shard_map/ppermute | solution.py:245
  525.4 38.2 %copy-start.32 = (f32[4,2,32,384]{3,2,1,0:T(8,128)}, f32[4,2,32,384]{3,2,1,0:T(8,128)S(1)}, u32[]{:S(2)}) copy-start(f32[4,2,32,384]{3,2,1,0:T(8,128)S(1)} %collective-permute-done.48.refs_11_) | copy-start | bytes 1179652
  525.4 47.1 %collective-permute-start.36 = (f32[8,2,32,128]{3,2,1,0:T(8,128)}, f32[8,2,32,128]{3,2,1,0:T(8,128)}, u32[]{:S(2)}, u32[]{:S(2)}) collective-permute-start(f32[8,2,32,128]{3,2,1,0:T(8,128)} %slice_add_fusion.18), channel_id=1, source_target_pairs={{4,6},{5,7},{12,14},{13,15},{20,22},{21,23},{28,30},{29,31}} | collective-permute-start | bytes 786440 | tf_op jit(solution)/shard_map/ppermute | solution.py:245
  558.1 14.3 %collective-permute-start.50 = (f32[4,2,32,128]{3,2,1,0:T(8,128)}, f32[4,2,32,128]{3,2,1,0:T(8,128)}, u32[]{:S(2)}, u32[]{:S(2)}) collective-permute-start(f32[4,2,32,128]{3,2,1,0:T(8,128)} %slice_add_fusion.20), channel_id=1, source_target_pairs={{4,6},{5,7},{12,14},{13,15},{20,22},{21,23},{28,30},{29,31}} | collective-permute-start | bytes 393224 | tf_op jit(solution)/shard_map/ppermute | solution.py:245
  (45 other events, 511.2 us)
